TPU v7x, 256 devices: a whole 4x4x8 slice. The times are simulated.
256 devices in a mesh: dir: 16 (over x_hi, y, core), psi: 16 (over z, x_lo).
Axes of the slice: x: 4 (x_hi: 2, x_lo: 2; x = x_hi * 2 + x_lo), y: 4, z: 8, core: 2. Of those that a mesh axis runs over, the one named last changes fastest.
Arguments:
- images: float32 [32768, 9216], P(('dir', 'psi')), may hold values from -6 to 6
- prior_bin: int32 [32768], P(('dir', 'psi')), may hold values from 0 to 63, as said below
- prior_center: int32 [32768], P(('dir', 'psi')), may hold values from 0 to 63, as said below
- defocus_class: int32 [32768], P(('dir', 'psi')), may hold values from 0 to 15
- templates: float32 [64, 64, 9216], P('dir', 'psi'), may hold values from -0.125 to 0.125
- ctf_table: float32 [16, 9216], replicated, may hold values from -1 to 1
Outputs:
- log_total: float32 [32768], P(('dir', 'psi'))
- mean_shift: float32 [32768], P(('dir', 'psi'))
- average: float32 [64, 64, 9216], P('dir', 'psi')
Inputs may be any that keep to these rules, and one draw needn't show every extreme that they name: `prior_bin`: in each aligned block of 128 rows (the particles of one device) no bin is named more than 4 times, and some bin exactly 4 times. `prior_center`: A particle in aligned block q of 128 rows has its prior centre among the 4 angles that start at (q mod 16) * 4.
All inputs are finite; a program needn't handle non-finite values.
Results may differ from a plain program's by a relative error of at most 0.0003.
Values sent between devices are 32-bit elements; how exact they have to be, the bound alone decides.
No kernel may reach another device: no remote copies, remote signals or barrier semaphores. Data moves between devices by JAX's collectives and lax.ppermute only.
A program may use at most 128 MiB of HBM per device.

v0:
```python
import jax
import jax.numpy as jnp
from jax import lax
from jax.sharding import PartitionSpec as P

HALF = 4
CAP_BIN = 4


def in_one_piece(arrays, axis, split_dim, concat_dim, along):
    widths = [a.shape[along] for a in arrays]
    both = jnp.concatenate(arrays, axis=along)
    out = lax.all_to_all(both, axis, split_axis=split_dim, concat_axis=concat_dim, tiled=True)
    return tuple(jnp.split(out, [sum(widths[:k]) for k in range(1, len(widths))], axis=along))


def with_halo(value, sides, width):
    for axis, dim in sides:
        size, length = (lax.axis_size(axis), value.shape[dim])
        up = [(i, (i + 1) % size) for i in range(size)]
        down = [(j, i) for i, j in up]
        last = lax.slice_in_dim(value, length - width, length, axis=dim)
        first = lax.slice_in_dim(value, 0, width, axis=dim)
        before = lax.ppermute(last, axis, up)
        after = lax.ppermute(first, axis, down)
        value = jnp.concatenate([before, value, after], axis=dim)
    return value


def shifted(value, axis, by):
    size = lax.axis_size(axis)
    return lax.ppermute(value, axis, [(i, (i + by) % size) for i in range(size)])


def local(images, prior_bin, prior_center, defocus_class, templates, ctf_table):
    highest = lax.Precision.HIGHEST
    dir_count = lax.axis_size("dir")
    psi_index = lax.axis_index("psi")
    part_rows = images.shape[0]
    pixels = images.shape[1]
    dir_bins = templates.shape[0]
    ang_block = templates.shape[1]
    classes = ctf_table.shape[0]
    total_slots = dir_bins * dir_count * CAP_BIN
    positions = jnp.arange(part_rows)
    same_bin = prior_bin[:, None] == prior_bin[None, :]
    earlier = positions[None, :] < positions[:, None]
    slot_rank = jnp.sum(jnp.logical_and(same_bin, earlier), axis=1)
    slot_index = prior_bin * CAP_BIN + slot_rank
    first_angle = psi_index * ang_block
    layout = (dir_count, dir_bins, CAP_BIN)
    send_images = (
        jnp.zeros((total_slots, pixels), jnp.float32)
        .at[slot_index]
        .set(images)
        .reshape(layout + (pixels,))
    )
    send_class = (
        jnp.full((total_slots,), -1, jnp.int32).at[slot_index].set(defocus_class).reshape(layout)
    )
    send_centre = (
        (jnp.zeros((total_slots,), jnp.int32) + first_angle)
        .at[slot_index]
        .set(prior_center)
        .reshape(layout)
    )
    got_images, got_class, got_centre = (
        lax.all_to_all(send_images, "dir", split_axis=0, concat_axis=2, tiled=True),
        *in_one_piece((send_class, send_centre), "dir", 0, 2, 1),
    )
    got_images = got_images[0]
    got_class = got_class[0]
    got_centre = got_centre[0]
    nearby = with_halo(templates, (("psi", 1),), ang_block)
    onehot = (got_class[:, :, None] == jnp.arange(classes)[None, None, :]).astype(jnp.float32)
    ctf_rows = jnp.einsum("bsc,ck->bsk", onehot, ctf_table, precision=highest)
    weighted = ctf_rows * got_images
    ctf_squares = ctf_table * ctf_table
    class_terms = jnp.einsum("ck,bak->bca", ctf_squares, nearby * nearby, precision=highest)
    quadratic = jnp.einsum("bsc,bca->bsa", onehot, class_terms, precision=highest)
    crossed = jnp.einsum("bsk,bak->bsa", weighted, nearby, precision=highest)
    scores = crossed - 0.5 * quadratic
    local_angle = jnp.arange(3 * ang_block, dtype=jnp.int32)
    centre = got_centre - first_angle + ang_block
    offset_ids = local_angle[None, None, :] - centre[:, :, None]
    inside = jnp.abs(offset_ids) <= HALF
    safe_scores = jnp.where(inside, scores, 0.0)
    exp_terms = jnp.where(inside, jnp.exp(safe_scores), 0.0)
    log_total = jnp.log(jnp.sum(exp_terms, axis=2))
    posterior = jnp.where(inside, jnp.exp(safe_scores - log_total[:, :, None]), 0.0)
    mean_shift = jnp.sum(posterior * offset_ids.astype(jnp.float32), axis=2)
    data_all = jnp.einsum("bsa,bsk->bak", posterior, weighted, precision=highest)
    upper_start = 2 * ang_block
    class_mass = jnp.einsum("bsa,bsc->bac", posterior, onehot, precision=highest)
    from_above = shifted((data_all[:, :ang_block], class_mass[:, :ang_block]), "psi", -1)
    from_below = shifted((data_all[:, upper_start:], class_mass[:, upper_start:]), "psi", 1)
    data_total = data_all[:, ang_block:upper_start] + from_above[0] + from_below[0]
    mass_total = class_mass[:, ang_block:upper_start] + from_above[1] + from_below[1]
    weight_total = jnp.einsum("bac,ck->bak", mass_total, ctf_squares, precision=highest)
    average = data_total / (weight_total + 1.0)
    back_total, back_shift = in_one_piece((log_total[None], mean_shift[None]), "dir", 2, 0, 1)
    log_home = back_total.reshape(total_slots)[slot_index]
    shift_home = back_shift.reshape(total_slots)[slot_index]
    return (log_home, shift_home, average)


def solution(mesh):
    return jax.shard_map(
        local,
        mesh=mesh,
        in_specs=(
            P(("dir", "psi"), None),
            P(("dir", "psi")),
            P(("dir", "psi")),
            P(("dir", "psi")),
            P("dir", "psi", None),
            P(),
        ),
        out_specs=(P(("dir", "psi")), P(("dir", "psi")), P("dir", "psi", None)),
        check_vma=False,
    )
```

profile of v0, /device:TPU:96, one launch (start us, length us, event | category | flops | bytes accessed | tf_op | source)
XLA Modules:
  0.0 290.8 jit_solution(4487096930045674783)
XLA Ops:
  5.5 7.0 %all-to-all-start = ((s32[16,8,4]{1,2,0:T(4,128)}), s32[16,8,4]{1,2,0:T(4,128)S(1)}, u32[]{:S(2)}, u32[]{:S(2)}) async-start(s32[16,8,4]{1,2,0:T(4,128)} %copy.25), calls=%async_computation | async-start | bytes 65536 | tf_op jit(solution)/shard_map/all_to_all | solution.py:13
  12.5 9.1 %scatter_custom_fusion.2 = f32[256,9216]{1,0:T(8,128)} fusion(s32[128]{0:T(128)S(1)} %compare_select_fusion, f32[128,9216]{1,0:T(8,128)} %param.6, f32[]{:T(128)} %constant.13.clone.1), kind=kCustom, calls=%fused_computation.7 | custom fusion | bytes 9437696 | tf_op jit(solution)/shard_map/scatter | solution.py:55
  21.6 10.5 %reshape.48 = f32[16,4,4,9216]{3,2,1,0:T(4,128)} reshape(f32[256,9216]{1,0:T(8,128)} %scatter_custom_fusion.2) | data formatting | bytes 18874368 | tf_op jit(solution)/shard_map/reshape | solution.py:56
  32.1 7.4 %all-to-all-start.1 = ((f32[16,4,4,9216]{3,2,1,0:T(4,128)}), f32[16,4,4,9216]{3,2,1,0:T(4,128)}, u32[]{:S(2)}, u32[]{:S(2)}) async-start(f32[16,4,4,9216]{3,2,1,0:T(4,128)} %reshape.48), calls=%async_computation.1 | async-start | bytes 18874368 | tf_op jit(solution)/shard_map/all_to_all | solution.py:68
  40.2 2.3 collective-permute-start.1
  43.4 150.3 %collective-permute-done = f32[4,4,9216]{2,1,0:T(4,128)S(1)} collective-permute-done((f32[4,4,9216]{2,1,0:T(4,128)S(1)}, f32[4,4,9216]{2,1,0:T(4,128)S(1)}, u32[]{:S(2)}, u32[]{:S(2)}) %collective-permute-start) | collective-permute-done | bytes 589856 | tf_op jit(solution)/shard_map/ppermute | solution.py:24
  193.6 3.8 %collective-permute-done.1 = f32[4,4,9216]{2,1,0:T(4,128)S(1)} collective-permute-done((f32[4,4,9216]{2,1,0:T(4,128)S(1)}, f32[4,4,9216]{2,1,0:T(4,128)S(1)}, u32[]{:S(2)}, u32[]{:S(2)}) %collective-permute-start.1) | collective-permute-done | bytes 589856 | tf_op jit(solution)/shard_map/ppermute | solution.py:25
  197.5 2.2 fusion.2
  199.9 8.1 %copy.28 = f32[1,4,16,4,9216]{4,3,2,1,0:T(4,128)} copy(f32[1,4,16,4,9216]{4,3,1,2,0:T(4,128)} %bitcast.9) | data formatting | bytes 18874368 | tf_op jit(solution)/shard_map/all_to_all | solution.py:68
  208.0 10.8 %squeeze.4 = f32[4,64,9216]{2,1,0:T(8,128)} reshape(f32[1,4,16,4,9216]{4,3,2,1,0:T(4,128)} %copy.28) | data formatting | bytes 18874368 | tf_op jit(solution)/shard_map/squeeze | solution.py:71
  218.8 6.9 %convolution_multiply_fusion = f32[4,64,9216]{2,1,0:T(8,128)S(1)} fusion(f32[4,64,9216]{2,1,0:T(8,128)} %squeeze.4, f32[16,9216]{1,0:T(8,128)S(1)} %copy-done.1, s32[4,64]{1,0:T(4,128)S(1)} %copy.27), kind=kOutput, calls=%fused_computation.5 | convolution fusion | flops 455348224 | bytes 19465216 | tf_op jit(solution)/shard_map/bsc,ck->bsk/dot_general | solution.py:76
  225.8 8.4 %select_reduce_fusion = (f32[4,64]{1,0:T(4,128)S(1)}, f32[4,64,12]{1,2,0:T(8,128)S(1)}) fusion(s32[4,64]{1,0:T(4,128)S(1)} %copy.26, f32[4,64,12]{1,2,0:T(8,128)S(1)} %convolution_multiply_fusion.1, f32[4,64,9216]{2,1,0:T(8,128)S(1)} %convolution_multiply_fusion, f32[4,4,9216]{2,1,0:T(4,128)S(1)} %collective-permute-done.1, f32[4,4,9216]{2,1,0:T(4,128)S(1)} %copy-done, ...), kind=kOutput, calls=%fused_computation.34 | convolution fusion | flops 340644608 | bytes 11233280 | tf_op jit(solution)/shard_map/bsk,bak->bsa/dot_general | solution.py:81
  234.2 4.9 %fusion.25 = f32[4,12,9216]{2,1,0:T(8,128)S(1)} fusion(f32[4,64,9216]{2,1,0:T(8,128)S(1)} %convolution_multiply_fusion, f32[4,64,12]{1,2,0:T(8,128)S(1)} %get-tuple-element.14, f32[4,64]{1,0:T(4,128)S(1)} %get-tuple-element.12, s32[4,64]{1,0:T(4,128)S(1)} %copy.26), kind=kOutput, calls=%fused_computation.44 | convolution fusion | flops 339753984 | bytes 11220992 | tf_op jit(solution)/shard_map/bsa,bsk->bak/dot_general | solution.py:92
  240.2 2.0 collective-permute-start.3
  242.9 10.8 %all-to-all-start.2 = ((f32[1,8,64]{1,0,2:T(1,128)}), f32[1,8,64]{1,0,2:T(1,128)}, u32[]{:S(2)}, u32[]{:S(2)}) async-start(f32[1,8,64]{1,0,2:T(1,128)} %copy.29), calls=%async_computation.2 | async-start | bytes 65536 | tf_op jit(solution)/shard_map/all_to_all | solution.py:13
  255.8 1.9 collective-permute-start.4
  257.7 1.7 collective-permute-start.5
  259.3 18.2 %all-to-all-done.2 = f32[1,8,64]{1,0,2:T(1,128)} async-done(((f32[1,8,64]{1,0,2:T(1,128)}), f32[1,8,64]{1,0,2:T(1,128)}, u32[]{:S(2)}, u32[]{:S(2)}) %all-to-all-start.2) | async-done | bytes 2080 | tf_op jit(solution)/shard_map/all_to_all | solution.py:13
  277.5 1.5 fusion.38
  279.0 1.5 copy.31
  281.4 1.6 copy.30
  283.9 1.9 gather_fusion.1
  285.7 1.9 gather_fusion
  287.7 3.2 %fusion.8 = f32[4,4,9216]{2,1,0:T(4,128)} fusion(f32[4,4,9216]{2,1,0:T(4,128)} %collective-permute-done.3, f32[4,4,9216]{2,1,0:T(4,128)} %collective-permute-done.2, f32[4,12,9216]{2,1,0:T(8,128)S(1)} %fusion.25, f32[16,9216]{1,0:T(8,128)S(1)} %copy-done.1, f32[4,4,16]{2,1,0:T(4,128)} %collective-permute-done.5, f32[4,4,16]{2,1,0:T(4,128)} %collective-permute-done.4, ...), kind=kOutput, calls=%fused_computation.18 | convolution fusion | flops 29049344 | bytes 2973696 | tf_op jit(solution)/shard_map/bac,ck->bak/dot_general | solution.py:99
  (38 shorter events, 12.0 us)
Async XLA Ops:
  5.5 26.6 %all-to-all-start = ((s32[16,8,4]{1,2,0:T(4,128)}), s32[16,8,4]{1,2,0:T(4,128)S(1)}, u32[]{:S(2)}, u32[]{:S(2)}) async-start(s32[16,8,4]{1,2,0:T(4,128)} %copy.25), calls=%async_computation | async-start | bytes 65536 | tf_op jit(solution)/shard_map/all_to_all | solution.py:13
  32.1 7.4 %copy-start = (f32[4,4,9216]{2,1,0:T(4,128)S(1)}, f32[4,4,9216]{2,1,0:T(4,128)}, u32[]{:S(2)}) copy-start(f32[4,4,9216]{2,1,0:T(4,128)} %param.10) | copy-start | bytes 1769476
  32.1 165.4 %copy-start.1 = (f32[16,9216]{1,0:T(8,128)S(1)}, f32[16,9216]{1,0:T(8,128)}, u32[]{:S(2)}) copy-start(f32[16,9216]{1,0:T(8,128)} %param.11) | copy-start | bytes 1769476
  32.1 167.8 %all-to-all-start.1 = ((f32[16,4,4,9216]{3,2,1,0:T(4,128)}), f32[16,4,4,9216]{3,2,1,0:T(4,128)}, u32[]{:S(2)}, u32[]{:S(2)}) async-start(f32[16,4,4,9216]{3,2,1,0:T(4,128)} %reshape.48), calls=%async_computation.1 | async-start | bytes 18874368 | tf_op jit(solution)/shard_map/all_to_all | solution.py:68
  39.5 154.1 %collective-permute-start = (f32[4,4,9216]{2,1,0:T(4,128)S(1)}, f32[4,4,9216]{2,1,0:T(4,128)S(1)}, u32[]{:S(2)}, u32[]{:S(2)}) collective-permute-start(f32[4,4,9216]{2,1,0:T(4,128)S(1)} %copy-done), channel_id=1, source_target_pairs={{0,1},{1,2},{2,3},{3,4},{4,5},{5,6},{6,7},{7,8},{8,9},{9,10},{10,1... | collective-permute-start | bytes 1769480 | tf_op jit(solution)/shard_map/ppermute | solution.py:24
  40.2 157.3 %collective-permute-start.1 = (f32[4,4,9216]{2,1,0:T(4,128)S(1)}, f32[4,4,9216]{2,1,0:T(4,128)S(1)}, u32[]{:S(2)}, u32[]{:S(2)}) collective-permute-start(f32[4,4,9216]{2,1,0:T(4,128)S(1)} %copy-done), channel_id=1, source_target_pairs={{1,0},{2,1},{3,2},{4,3},{5,4},{6,5},{7,6},{8,7},{9,8},{10,9},{11,1... | collective-permute-start | bytes 1769480 | tf_op jit(solution)/shard_map/ppermute | solution.py:25
  234.2 5.0 %copy-start.2 = (f32[4,64,12]{1,2,0:T(8,128)}, f32[4,64,12]{1,2,0:T(8,128)S(1)}, u32[]{:S(2)}) copy-start(f32[4,64,12]{1,2,0:T(8,128)S(1)} %get-tuple-element.14) | copy-start | bytes 36868
  240.2 47.5 %collective-permute-start.2 = (f32[4,4,9216]{2,1,0:T(4,128)}, f32[4,4,9216]{2,1,0:T(4,128)}, u32[]{:S(2)}, u32[]{:S(2)}) collective-permute-start(f32[4,4,9216]{2,1,0:T(4,128)} %get-tuple-element.3), channel_id=1, source_target_pairs={{0,15},{1,0},{2,1},{3,2},{4,3},{5,4},{6,5},{7,6},{8,7},{9,8},{10,9... | collective-permute-start | bytes 1769480 | tf_op jit(solution)/shard_map/ppermute | solution.py:32
  240.2 47.5 %collective-permute-start.3 = (f32[4,4,9216]{2,1,0:T(4,128)S(1)}, f32[4,4,9216]{2,1,0:T(4,128)}, u32[]{:S(2)}, u32[]{:S(2)}) collective-permute-start(f32[4,4,9216]{2,1,0:T(4,128)S(1)} %get-tuple-element.4), channel_id=1, source_target_pairs={{0,1},{1,2},{2,3},{3,4},{4,5},{5,6},{6,7},{7,8},{8,9},{9,10},{10,1... | collective-permute-start | bytes 1769480 | tf_op jit(solution)/shard_map/ppermute | solution.py:32
  242.9 34.6 %all-to-all-start.2 = ((f32[1,8,64]{1,0,2:T(1,128)}), f32[1,8,64]{1,0,2:T(1,128)}, u32[]{:S(2)}, u32[]{:S(2)}) async-start(f32[1,8,64]{1,0,2:T(1,128)} %copy.29), calls=%async_computation.2 | async-start | bytes 65536 | tf_op jit(solution)/shard_map/all_to_all | solution.py:13
  254.6 0.6 copy-start.3
  255.8 31.8 %collective-permute-start.4 = (f32[4,4,16]{2,1,0:T(4,128)}, f32[4,4,16]{2,1,0:T(4,128)}, u32[]{:S(2)}, u32[]{:S(2)}) collective-permute-start(f32[4,4,16]{2,1,0:T(4,128)} %get-tuple-element.5), channel_id=1, source_target_pairs={{0,15},{1,0},{2,1},{3,2},{4,3},{5,4},{6,5},{7,6},{8,7},{9,8},{10,9... | collective-permute-start | bytes 3080 | tf_op jit(solution)/shard_map/ppermute | solution.py:32
  257.7 30.0 %collective-permute-start.5 = (f32[4,4,16]{2,1,0:T(4,128)S(1)}, f32[4,4,16]{2,1,0:T(4,128)}, u32[]{:S(2)}, u32[]{:S(2)}) collective-permute-start(f32[4,4,16]{2,1,0:T(4,128)S(1)} %get-tuple-element.6), channel_id=1, source_target_pairs={{0,1},{1,2},{2,3},{3,4},{4,5},{5,6},{6,7},{7,8},{8,9},{9,10},{10,1... | collective-permute-start | bytes 3080 | tf_op jit(solution)/shard_map/ppermute | solution.py:32
where the time goes:
time: 294 us; the launch traced here: 291 us
  waiting for transfers between devices  172 us (59%)
  local copies, waits for them, and re-layouts  54.8 us (19%)
  starting transfers between devices  33.8 us (11%)
  matrix products  26.8 us (9%)
    ppermute x1, waiting for transfers between devices, with_halo(): before = lax.ppermute(last, axis, up)  150 us
    all_to_all x2, waiting for transfers between devices, in_one_piece(): lax.all_to_all(both, axis, split_axis=split_dim, concat_axis=concat_dim,...  18.2 us
    all_to_all x2, starting transfers between devices, in_one_piece(): lax.all_to_all(both, axis, split_axis=split_dim, concat_axis=concat_dim,...  17.8 us
    squeeze x1, local copies, waits for them, and re-layouts, local(): got_images = got_images[0]  10.8 us
    reshape x1, local copies, waits for them, and re-layouts, local(): send_images = jnp.zeros((total_slots, pixels), jnp.float32).at[slot_index...  10.5 us
    scatter x1, local copies, waits for them, and re-layouts, local(): send_images = jnp.zeros((total_slots, pixels), jnp.float32).at[slot_index...  9.08 us
    dot_general x1, matrix products, local(): crossed = jnp.einsum('bsk,bak->bsa', weighted, nearby, precision=highest)  8.44 us
    all_to_all x1, local copies, waits for them, and re-layouts, local(): lax.all_to_all(send_images, 'dir', split_axis=0, concat_axis=2, tiled=True)  8.13 us
  transfers between devices with their start and end apart: 9, of which 3 were waited for; matrix products, arithmetic and copies ran while one was open for 12% of the time, Pallas kernels for 0%

commit v1 on v0

v1 whole, which is shorter than its diff:
```python
import jax
import jax.numpy as jnp
from jax import lax
from jax.experimental import pallas as pl
from jax.experimental.pallas import tpu as pltpu
from jax.sharding import Mesh
from jax.sharding import PartitionSpec as P

HALF = 4
LANES = 128
CLASSES = 16
IMG = 288
TPL = 40
ROWS = IMG + TPL
META = 36
BF = jnp.bfloat16
F32 = jnp.float32
HIGHEST = lax.Precision.HIGHEST
PLANE = ("dir", "xlo")


def params(mib):
    return pltpu.CompilerParams(vmem_limit_bytes=mib * 1024 * 1024)


def cost(flops, moved):
    return pl.CostEstimate(flops=flops, bytes_accessed=moved, transcendentals=0)


def lane_group(shape):
    return lax.broadcasted_iota(jnp.int32, shape, len(shape) - 1) // 32


def turned(x, groups):
    groups = groups % 4
    return x if groups == 0 else pltpu.roll(x, 32 * groups, x.ndim - 1)


def pick_groups(parts):
    group = lane_group(parts[0].shape)
    out = parts[3]
    for q in (2, 1, 0):
        out = jnp.where(group == q, parts[q], out)
    return out


def split(x):
    hi = x.astype(BF)
    return hi, (x - hi.astype(F32)).astype(BF)


def pack_kernel(img_ref, rem_ref, tpl_ref, tplrem_ref, meta_ref, out_ref):
    meta = meta_ref[...]
    for q in range(4):
        for j in range(2):
            tile = pl.ds((2 * q + j) * LANES, LANES)
            out_ref[q, pl.ds(j * 128, 128), :] = img_ref[:, tile]
            for b in range(4):
                out_ref[q, pl.ds(IMG + 16 * j + 4 * b, 4), :] = tpl_ref[b, :, tile]
        out_ref[q, pl.ds(256, 32), :] = pick_groups([turned(rem_ref[pl.ds(32 * g, 32), :], g - q) for g in range(4)])
        out_ref[q, pl.ds(IMG + 32, 4), :] = pick_groups([turned(tplrem_ref[b], b - q) for b in range(4)])
        out_ref[q, pl.ds(IMG + META, 4), :] = meta


def pack(images, templates, meta):
    steps = 8
    return pl.pallas_call(
        pack_kernel,
        grid=(steps,),
        in_specs=[
            pl.BlockSpec((128, 1024), lambda t: (0, t)),
            pl.BlockSpec((128, LANES), lambda t: (0, 64 + t)),
            pl.BlockSpec((4, 4, 1024), lambda t: (0, 0, t)),
            pl.BlockSpec((4, 4, LANES), lambda t: (0, 0, 64 + t)),
            pl.BlockSpec((4, LANES), lambda t: (0, 0)),
        ],
        out_specs=pl.BlockSpec((4, ROWS, LANES), lambda t: (t, 0, 0)),
        out_shape=jax.ShapeDtypeStruct((4 * steps, ROWS, LANES), F32),
        compiler_params=params(16),
        cost_estimate=cost(0, 11_000_000),
        name="pack",
    )(images, images, templates, templates, meta)


def fill_templates(tpl_ref, sources, sq_ref, tf_ref, base, yh_ref, yl_ref, yr_ref):
    for d, s in enumerate(sources):
        rows = pl.ds(16 * d, 16)
        tf_ref[rows, pl.ds(0, 128)] = tpl_ref[s, pl.ds(0, 16), :]
        tf_ref[rows, pl.ds(128, 128)] = tpl_ref[s, pl.ds(16, 16), :]
        packed = tpl_ref[s, pl.ds(32, 4), :]
        v = [turned(packed, j) for j in range(4)]
        for b in range(4):
            tf_ref[pl.ds(16 * d + 4 * b, 4), pl.ds(256, 128)] = pick_groups([v[(q - b) % 4] for q in (0, 1, 2)] + [jnp.zeros_like(packed)])
    for c in range(4):
        rows = pl.ds(64 * c, 64)
        out = pl.ds(base + 64 * c, 64)
        full = tf_ref[rows, :]
        quad = jnp.dot(full * full, sq_ref[...], precision=HIGHEST, preferred_element_type=F32)
        hi, lo = split(full)
        yh_ref[out, :] = hi[:, :256]
        yl_ref[out, :] = lo[:, :256]
        vh, vl = split(-0.5 * quad)
        lane = lax.broadcasted_iota(jnp.int32, (64, LANES), 1)
        last = jnp.where(lane < 112, vh.astype(F32), vl.astype(F32))
        tail = jnp.where(lane < 64, hi[:, 256:].astype(F32), lo[:, 256:].astype(F32))
        yr_ref[out, :] = jnp.where(lane < 96, tail, last).astype(BF)


def gathered(yh_ref, yl_ref, yr_ref, rows, x):
    y = jnp.concatenate([yh_ref[rows, :], yl_ref[rows, :], yh_ref[rows, :], yr_ref[rows, :]], axis=1)
    return lax.dot_general(y, x, (((1,), (1,)), ((), ())), preferred_element_type=F32)


def by_bin(scores, first_bin, bins):
    rows = scores.shape[0]
    row_bin = lax.broadcasted_iota(jnp.int32, scores.shape, 0) // 4 + first_bin
    kept = jnp.where(row_bin == bins, scores, 0.0)
    return jnp.sum(kept.reshape(rows // 8, 8, scores.shape[1]), axis=0)


def bins_of(tpl_ref, first, second):
    both = [tpl_ref[s, pl.ds(META, 1), :] for s in (first, second)]
    return jnp.concatenate(both, axis=1).astype(jnp.int32)


def window(yh_ref, yl_ref, yr_ref, base, x, bins):
    total = jnp.zeros((8, 256), F32)
    for c in range(2):
        part = gathered(yh_ref, yl_ref, yr_ref, pl.ds(base + 128 * c, 128), x)
        total = total + by_bin(part, 32 * c, bins)
    return total + pltpu.roll(total, 4, 0)


def own_kernel(buf_ref, tpl_ref, ctf_ref, sq_ref, xh_ref, xl_ref, xr_ref, out_ref, tf_ref, yh_ref, yl_ref, yr_ref, ce_ref):
    step = pl.program_id(0)

    @pl.when(step == 0)
    def _():
        for side in range(2):
            fill_templates(tpl_ref, [2 * d + side for d in range(16)], sq_ref, tf_ref, 256 * side, yh_ref, yl_ref, yr_ref)
        ctf = ctf_ref[...]
        hi, mid = split(ctf)
        low = (ctf - hi.astype(F32) - mid.astype(F32)).astype(BF)
        ce_ref[pl.ds(0, 16), :] = hi
        ce_ref[pl.ds(16, 16), :] = mid
        ce_ref[pl.ds(32, 16), :] = low

    half = lax.broadcasted_iota(jnp.int32, (8, 128), 0) < 4
    group = lane_group((128, LANES))
    for s in range(4):
        source = 4 * step + s
        classes = tpl_ref[source, pl.ds(META + 2, 1), :].astype(jnp.int32)
        row_class = lax.broadcasted_iota(jnp.int32, (48, 128), 0) % CLASSES
        onehot = jnp.where(row_class == classes, 1.0, 0.0).astype(BF)
        ctf = lax.dot_general(onehot, ce_ref[...], (((0,), (0,)), ((), ())), preferred_element_type=F32)
        for j in range(2):
            hi, lo = split(ctf[:, 128 * j : 128 * j + 128] * buf_ref[s, pl.ds(128 * j, 128), :])
            xh_ref[s, :, pl.ds(128 * j, 128)] = hi
            xl_ref[s, :, pl.ds(128 * j, 128)] = lo
        packed = buf_ref[s, pl.ds(256, 32), :]
        v = [turned(packed, j) for j in range(4)]
        one = jnp.ones_like(packed)
        rem = jnp.concatenate([pick_groups([v[(q - g) % 4] for q in (0, 1, 2)] + [one]) for g in range(4)], axis=0)
        hi, lo = split(ctf[:, 256:] * rem)
        xr_ref[s, :, :] = jnp.where(group == 1, lo.astype(F32), hi.astype(F32)).astype(BF)
    for side in range(2):
        first, second = side, 2 + side
        x = jnp.concatenate(
            [jnp.concatenate([xh_ref[s], xh_ref[s], xl_ref[s], xr_ref[s]], axis=1) for s in (first, second)], axis=0
        )
        bins = bins_of(tpl_ref, 4 * step + first, 4 * step + second)
        low = window(yh_ref, yl_ref, yr_ref, 0, x, bins)
        high = window(yh_ref, yl_ref, yr_ref, 256, x, bins)
        for k, s in enumerate((first, second)):
            cols = slice(128 * k, 128 * k + 128)
            out_ref[s] = jnp.where(half, low[:, cols], high[:, cols])


def own_scores(buf, tpl, ctf_ext, squares):
    n = buf.shape[0]
    whole = lambda shape: pl.BlockSpec(shape, lambda p: (0,) * len(shape))
    block = lambda *shape: pl.BlockSpec(shape, lambda p: (p,) + (0,) * (len(shape) - 1))
    return pl.pallas_call(
        own_kernel,
        grid=(n // 4,),
        in_specs=[block(4, IMG, LANES), whole((n, TPL, LANES)), whole((16, 384)), whole((384, LANES))],
        out_specs=[block(4, 128, 256), block(4, 128, 256), block(4, 128, 128), block(4, 8, 128)],
        out_shape=[
            jax.ShapeDtypeStruct((n, 128, 256), BF),
            jax.ShapeDtypeStruct((n, 128, 256), BF),
            jax.ShapeDtypeStruct((n, 128, 128), BF),
            jax.ShapeDtypeStruct((n, 8, 128), F32),
        ],
        scratch_shapes=[
            pltpu.VMEM((256, 384), F32),
            pltpu.VMEM((512, 256), BF),
            pltpu.VMEM((512, 256), BF),
            pltpu.VMEM((512, 128), BF),
            pltpu.VMEM((48, 384), BF),
        ],
        compiler_params=params(24),
        cost_estimate=cost(4_000_000_000, 12_000_000),
        name="own_scores",
    )(buf, tpl, ctf_ext, squares)


def halo_kernel(xh_ref, xl_ref, xr_ref, own_ref, tpl_ref, halo_ref, sq_ref, out_ref, tf_ref, yh_ref, yl_ref, yr_ref):
    step = pl.program_id(0)

    @pl.when(step == 0)
    def _():
        for side in range(2):
            fill_templates(halo_ref, [16 * side + d for d in range(16)], sq_ref, tf_ref, 256 * side, yh_ref, yl_ref, yr_ref)

    for side in range(2):
        first, second = side, 2 + side
        x = jnp.concatenate(
            [jnp.concatenate([xh_ref[s], xh_ref[s], xl_ref[s], xr_ref[s]], axis=1) for s in (first, second)], axis=0
        )
        bins = bins_of(tpl_ref, 4 * step + first, 4 * step + second)
        edge = window(yh_ref, yl_ref, yr_ref, 256 * side, x, bins)
        for k, s in enumerate((first, second)):
            out_ref[s, pl.ds(0, 8), :] = own_ref[s]
            out_ref[s, pl.ds(8, 8), :] = edge[:, 128 * k : 128 * k + 128]


def halo_scores(xh, xl, xr, own, tpl, halo, squares):
    n = xh.shape[0]
    whole = lambda shape: pl.BlockSpec(shape, lambda p: (0,) * len(shape))
    block = lambda *shape: pl.BlockSpec(shape, lambda p: (p,) + (0,) * (len(shape) - 1))
    return pl.pallas_call(
        halo_kernel,
        grid=(n // 4,),
        in_specs=[
            block(4, 128, 256),
            block(4, 128, 256),
            block(4, 128, 128),
            block(4, 8, 128),
            whole((n, TPL, LANES)),
            whole((n, TPL, LANES)),
            whole((384, LANES)),
        ],
        out_specs=block(4, 16, 128),
        out_shape=jax.ShapeDtypeStruct((n, 16, 128), F32),
        scratch_shapes=[
            pltpu.VMEM((256, 384), F32),
            pltpu.VMEM((512, 256), BF),
            pltpu.VMEM((512, 256), BF),
            pltpu.VMEM((512, 128), BF),
        ],
        compiler_params=params(24),
        cost_estimate=cost(2_000_000_000, 6_000_000),
        name="halo_scores",
    )(xh, xl, xr, own, tpl, halo, squares)


def home_kernel(place_ref, scores_ref, centre_ref, total_ref, shift_ref, p_ref):
    xlo = place_ref[0]
    first = place_ref[1]
    n = scores_ref.shape[0]
    scores = scores_ref[0]
    for s in range(1, n):
        scores = scores + scores_ref[s]
    row = lax.broadcasted_iota(jnp.int32, scores.shape, 0)
    angle = jnp.where(row < 8, row + 4, row - 8 + 12 * xlo)
    offset = angle - (centre_ref[...] - first + 4)
    inside = jnp.logical_and(jnp.abs(offset) <= HALF, row < 12)
    safe = jnp.where(inside, scores, 0.0)
    total = jnp.log(jnp.sum(jnp.where(inside, jnp.exp(safe), 0.0), axis=0, keepdims=True))
    p = jnp.where(inside, jnp.exp(safe - total), 0.0)
    total_ref[...] = total
    shift_ref[...] = jnp.sum(p * offset.astype(F32), axis=0, keepdims=True)
    p = jnp.where(row < 12, p, pltpu.roll(p, 4, 0))
    for s in range(n):
        p_ref[s] = p


def home(place, scores, centre):
    n = scores.shape[0]
    vmem = pl.BlockSpec(memory_space=pltpu.VMEM)
    return pl.pallas_call(
        home_kernel,
        in_specs=[pl.BlockSpec(memory_space=pltpu.SMEM), vmem, vmem],
        out_specs=[vmem, vmem, vmem],
        out_shape=[
            jax.ShapeDtypeStruct((1, 128), F32),
            jax.ShapeDtypeStruct((1, 128), F32),
            jax.ShapeDtypeStruct((n, 16, 128), F32),
        ],
        compiler_params=params(4),
        cost_estimate=cost(200_000, 600_000),
        name="home",
    )(place, scores, centre)


def spread(p8, bins, first_bin, rows):
    n = p8.shape[1]
    row_bin = lax.broadcasted_iota(jnp.int32, (rows, n), 0) // 4 + first_bin
    mine = row_bin == bins
    hi = p8.astype(BF).astype(F32)
    lo = p8 - hi
    wide = lambda v: jnp.broadcast_to(v[None], (rows // 8, 8, n)).reshape(rows, n)
    return [jnp.where(mine, wide(v), 0.0).astype(BF) for v in (hi, lo)]


def add_sums(out_ref, rows, high, low, xh, xl, xr):
    main = jnp.dot(high, xh, preferred_element_type=F32)
    main = main + jnp.dot(low, xh, preferred_element_type=F32)
    main = main + jnp.dot(high, xl, preferred_element_type=F32)
    tail = jnp.dot(high, xr, preferred_element_type=F32) + jnp.dot(low, xr, preferred_element_type=F32)
    out_ref[rows, pl.ds(0, 256)] += main
    out_ref[rows, pl.ds(256, 128)] += tail


def sums_kernel(which, p_ref, tpl_ref, xh_ref, xl_ref, xr_ref, out_ref):
    step = pl.program_id(0)

    @pl.when(step == 0)
    def _():
        out_ref[...] = jnp.zeros_like(out_ref)

    half = lax.broadcasted_iota(jnp.int32, (8, 256), 0) < 4
    for side in range(2):
        first, second = side, 2 + side
        pair = lambda ref: jnp.concatenate([ref[first], ref[second]], axis=0)
        xh, xl, xr = pair(xh_ref), pair(xl_ref), pair(xr_ref)
        bins = bins_of(tpl_ref, 4 * step + first, 4 * step + second)
        if which == "halo":
            p8 = jnp.concatenate([p_ref[first, pl.ds(8, 8), :], p_ref[second, pl.ds(8, 8), :]], axis=1)
            for c in range(2):
                high, low = spread(p8, bins, 32 * c, 128)
                add_sums(out_ref, pl.ds(256 * side + 128 * c, 128), high, low, xh, xl, xr)
        else:
            own = jnp.concatenate([p_ref[first, pl.ds(0, 8), :], p_ref[second, pl.ds(0, 8), :]], axis=1)
            other = pltpu.roll(own, 4, 0)
            for k, p8 in enumerate((jnp.where(half, own, other), jnp.where(half, other, own))):
                for c in range(2):
                    high, low = spread(p8, bins, 32 * c, 128)
                    add_sums(out_ref, pl.ds(256 * k + 128 * c, 128), high, low, xh, xl, xr)


def sums(which, p, tpl, xh, xl, xr):
    n = xh.shape[0]
    whole = lambda shape: pl.BlockSpec(shape, lambda i: (0,) * len(shape))
    block = lambda *shape: pl.BlockSpec(shape, lambda i: (i,) + (0,) * (len(shape) - 1))

    def body(*refs):
        sums_kernel(which, *refs)

    return pl.pallas_call(
        body,
        grid=(n // 4,),
        in_specs=[block(4, 16, 128), whole((n, TPL, LANES)), block(4, 128, 256), block(4, 128, 256), block(4, 128, 128)],
        out_specs=whole((512, 384)),
        out_shape=jax.ShapeDtypeStruct((512, 384), F32),
        compiler_params=params(24),
        cost_estimate=cost(4_000_000_000, 6_000_000),
        name="sums_" + which,
    )(p, tpl, xh, xl, xr)


def average_kernel(own_ref, below_ref, above_ref, sq_ref, out_ref):
    for side, other_ref in ((0, below_ref), (1, above_ref)):
        for c in range(4):
            rows = pl.ds(64 * c, 64)
            total = own_ref[pl.ds(256 * side + 64 * c, 64), :] + other_ref[rows, :]
            weight = jnp.dot(total[:, 256:], sq_ref[...], precision=HIGHEST, preferred_element_type=F32)
            tail = total[:, 256:]
            tail = tail + pltpu.roll(tail, 96, 1)
            mean = jnp.concatenate([total[:, :256], tail], axis=1) / (weight + 1.0)
            for d in range(4):
                dest = 2 * (4 * c + d) + side
                piece = mean[16 * d : 16 * d + 16]
                out_ref[dest, pl.ds(0, 16), :] = piece[:, :128]
                out_ref[dest, pl.ds(16, 16), :] = piece[:, 128:256]
                rem = [piece[4 * b : 4 * b + 4, 256:] for b in range(4)]
                out_ref[dest, pl.ds(32, 4), :] = pick_groups([turned(rem[b], b) for b in range(4)])
                out_ref[dest, pl.ds(36, 4), :] = jnp.zeros((4, LANES), F32)


def averages(own, below, above, squares, n):
    vmem = pl.BlockSpec(memory_space=pltpu.VMEM)
    return pl.pallas_call(
        average_kernel,
        in_specs=[vmem] * 4,
        out_specs=vmem,
        out_shape=jax.ShapeDtypeStruct((n, 40, LANES), F32),
        compiler_params=params(8),
        cost_estimate=cost(200_000_000, 3_000_000),
        name="averages",
    )(own, below, above, squares)


def unpack_kernel(got_ref, out_ref):
    n = got_ref.shape[0]
    for i in range(n):
        for j in range(2):
            for b in range(4):
                out_ref[b, :, pl.ds(256 * i + 128 * j, 128)] = got_ref[i, pl.ds(16 * j + 4 * b, 4), :]
    for t in range(n // 4):
        rem = [got_ref[4 * t + q, pl.ds(32, 4), :] for q in range(4)]
        for b in range(4):
            out_ref[b, :, pl.ds(256 * n + 128 * t, 128)] = pick_groups([turned(rem[q], q - b) for q in range(4)])


def unpack(got, pixels):
    vmem = pl.BlockSpec(memory_space=pltpu.VMEM)
    return pl.pallas_call(
        unpack_kernel,
        in_specs=[vmem],
        out_specs=vmem,
        out_shape=jax.ShapeDtypeStruct((4, 4, pixels), F32),
        compiler_params=params(8),
        cost_estimate=cost(0, 1_200_000),
        name="unpack",
    )(got)


def exchange(value):
    return lax.all_to_all(value, PLANE, split_axis=0, concat_axis=0, tiled=True)


def along_z(value, by):
    size = lax.axis_size("z")
    return lax.ppermute(value, "z", [(i, (i + by) % size) for i in range(size)])


def local(images, prior_bin, prior_center, defocus_class, templates, ctf_table):
    pixels = images.shape[1]
    xlo = lax.axis_index("xlo")
    chunk = lax.axis_index("dir") * 2 + xlo
    first = lax.axis_index("z") * 8
    meta = jnp.stack([prior_bin, prior_center, defocus_class, defocus_class]).astype(F32)
    ctf_main = lax.dynamic_slice(ctf_table, (0, 256 * chunk), (CLASSES, 256))
    ctf_rem = lax.dynamic_slice(ctf_table, (0, 8192 + 32 * chunk), (CLASSES, 32))
    eye = jnp.eye(CLASSES, dtype=F32)
    ctf_ext = jnp.concatenate([ctf_main, ctf_rem, ctf_rem, ctf_rem, eye, eye], axis=1)
    square = jnp.concatenate([ctf_main, ctf_rem], axis=1)
    square = square * square
    to_class = jnp.pad(jnp.concatenate([square.T, square.T], axis=1), ((0, 96), (96, 0)))
    to_pixel = jnp.pad(square, ((96, 16), (0, 96)))

    buf = exchange(pack(images, templates, meta))
    n = buf.shape[0]
    tpl = buf[:, IMG:]
    sides = tpl.reshape(n // 2, 2, TPL, LANES)
    below = along_z(sides[:, 1], 1)
    above = along_z(sides[:, 0], -1)
    halo = jnp.concatenate([below, above], axis=0)
    xh, xl, xr, own = own_scores(buf, tpl, ctf_ext, to_class)
    partial = halo_scores(xh, xl, xr, own, tpl, halo, to_class)
    place = jnp.stack([xlo, first]).astype(jnp.int32)
    log_total, mean_shift, p = home(place, exchange(partial), prior_center[None])
    p = exchange(p)
    edge = sums("halo", p, tpl, xh, xl, xr)
    from_above = along_z(edge[:256], -1)
    from_below = along_z(edge[256:], 1)
    mine = sums("own", p, tpl, xh, xl, xr)
    out = averages(mine, from_below, from_above, to_pixel, n)
    average = unpack(exchange(out), pixels)
    return log_total[0], mean_shift[0], average


def solution(mesh):
    dirs, psis = mesh.devices.shape
    fine = Mesh(mesh.devices.reshape(dirs, psis // 2, 2), ("dir", "z", "xlo"))
    rows = P(("dir", "z", "xlo"))
    grid = P("dir", ("z", "xlo"), None)
    return jax.shard_map(
        local,
        mesh=fine,
        in_specs=(P(("dir", "z", "xlo"), None), rows, rows, rows, grid, P()),
        out_specs=(rows, rows, grid),
        check_vma=False,
    )
```

time: 294 us -> 191 us (0.65)
  waiting for transfers between devices: 172 us -> 82.8 us
  local copies, waits for them, and re-layouts: 54.8 us -> 13.3 us
  Pallas kernels: 0 us -> 38.6 us
  blocking collectives: 0 us -> 29.3 us
  matrix products: 26.8 us -> 0 us
  starting transfers between devices: 33.8 us -> 23.2 us
    ppermute x6 -> x4, waiting for transfers between devices: 154 us -> 4.37 us  [along_z(): return lax.ppermute(value, 'z', [(i, (i + by) % size) for i in range(size)])]
    all_to_all x3 -> x2, waiting for transfers between devices: 18.2 us -> 78.5 us  [exchange(): return lax.all_to_all(value, PLANE, split_axis=0, concat_axis=0, tiled=True)]
    pallas_call x0 -> x8, Pallas kernels: none -> 38.6 us  [the longest x1 14.9 us: own_scores(): pl.pallas_call(own_kernel, grid=(n // 4,), in_specs=[block(4, IMG, LANES)...]
    all_to_all x0 -> x2, blocking collectives: none -> 29.3 us  [exchange(): return lax.all_to_all(value, PLANE, split_axis=0, concat_axis=0, tiled=True)]
    dot_general x7 -> x0, matrix products: 26.8 us -> none  [the longest x1 8.44 us: local(): crossed = jnp.einsum('bsk,bak->bsa', weighted, nearby, precision=highest)]
    reshape x5 -> x0, local copies, waits for them, and re-layouts: 12.5 us -> none  [the longest x1 10.5 us: local(): send_images = jnp.zeros((total_slots, pixels), jnp.float32).at[slot_index...]
    scatter x3 -> x0, local copies, waits for them, and re-layouts: 11.3 us -> none  [the longest x1 9.08 us: local(): send_images = jnp.zeros((total_slots, pixels), jnp.float32).at[slot_index...]
    unnamed x8 -> x19, local copies, waits for them, and re-layouts: 0.6 us -> 11.7 us
  transfers between devices with their start and end apart: 9 -> 6, of which waited for: 3 -> 4; matrix products, arithmetic and copies ran while one was open for 12% -> 0% of each run, Pallas kernels for 0% -> 12%
where the time goes in v1:
time: 191 us; the launch traced here: 189 us
  waiting for transfers between devices  82.8 us (43%)
  Pallas kernels  38.6 us (20%)
  blocking collectives  29.3 us (15%)
  starting transfers between devices  23.2 us (12%)
  local copies, waits for them, and re-layouts  13.3 us (7%)
    all_to_all x2, waiting for transfers between devices, exchange(): return lax.all_to_all(value, PLANE, split_axis=0, concat_axis=0, tiled=True)  78.5 us
    all_to_all x2, blocking collectives, exchange(): return lax.all_to_all(value, PLANE, split_axis=0, concat_axis=0, tiled=True)  29.3 us
    all_to_all x2, starting transfers between devices, exchange(): return lax.all_to_all(value, PLANE, split_axis=0, concat_axis=0, tiled=True)  17.8 us
    pallas_call x1, Pallas kernels, own_scores(): pl.pallas_call(own_kernel, grid=(n // 4,), in_specs=[block(4, IMG, LANES)...  14.9 us
    unnamed x19, local copies, waits for them, and re-layouts  11.7 us
    pallas_call x2, Pallas kernels, sums(): pl.pallas_call(body, grid=(n // 4,), in_specs=[block(4, 16, 128), whole((...  11.1 us
    pallas_call x1, Pallas kernels, halo_scores(): pl.pallas_call(halo_kernel, grid=(n // 4,), in_specs=[block(4, 128, 256),...  7.66 us
    ppermute x4, starting transfers between devices, along_z(): return lax.ppermute(value, 'z', [(i, (i + by) % size) for i in range(size)])  5.42 us
  transfers between devices with their start and end apart: 6, of which 4 were waited for; matrix products, arithmetic and copies ran while one was open for 0% of the time, Pallas kernels for 12%

profile of v1, /device:TPU:96, one launch (start us, length us, event | category | flops | bytes accessed | tf_op | source)
XLA Modules:
  0.0 188.9 jit_solution(15447692399470628371)
XLA Ops:
  1.4 2.3 %copy-done.2 = f32[128,9216]{1,0:T(8,128)S(1)} copy-done((f32[128,9216]{1,0:T(8,128)S(1)}, f32[128,9216]{1,0:T(8,128)}, u32[]{:S(2)}) %copy-start.2) | copy-done | bytes 4718616
  4.8 1.7 pack.1
  6.5 2.4 %copy-done.1 = f32[32,328,128]{2,1,0:T(8,128)} copy-done((f32[32,328,128]{2,1,0:T(8,128)}, f32[32,328,128]{2,1,0:T(8,128)S(1)}, u32[]{:S(2)}) %copy-start.1) | copy-done | bytes 5373976
  8.9 7.4 %all-to-all-start = ((f32[32,328,128]{2,1,0:T(8,128)}), f32[32,328,128]{2,1,0:T(8,128)}, u32[]{:S(2)}, u32[]{:S(2)}) async-start(f32[32,328,128]{2,1,0:T(8,128)} %copy-done.1), calls=%async_computation | async-start | bytes 10747904 | tf_op jit(solution)/shard_map/all_to_all | solution.py:420
  16.8 69.1 %all-to-all-done.buf_ref = f32[32,328,128]{2,1,0:T(8,128)} async-done(((f32[32,328,128]{2,1,0:T(8,128)}), f32[32,328,128]{2,1,0:T(8,128)}, u32[]{:S(2)}, u32[]{:S(2)}) %all-to-all-start) | async-done | bytes 5373984 | tf_op jit(solution)/shard_map/all_to_all | solution.py:420
  85.9 1.1 slice.20.tpl_ref.refs_1_
  87.3 3.1 %collective-permute-start = (f32[16,40,128]{2,1,0:T(8,128)S(1)}, f32[16,40,128]{2,1,0:T(8,128)S(1)}, u32[]{:S(2)}, u32[]{:S(2)}) collective-permute-start(f32[16,40,128]{2,1,0:T(8,128)S(1)} %get-tuple-element.19), channel_id=1, source_target_pairs={{0,2},{2,4},{4,6},{6,8},{8,10},{10,12},{12,14},{14,0},{1,3},{3,5},... | collective-permute-start | bytes 983048 | tf_op jit(solution)/shard_map/ppermute | solution.py:425
  90.4 14.9 %own_scores.1 = (bf16[32,128,256]{2,1,0:T(8,128)(2,1)S(1)}, bf16[32,128,256]{2,1,0:T(8,128)(2,1)S(1)}, bf16[32,128,128]{2,1,0:T(8,128)(2,1)S(1)}, f32[32,8,128]{2,1,0:T(8,128)S(1)}) custom-call(f32[32,328,128]{2,1,0:T(8,128)} %all-to-all-done.buf_ref, f32[32,40,128]{2,1,0:T(8,128)S(1)} %slice.20.tpl_ref.refs_1_, f32[16,384]{1,0:T(8,128)S(1)} %concatenate.12.ctf_ref, ...), custom_call_target="tpu_custom_call" | custom-call | flops 4000000000 | bytes 12000000 | tf_op jit(solution)/shard_map/own_scores/pallas_call | solution.py:183
  105.5 7.7 %halo_scores.1 = f32[32,16,128]{2,1,0:T(8,128)} custom-call(bf16[32,128,256]{2,1,0:T(8,128)(2,1)S(1)} %get-tuple-element.10.xh_ref.refs_2_, bf16[32,128,256]{2,1,0:T(8,128)(2,1)S(1)} %get-tuple-element.11.xl_ref.refs_3_, bf16[32,128,128]{2,1,0:T(8,128)(2,1)S(1)} %get-tuple-element.12.xr_ref.refs_4_, f32[32,8,128]{2,1,0:T(8,128)S(1)} %get-tuple-element.13.own_ref, ...), custom_call_target="tpu_custom_call" | custom-call | flops 2000000000 | bytes 6000000 | tf_op jit(solution)/shard_map/halo_scores/pallas_call | solution.py:231
  113.1 1.3 copy-done.5
  114.5 1.3 copy-done.7
  115.8 10.3 %all-to-all-start.1 = ((f32[32,16,128]{2,1,0:T(8,128)}), f32[32,16,128]{2,1,0:T(8,128)S(1)}, u32[]{:S(2)}, u32[]{:S(2)}) async-start(f32[32,16,128]{2,1,0:T(8,128)} %halo_scores.1), calls=%async_computation.1 | async-start | bytes 524288 | tf_op jit(solution)/shard_map/all_to_all | solution.py:420
  126.2 9.4 %all-to-all-done.1.scores_ref = f32[32,16,128]{2,1,0:T(8,128)S(1)} async-done(((f32[32,16,128]{2,1,0:T(8,128)}), f32[32,16,128]{2,1,0:T(8,128)S(1)}, u32[]{:S(2)}, u32[]{:S(2)}) %all-to-all-start.1) | async-done | bytes 262176 | tf_op jit(solution)/shard_map/all_to_all | solution.py:420
  135.5 1.1 home.1
  136.7 12.4 %all_to_all.20.refs_0_ = f32[32,16,128]{2,1,0:T(8,128)S(1)} all-to-all(f32[32,16,128]{2,1,0:T(8,128)S(1)} %get-tuple-element.16), channel_id=1, replica_groups=mesh['dir'=16,'z'=8,'xlo'=2] {'dir','xlo'}, dimensions={0} | all-to-all | bytes 524288 | tf_op jit(solution)/shard_map/all_to_all | solution.py:420
  149.1 1.6 copy-done.6
  150.7 1.6 copy-done.8
  152.3 4.1 %sums_halo.1 = f32[512,384]{1,0:T(8,128)S(1)} custom-call(f32[32,16,128]{2,1,0:T(8,128)S(1)} %all_to_all.20.refs_0_, f32[32,40,128]{2,1,0:T(8,128)S(1)} %slice.20.tpl_ref.refs_1_, bf16[32,128,256]{2,1,0:T(8,128)(2,1)S(1)} %copy-done.6, bf16[32,128,256]{2,1,0:T(8,128)(2,1)S(1)} %copy-done.8, bf16[32,128,128]{2,1,0:T(8,128)(2,1)S(1)} %get-tuple-element.12.xr_ref.refs_4_), custom_call_target="tpu_custom_call" | custom-call | flops 4000000000 | bytes 6000000 | tf_op jit(solution)/shard_map/sums_halo/pallas_call | solution.py:350
  156.5 2.0 %collective-permute-start.2 = (f32[256,384]{1,0:T(8,128)S(1)}, f32[256,384]{1,0:T(8,128)S(1)}, u32[]{:S(2)}, u32[]{:S(2)}) collective-permute-start(f32[256,384]{1,0:T(8,128)S(1)} %get-tuple-element.18), channel_id=1, source_target_pairs={{0,2},{2,4},{4,6},{6,8},{8,10},{10,12},{12,14},{14,0},{1,3},{3,5},... | collective-permute-start | bytes 1179656 | tf_op jit(solution)/shard_map/ppermute | solution.py:425
  158.6 6.9 %sums_own.1.own_ref = f32[512,384]{1,0:T(8,128)S(1)} custom-call(f32[32,16,128]{2,1,0:T(8,128)S(1)} %all_to_all.20.refs_0_, f32[32,40,128]{2,1,0:T(8,128)S(1)} %slice.20.tpl_ref.refs_1_, bf16[32,128,256]{2,1,0:T(8,128)(2,1)S(1)} %copy-done.6, bf16[32,128,256]{2,1,0:T(8,128)(2,1)S(1)} %copy-done.8, bf16[32,128,128]{2,1,0:T(8,128)(2,1)S(1)} %get-tuple-element.12.xr_ref.refs_4_), custom_call_target="tpu_custom_call" | custom-call | flops 4000000000 | bytes 6000000 | tf_op jit(solution)/shard_map/sums_own/pallas_call | solution.py:350
  165.5 1.5 collective-permute-done.2.below_ref
  167.0 2.9 %collective-permute-done.3.above_ref = f32[256,384]{1,0:T(8,128)S(1)} collective-permute-done((f32[256,384]{1,0:T(8,128)S(1)}, f32[256,384]{1,0:T(8,128)S(1)}, u32[]{:S(2)}, u32[]{:S(2)}) %collective-permute-start.3) | collective-permute-done | bytes 393248 | tf_op jit(solution)/shard_map/ppermute | solution.py:425
  169.9 1.1 averages.1
  171.0 16.9 %all_to_all.21.got_ref = f32[32,40,128]{2,1,0:T(8,128)S(1)} all-to-all(f32[32,40,128]{2,1,0:T(8,128)S(1)} %averages.1), channel_id=1, replica_groups=mesh['dir'=16,'z'=8,'xlo'=2] {'dir','xlo'}, dimensions={0} | all-to-all | bytes 1310720 | tf_op jit(solution)/shard_map/all_to_all | solution.py:420
  (31 shorter events, 3.8 us)
Async XLA Ops:
  0.6 15.8 %copy-start = (f32[16,9216]{1,0:T(8,128)S(1)}, f32[16,9216]{1,0:T(8,128)}, u32[]{:S(2)}) copy-start(f32[16,9216]{1,0:T(8,128)} %param.11) | copy-start | bytes 1769476
  1.4 2.3 %copy-start.2 = (f32[128,9216]{1,0:T(8,128)S(1)}, f32[128,9216]{1,0:T(8,128)}, u32[]{:S(2)}) copy-start(f32[128,9216]{1,0:T(8,128)} %rem_ref.1) | copy-start | bytes 14155780
  3.8 1.1 copy-start.3
  6.5 2.4 %copy-start.1 = (f32[32,328,128]{2,1,0:T(8,128)}, f32[32,328,128]{2,1,0:T(8,128)S(1)}, u32[]{:S(2)}) copy-start(f32[32,328,128]{2,1,0:T(8,128)S(1)} %pack.1) | copy-start | bytes 16121860
  8.9 77.0 %all-to-all-start = ((f32[32,328,128]{2,1,0:T(8,128)}), f32[32,328,128]{2,1,0:T(8,128)}, u32[]{:S(2)}, u32[]{:S(2)}) async-start(f32[32,328,128]{2,1,0:T(8,128)} %copy-done.1), calls=%async_computation | async-start | bytes 10747904 | tf_op jit(solution)/shard_map/all_to_all | solution.py:420
  87.1 18.3 %collective-permute-start.1 = (f32[16,40,128]{2,1,0:T(8,128)S(1)}, f32[16,40,128]{2,1,0:T(8,128)S(1)}, u32[]{:S(2)}, u32[]{:S(2)}) collective-permute-start(f32[16,40,128]{2,1,0:T(8,128)S(1)} %get-tuple-element.20), channel_id=1, source_target_pairs={{0,14},{2,0},{4,2},{6,4},{8,6},{10,8},{12,10},{14,12},{1,15},{3,1}... | collective-permute-start | bytes 983048 | tf_op jit(solution)/shard_map/ppermute | solution.py:425
  87.3 18.1 %collective-permute-start = (f32[16,40,128]{2,1,0:T(8,128)S(1)}, f32[16,40,128]{2,1,0:T(8,128)S(1)}, u32[]{:S(2)}, u32[]{:S(2)}) collective-permute-start(f32[16,40,128]{2,1,0:T(8,128)S(1)} %get-tuple-element.19), channel_id=1, source_target_pairs={{0,2},{2,4},{4,6},{6,8},{8,10},{10,12},{12,14},{14,0},{1,3},{3,5},... | collective-permute-start | bytes 983048 | tf_op jit(solution)/shard_map/ppermute | solution.py:425
  105.4 30.2 %copy-start.4 = (s32[128]{0:T(128)S(1)}, s32[128]{0:T(128)}, u32[]{:S(2)}) copy-start(s32[128]{0:T(128)} %param.8) | copy-start | bytes 1540
  113.1 1.3 copy-start.5
  114.5 1.3 copy-start.7
  115.8 19.8 %all-to-all-start.1 = ((f32[32,16,128]{2,1,0:T(8,128)}), f32[32,16,128]{2,1,0:T(8,128)S(1)}, u32[]{:S(2)}, u32[]{:S(2)}) async-start(f32[32,16,128]{2,1,0:T(8,128)} %halo_scores.1), calls=%async_computation.1 | async-start | bytes 524288 | tf_op jit(solution)/shard_map/all_to_all | solution.py:420
  149.1 1.6 copy-start.6
  150.7 1.6 copy-start.8
  156.5 10.6 %collective-permute-start.2 = (f32[256,384]{1,0:T(8,128)S(1)}, f32[256,384]{1,0:T(8,128)S(1)}, u32[]{:S(2)}, u32[]{:S(2)}) collective-permute-start(f32[256,384]{1,0:T(8,128)S(1)} %get-tuple-element.18), channel_id=1, source_target_pairs={{0,2},{2,4},{4,6},{6,8},{8,10},{10,12},{12,14},{14,0},{1,3},{3,5},... | collective-permute-start | bytes 1179656 | tf_op jit(solution)/shard_map/ppermute | solution.py:425
  158.5 11.4 %collective-permute-start.3 = (f32[256,384]{1,0:T(8,128)S(1)}, f32[256,384]{1,0:T(8,128)S(1)}, u32[]{:S(2)}, u32[]{:S(2)}) collective-permute-start(f32[256,384]{1,0:T(8,128)S(1)} %get-tuple-element.17), channel_id=1, source_target_pairs={{0,14},{2,0},{4,2},{6,4},{8,6},{10,8},{12,10},{14,12},{1,15},{3,1}... | collective-permute-start | bytes 1179656 | tf_op jit(solution)/shard_map/ppermute | solution.py:425

commit v2 on v1

v2 whole, which is shorter than its diff:
```python
import jax
import jax.numpy as jnp
from jax import lax
from jax.experimental import pallas as pl
from jax.experimental.pallas import tpu as pltpu
from jax.sharding import Mesh
from jax.sharding import PartitionSpec as P

HALF = 4
LANES = 128
CLASSES = 16
IMG = 288
TPL = 40
META = 36
BF = jnp.bfloat16
F32 = jnp.float32
HIGHEST = lax.Precision.HIGHEST
PLANE = ("dir", "xlo")


def params(mib):
    return pltpu.CompilerParams(vmem_limit_bytes=mib * 1024 * 1024)


def cost(flops, moved):
    return pl.CostEstimate(flops=flops, bytes_accessed=moved, transcendentals=0)


def lane_group(shape):
    return lax.broadcasted_iota(jnp.int32, shape, len(shape) - 1) // 32


def turned(x, groups):
    groups = groups % 4
    return x if groups == 0 else pltpu.roll(x, 32 * groups, x.ndim - 1)


def pick_groups(parts):
    group = lane_group(parts[0].shape)
    out = parts[3]
    for q in (2, 1, 0):
        out = jnp.where(group == q, parts[q], out)
    return out


def split(x):
    hi = x.astype(BF)
    return hi, (x - hi.astype(F32)).astype(BF)


def pack_images_kernel(img_ref, rem_ref, out_ref):
    for q in range(4):
        for j in range(2):
            out_ref[q, pl.ds(j * 128, 128), :] = img_ref[:, pl.ds((2 * q + j) * LANES, LANES)]
        out_ref[q, pl.ds(256, 32), :] = pick_groups([turned(rem_ref[pl.ds(32 * g, 32), :], g - q) for g in range(4)])


def pack_images(images):
    steps = 8
    return pl.pallas_call(
        pack_images_kernel,
        grid=(steps,),
        in_specs=[
            pl.BlockSpec((128, 1024), lambda t: (0, t)),
            pl.BlockSpec((128, LANES), lambda t: (0, 64 + t)),
        ],
        out_specs=pl.BlockSpec((4, IMG, LANES), lambda t: (t, 0, 0)),
        out_shape=jax.ShapeDtypeStruct((4 * steps, IMG, LANES), F32),
        compiler_params=params(60),
        cost_estimate=cost(0, 9_500_000),
        name="pack_images",
    )(images, images)


def pack_templates_kernel(tpl_ref, meta_ref, out_ref):
    meta = meta_ref[...]
    for t in range(8):
        rem = [tpl_ref[b, :, pl.ds((64 + t) * LANES, LANES)] for b in range(4)]
        for q in range(4):
            dest = 4 * t + q
            for j in range(2):
                for b in range(4):
                    out_ref[dest, pl.ds(16 * j + 4 * b, 4), :] = tpl_ref[b, :, pl.ds((2 * dest + j) * LANES, LANES)]
            out_ref[dest, pl.ds(32, 4), :] = pick_groups([turned(rem[b], b - q) for b in range(4)])
            out_ref[dest, pl.ds(META, 4), :] = meta


def pack_templates(templates, meta):
    vmem = pl.BlockSpec(memory_space=pltpu.VMEM)
    return pl.pallas_call(
        pack_templates_kernel,
        in_specs=[vmem, vmem],
        out_specs=vmem,
        out_shape=jax.ShapeDtypeStruct((32, TPL, LANES), F32),
        compiler_params=params(8),
        cost_estimate=cost(0, 1_300_000),
        name="pack_templates",
    )(templates, meta)


def operands_kernel(tpl_ref, below_ref, above_ref, ctf_ref, sq_ref, y_ref, ce_ref, tf_ref):
    for block in range(4):
        for d in range(16):
            at = lambda rows: (below_ref, tpl_ref, tpl_ref, above_ref)[block][(d, 2 * d, 2 * d + 1, d)[block], rows, :]
            rows = pl.ds(16 * d, 16)
            tf_ref[rows, pl.ds(0, 128)] = at(pl.ds(0, 16))
            tf_ref[rows, pl.ds(128, 128)] = at(pl.ds(16, 16))
            packed = at(pl.ds(32, 4))
            v = [turned(packed, j) for j in range(4)]
            for b in range(4):
                tail = pick_groups([v[(q - b) % 4] for q in (0, 1, 2)] + [jnp.zeros_like(packed)])
                tf_ref[pl.ds(16 * d + 4 * b, 4), pl.ds(256, 128)] = tail
        for c in range(4):
            out = pl.ds(256 * block + 64 * c, 64)
            full = tf_ref[pl.ds(64 * c, 64), :]
            quad = jnp.dot(full * full, sq_ref[...], precision=HIGHEST, preferred_element_type=F32)
            hi, lo = split(full)
            vh, vl = split(-0.5 * quad)
            lane = lax.broadcasted_iota(jnp.int32, (64, LANES), 1)
            last = jnp.where(lane < 112, vh.astype(F32), vl.astype(F32))
            tail = jnp.where(lane < 64, hi[:, 256:].astype(F32), lo[:, 256:].astype(F32))
            y_ref[out, pl.ds(0, 256)] = hi[:, :256]
            y_ref[out, pl.ds(256, 256)] = lo[:, :256]
            y_ref[out, pl.ds(512, 256)] = hi[:, :256]
            y_ref[out, pl.ds(768, 128)] = jnp.where(lane < 96, tail, last).astype(BF)
    ctf = ctf_ref[...]
    hi, mid = split(ctf)
    ce_ref[pl.ds(0, 16), :] = hi
    ce_ref[pl.ds(16, 16), :] = mid
    ce_ref[pl.ds(32, 16), :] = (ctf - hi.astype(F32) - mid.astype(F32)).astype(BF)


def operands(tpl, below, above, ctf_ext, squares):
    vmem = pl.BlockSpec(memory_space=pltpu.VMEM)
    return pl.pallas_call(
        operands_kernel,
        in_specs=[vmem] * 5,
        out_specs=[vmem, vmem],
        out_shape=[jax.ShapeDtypeStruct((1024, 896), BF), jax.ShapeDtypeStruct((48, 384), BF)],
        scratch_shapes=[pltpu.VMEM((256, 384), F32)],
        compiler_params=params(12),
        cost_estimate=cost(600_000_000, 4_000_000),
        name="operands",
    )(tpl, below, above, ctf_ext, squares)


def bins_of(tpl_ref, sources):
    rows = [tpl_ref[s, pl.ds(META, 1), :] for s in sources]
    return jnp.concatenate(rows, axis=1).astype(jnp.int32)


def scores_kernel(buf_ref, tpl_ref, y_ref, ce_ref, xh_ref, xl_ref, xr_ref, out_ref):
    step = pl.program_id(0)
    group = lane_group((128, LANES))
    for s in range(4):
        source = 4 * step + s
        classes = tpl_ref[source, pl.ds(META + 2, 1), :].astype(jnp.int32)
        row_class = lax.broadcasted_iota(jnp.int32, (48, 128), 0) % CLASSES
        onehot = jnp.where(row_class == classes, 1.0, 0.0).astype(BF)
        ctf = lax.dot_general(onehot, ce_ref[...], (((0,), (0,)), ((), ())), preferred_element_type=F32)
        for j in range(2):
            hi, lo = split(ctf[:, 128 * j : 128 * j + 128] * buf_ref[s, pl.ds(128 * j, 128), :])
            xh_ref[s, :, pl.ds(128 * j, 128)] = hi
            xl_ref[s, :, pl.ds(128 * j, 128)] = lo
        packed = buf_ref[s, pl.ds(256, 32), :]
        v = [turned(packed, j) for j in range(4)]
        one = jnp.ones_like(packed)
        rem = jnp.concatenate([pick_groups([v[(q - g) % 4] for q in (0, 1, 2)] + [one]) for g in range(4)], axis=0)
        hi, lo = split(ctf[:, 256:] * rem)
        xr_ref[s, :, :] = jnp.where(group == 1, lo.astype(F32), hi.astype(F32)).astype(BF)
    row_bin = lax.broadcasted_iota(jnp.int32, (256, 256), 0) // 4
    half = lax.broadcasted_iota(jnp.int32, (8, 256), 0) < 4
    for side in range(2):
        pair = (side, 2 + side)
        x = jnp.concatenate(
            [jnp.concatenate([xh_ref[s], xh_ref[s], xl_ref[s], xr_ref[s]], axis=1) for s in pair], axis=0
        )
        mine = row_bin == bins_of(tpl_ref, [4 * step + s for s in pair])
        all_rows = lax.dot_general(
            y_ref[pl.ds(256 * side, 768), :], x, (((1,), (1,)), ((), ())), preferred_element_type=F32
        )
        blocks = []
        for k in range(3):
            kept = jnp.where(mine, all_rows[256 * k : 256 * k + 256], 0.0)
            total = jnp.sum(kept.reshape(32, 8, 256), axis=0)
            blocks.append(total + pltpu.roll(total, 4, 0))
        edge, low, high = blocks if side == 0 else (blocks[2], blocks[0], blocks[1])
        own = jnp.where(half, low, high)
        for k, s in enumerate(pair):
            cols = slice(128 * k, 128 * k + 128)
            out_ref[s, pl.ds(0, 8), :] = own[:, cols]
            out_ref[s, pl.ds(8, 8), :] = edge[:, cols]


def window_scores(buf, tpl, y, ctf):
    n = buf.shape[0]
    whole = lambda shape: pl.BlockSpec(shape, lambda p: (0,) * len(shape))
    block = lambda *shape: pl.BlockSpec(shape, lambda p: (p,) + (0,) * (len(shape) - 1))
    return pl.pallas_call(
        scores_kernel,
        grid=(n // 4,),
        in_specs=[block(4, IMG, LANES), whole((n, TPL, LANES)), whole((1024, 896)), whole((48, 384))],
        out_specs=[block(4, 128, 256), block(4, 128, 256), block(4, 128, 128), block(4, 16, 128)],
        out_shape=[
            jax.ShapeDtypeStruct((n, 128, 256), BF),
            jax.ShapeDtypeStruct((n, 128, 256), BF),
            jax.ShapeDtypeStruct((n, 128, 128), BF),
            jax.ShapeDtypeStruct((n, 16, 128), F32),
        ],
        compiler_params=params(60),
        cost_estimate=cost(6_000_000_000, 14_000_000),
        name="window_scores",
    )(buf, tpl, y, ctf)


def home_kernel(place_ref, scores_ref, centre_ref, total_ref, shift_ref, p_ref):
    xlo = place_ref[0]
    first = place_ref[1]
    n = scores_ref.shape[0]
    scores = scores_ref[0]
    for s in range(1, n):
        scores = scores + scores_ref[s]
    row = lax.broadcasted_iota(jnp.int32, scores.shape, 0)
    angle = jnp.where(row < 8, row + 4, row - 8 + 12 * xlo)
    offset = angle - (centre_ref[...] - first + 4)
    inside = jnp.logical_and(jnp.abs(offset) <= HALF, row < 12)
    safe = jnp.where(inside, scores, 0.0)
    total = jnp.log(jnp.sum(jnp.where(inside, jnp.exp(safe), 0.0), axis=0, keepdims=True))
    p = jnp.where(inside, jnp.exp(safe - total), 0.0)
    total_ref[...] = total
    shift_ref[...] = jnp.sum(p * offset.astype(F32), axis=0, keepdims=True)
    p = jnp.where(row < 12, p, pltpu.roll(p, 4, 0))
    for s in range(n):
        p_ref[s] = p


def home(place, scores, centre):
    n = scores.shape[0]
    vmem = pl.BlockSpec(memory_space=pltpu.VMEM)
    return pl.pallas_call(
        home_kernel,
        in_specs=[pl.BlockSpec(memory_space=pltpu.SMEM), vmem, vmem],
        out_specs=[vmem, vmem, vmem],
        out_shape=[
            jax.ShapeDtypeStruct((1, 128), F32),
            jax.ShapeDtypeStruct((1, 128), F32),
            jax.ShapeDtypeStruct((n, 16, 128), F32),
        ],
        compiler_params=params(4),
        cost_estimate=cost(200_000, 600_000),
        name="home",
    )(place, scores, centre)


def spread(p8, bins, first_bin, rows):
    n = p8.shape[1]
    row_bin = lax.broadcasted_iota(jnp.int32, (rows, n), 0) // 4 + first_bin
    mine = row_bin == bins
    hi = p8.astype(BF).astype(F32)
    lo = p8 - hi
    wide = lambda v: jnp.broadcast_to(v[None], (rows // 8, 8, n)).reshape(rows, n)
    return [jnp.where(mine, wide(v), 0.0).astype(BF) for v in (hi, lo)]


def sums_kernel(which, p_ref, tpl_ref, xh_ref, xl_ref, xr_ref, out_ref):
    step = pl.program_id(0)

    @pl.when(step == 0)
    def _():
        out_ref[...] = jnp.zeros_like(out_ref)

    def add(rows, high, low, sources):
        stack = lambda ref: jnp.concatenate([ref[s] for s in sources], axis=0)
        xh, xl, xr = stack(xh_ref), stack(xl_ref), stack(xr_ref)
        left = jnp.concatenate([high, low, high], axis=1)
        main = jnp.dot(left, jnp.concatenate([xh, xh, xl], axis=0), preferred_element_type=F32)
        wide = left.shape[1] // 3 * 2
        tail = jnp.dot(left[:, :wide], jnp.concatenate([xr, xr], axis=0), preferred_element_type=F32)
        out_ref[rows, pl.ds(0, 256)] += main
        out_ref[rows, pl.ds(256, 128)] += tail

    if which == "halo":
        for side in range(2):
            pair = (side, 2 + side)
            p8 = jnp.concatenate([p_ref[s, pl.ds(8, 8), :] for s in pair], axis=1)
            high, low = spread(p8, bins_of(tpl_ref, [4 * step + s for s in pair]), 0, 256)
            add(pl.ds(256 * side, 256), high, low, pair)
    else:
        four = range(4)
        half = lax.broadcasted_iota(jnp.int32, (8, 512), 0) < 4
        bins = bins_of(tpl_ref, [4 * step + s for s in four])
        own = jnp.concatenate([p_ref[s, pl.ds(0, 8), :] for s in four], axis=1)
        other = pltpu.roll(own, 4, 0)
        for k, p8 in enumerate((jnp.where(half, own, other), jnp.where(half, other, own))):
            high, low = spread(p8, bins, 0, 256)
            add(pl.ds(256 * k, 256), high, low, four)


def sums(which, p, tpl, xh, xl, xr):
    n = xh.shape[0]
    whole = lambda shape: pl.BlockSpec(shape, lambda i: (0,) * len(shape))
    block = lambda *shape: pl.BlockSpec(shape, lambda i: (i,) + (0,) * (len(shape) - 1))

    def body(*refs):
        sums_kernel(which, *refs)

    return pl.pallas_call(
        body,
        grid=(n // 4,),
        in_specs=[block(4, 16, 128), whole((n, TPL, LANES)), block(4, 128, 256), block(4, 128, 256), block(4, 128, 128)],
        out_specs=whole((512, 384)),
        out_shape=jax.ShapeDtypeStruct((512, 384), F32),
        compiler_params=params(60),
        cost_estimate=cost(4_000_000_000, 6_000_000),
        name="sums_" + which,
    )(p, tpl, xh, xl, xr)


def average_kernel(own_ref, below_ref, above_ref, sq_ref, out_ref):
    for side, other_ref in ((0, below_ref), (1, above_ref)):
        for c in range(4):
            rows = pl.ds(64 * c, 64)
            total = own_ref[pl.ds(256 * side + 64 * c, 64), :] + other_ref[rows, :]
            weight = jnp.dot(total[:, 256:], sq_ref[...], precision=HIGHEST, preferred_element_type=F32)
            tail = total[:, 256:]
            tail = tail + pltpu.roll(tail, 96, 1)
            mean = jnp.concatenate([total[:, :256], tail], axis=1) / (weight + 1.0)
            for d in range(4):
                dest = 2 * (4 * c + d) + side
                piece = mean[16 * d : 16 * d + 16]
                out_ref[dest, pl.ds(0, 16), :] = piece[:, :128]
                out_ref[dest, pl.ds(16, 16), :] = piece[:, 128:256]
                rem = [piece[4 * b : 4 * b + 4, 256:] for b in range(4)]
                out_ref[dest, pl.ds(32, 4), :] = pick_groups([turned(rem[b], b) for b in range(4)])
                out_ref[dest, pl.ds(36, 4), :] = jnp.zeros((4, LANES), F32)


def averages(own, below, above, squares, n):
    vmem = pl.BlockSpec(memory_space=pltpu.VMEM)
    return pl.pallas_call(
        average_kernel,
        in_specs=[vmem] * 4,
        out_specs=vmem,
        out_shape=jax.ShapeDtypeStruct((n, 40, LANES), F32),
        compiler_params=params(8),
        cost_estimate=cost(200_000_000, 3_000_000),
        name="averages",
    )(own, below, above, squares)


def unpack_kernel(got_ref, out_ref):
    n = got_ref.shape[0]
    for i in range(n):
        for j in range(2):
            for b in range(4):
                out_ref[b, :, pl.ds(256 * i + 128 * j, 128)] = got_ref[i, pl.ds(16 * j + 4 * b, 4), :]
    for t in range(n // 4):
        rem = [got_ref[4 * t + q, pl.ds(32, 4), :] for q in range(4)]
        for b in range(4):
            out_ref[b, :, pl.ds(256 * n + 128 * t, 128)] = pick_groups([turned(rem[q], q - b) for q in range(4)])


def unpack(got, pixels):
    vmem = pl.BlockSpec(memory_space=pltpu.VMEM)
    return pl.pallas_call(
        unpack_kernel,
        in_specs=[vmem],
        out_specs=vmem,
        out_shape=jax.ShapeDtypeStruct((4, 4, pixels), F32),
        compiler_params=params(8),
        cost_estimate=cost(0, 1_200_000),
        name="unpack",
    )(got)


def exchange(value):
    return lax.all_to_all(value, PLANE, split_axis=0, concat_axis=0, tiled=True)


def along_z(value, by):
    size = lax.axis_size("z")
    return lax.ppermute(value, "z", [(i, (i + by) % size) for i in range(size)])


def local(images, prior_bin, prior_center, defocus_class, templates, ctf_table):
    pixels = images.shape[1]
    xlo = lax.axis_index("xlo")
    chunk = lax.axis_index("dir") * 2 + xlo
    first = lax.axis_index("z") * 8
    meta = jnp.stack([prior_bin, prior_center, defocus_class, defocus_class]).astype(F32)
    ctf_main = lax.dynamic_slice(ctf_table, (0, 256 * chunk), (CLASSES, 256))
    ctf_rem = lax.dynamic_slice(ctf_table, (0, 8192 + 32 * chunk), (CLASSES, 32))
    eye = jnp.eye(CLASSES, dtype=F32)
    ctf_ext = jnp.concatenate([ctf_main, ctf_rem, ctf_rem, ctf_rem, eye, eye], axis=1)
    square = jnp.concatenate([ctf_main, ctf_rem], axis=1)
    square = square * square
    to_class = jnp.pad(jnp.concatenate([square.T, square.T], axis=1), ((0, 96), (96, 0)))
    to_pixel = jnp.pad(square, ((96, 16), (0, 96)))

    tpl = exchange(pack_templates(templates, meta))
    n = tpl.shape[0]
    buf = exchange(pack_images(images))
    sides = tpl.reshape(n // 2, 2, TPL, LANES)
    below = along_z(sides[:, 1], 1)
    above = along_z(sides[:, 0], -1)
    y, ctf = operands(tpl, below, above, ctf_ext, to_class)
    xh, xl, xr, partial = window_scores(buf, tpl, y, ctf)
    place = jnp.stack([xlo, first]).astype(jnp.int32)
    log_total, mean_shift, p = home(place, exchange(partial), prior_center[None])
    p = exchange(p)
    edge = sums("halo", p, tpl, xh, xl, xr)
    from_above = along_z(edge[:256], -1)
    from_below = along_z(edge[256:], 1)
    mine = sums("own", p, tpl, xh, xl, xr)
    out = averages(mine, from_below, from_above, to_pixel, n)
    average = unpack(exchange(out), pixels)
    return log_total[0], mean_shift[0], average


def solution(mesh):
    dirs, psis = mesh.devices.shape
    fine = Mesh(mesh.devices.reshape(dirs, psis // 2, 2), ("dir", "z", "xlo"))
    rows = P(("dir", "z", "xlo"))
    grid = P("dir", ("z", "xlo"), None)
    return jax.shard_map(
        local,
        mesh=fine,
        in_specs=(P(("dir", "z", "xlo"), None), rows, rows, rows, grid, P()),
        out_specs=(rows, rows, grid),
        check_vma=False,
    )
```

time: 191 us -> 182 us (0.953)
  waiting for transfers between devices: 82.8 us -> 68.5 us
  local copies, waits for them, and re-layouts: 13.3 us -> 5.66 us
  Pallas kernels: 38.6 us -> 45.1 us
  starting transfers between devices: 23.2 us -> 29.3 us
    all_to_all x2 -> x3, waiting for transfers between devices: 78.5 us -> 56.8 us  [exchange(): return lax.all_to_all(value, PLANE, split_axis=0, concat_axis=0, tiled=True)]
    unnamed x19 -> x15, local copies, waits for them, and re-layouts: 11.7 us -> 4.16 us
    ppermute x4, waiting for transfers between devices: 4.37 us -> 11.7 us  [along_z(): return lax.ppermute(value, 'z', [(i, (i + by) % size) for i in range(size)])]
    pallas_call x2, Pallas kernels: 11.1 us -> 18.2 us  [sums(): pl.pallas_call(body, grid=(n // 4,), in_specs=[block(4, 16, 128), whole((...]
    all_to_all x2 -> x3, starting transfers between devices: 17.8 us -> 22.9 us  [exchange(): return lax.all_to_all(value, PLANE, split_axis=0, concat_axis=0, tiled=True)]
    pallas_call x3 -> x4, Pallas kernels: 24.3 us -> 23.6 us  [the longest x1 13.3 us: window_scores(): pl.pallas_call(scores_kernel, grid=(n // 4,), in_specs=[block(4, IMG, LAN...]
  transfers between devices with their start and end apart: 6 -> 7, of which waited for: 4 -> 6; matrix products, arithmetic and copies ran while one was open for 0% -> 0% of each run, Pallas kernels for 12% -> 11%
where the time goes in v2:
time: 182 us; the launch traced here: 180 us
  waiting for transfers between devices  68.5 us (38%)
  Pallas kernels  45.1 us (25%)
  blocking collectives  30 us (16%)
  starting transfers between devices  29.3 us (16%)
  local copies, waits for them, and re-layouts  5.66 us (3%)
    all_to_all x3, waiting for transfers between devices, exchange(): return lax.all_to_all(value, PLANE, split_axis=0, concat_axis=0, tiled=True)  56.8 us
    all_to_all x2, blocking collectives, exchange(): return lax.all_to_all(value, PLANE, split_axis=0, concat_axis=0, tiled=True)  30 us
    all_to_all x3, starting transfers between devices, exchange(): return lax.all_to_all(value, PLANE, split_axis=0, concat_axis=0, tiled=True)  22.9 us
    pallas_call x2, Pallas kernels, sums(): pl.pallas_call(body, grid=(n // 4,), in_specs=[block(4, 16, 128), whole((...  18.2 us
    pallas_call x1, Pallas kernels, window_scores(): pl.pallas_call(scores_kernel, grid=(n // 4,), in_specs=[block(4, IMG, LAN...  13.3 us
    ppermute x4, waiting for transfers between devices, along_z(): return lax.ppermute(value, 'z', [(i, (i + by) % size) for i in range(size)])  11.7 us
    pallas_call x1, Pallas kernels, pack_images(): pl.pallas_call(pack_images_kernel, grid=(steps,), in_specs=[pl.BlockSpec(...  7.03 us
    ppermute x4, starting transfers between devices, along_z(): return lax.ppermute(value, 'z', [(i, (i + by) % size) for i in range(size)])  6.42 us
  transfers between devices with their start and end apart: 7, of which 6 were waited for; matrix products, arithmetic and copies ran while one was open for 0% of the time, Pallas kernels for 11%

profile of v2, /device:TPU:96, one launch (start us, length us, event | category | flops | bytes accessed | tf_op | source)
XLA Modules:
  0.0 180.1 jit_solution(17763073445474729601)
XLA Ops:
  1.4 1.1 copy-done.3
  3.5 7.3 %all-to-all-start.1 = ((f32[32,40,128]{2,1,0:T(8,128)}), f32[32,40,128]{2,1,0:T(8,128)S(1)}, u32[]{:S(2)}, u32[]{:S(2)}) async-start(f32[32,40,128]{2,1,0:T(8,128)} %pack_templates.1), calls=%async_computation.1 | async-start | bytes 1310720 | tf_op jit(solution)/shard_map/all_to_all | solution.py:377
  10.9 7.0 %pack_images.1 = f32[32,288,128]{2,1,0:T(8,128)} custom-call(f32[128,9216]{1,0:T(8,128)} %rem_ref.1, f32[128,9216]{1,0:T(8,128)} %rem_ref.1), custom_call_target="tpu_custom_call" | custom-call | bytes 9500000 | tf_op jit(solution)/shard_map/pack_images/pallas_call | solution.py:60
  17.9 6.4 %all-to-all-done.1.tpl_ref.refs_1_ = f32[32,40,128]{2,1,0:T(8,128)S(1)} async-done(((f32[32,40,128]{2,1,0:T(8,128)}), f32[32,40,128]{2,1,0:T(8,128)S(1)}, u32[]{:S(2)}, u32[]{:S(2)}) %all-to-all-start.1) | async-done | bytes 655392 | tf_op jit(solution)/shard_map/all_to_all | solution.py:377
  24.3 4.9 %all-to-all-start = ((f32[32,288,128]{2,1,0:T(8,128)}), f32[32,288,128]{2,1,0:T(8,128)}, u32[]{:S(2)}, u32[]{:S(2)}) async-start(f32[32,288,128]{2,1,0:T(8,128)} %pack_images.1), calls=%async_computation | async-start | bytes 9437184 | tf_op jit(solution)/shard_map/all_to_all | solution.py:377
  29.2 3.2 %collective-permute-start = (f32[16,40,128]{2,1,0:T(8,128)S(1)}, f32[16,40,128]{2,1,0:T(8,128)S(1)}, u32[]{:S(2)}, u32[]{:S(2)}) collective-permute-start(f32[16,40,128]{2,1,0:T(8,128)S(1)} %get-tuple-element.24), channel_id=1, source_target_pairs={{0,2},{2,4},{4,6},{6,8},{8,10},{10,12},{12,14},{14,0},{1,3},{3,5},... | collective-permute-start | bytes 983048 | tf_op jit(solution)/shard_map/ppermute | solution.py:382
  32.8 6.8 %collective-permute-done.below_ref = f32[16,40,128]{2,1,0:T(8,128)S(1)} collective-permute-done((f32[16,40,128]{2,1,0:T(8,128)S(1)}, f32[16,40,128]{2,1,0:T(8,128)S(1)}, u32[]{:S(2)}, u32[]{:S(2)}) %collective-permute-start) | collective-permute-done | bytes 327712 | tf_op jit(solution)/shard_map/ppermute | solution.py:382
  39.7 3.4 %collective-permute-done.1.above_ref = f32[16,40,128]{2,1,0:T(8,128)S(1)} collective-permute-done((f32[16,40,128]{2,1,0:T(8,128)S(1)}, f32[16,40,128]{2,1,0:T(8,128)S(1)}, u32[]{:S(2)}, u32[]{:S(2)}) %collective-permute-start.1) | collective-permute-done | bytes 327712 | tf_op jit(solution)/shard_map/ppermute | solution.py:382
  43.1 2.3 %operands.1 = (bf16[1024,896]{1,0:T(8,128)(2,1)S(1)}, bf16[48,384]{1,0:T(8,128)(2,1)S(1)}) custom-call(f32[32,40,128]{2,1,0:T(8,128)S(1)} %all-to-all-done.1.tpl_ref.refs_1_, f32[16,40,128]{2,1,0:T(8,128)S(1)} %collective-permute-done.below_ref, f32[16,40,128]{2,1,0:T(8,128)S(1)} %collective-permute-done.1.above_ref, f32[16,384]{1,0:T(8,128)S(1)} %concatenate.9.ctf_ref, ...), custom_call_target="tpu_custom_call" | custom-call | flops 600000000 | bytes 4000000 | tf_op jit(solution)/shard_map/operands/pallas_call | solution.py:135
  45.4 1.2 copy-done.5
  47.2 41.1 %all-to-all-done.buf_ref = f32[32,288,128]{2,1,0:T(8,128)} async-done(((f32[32,288,128]{2,1,0:T(8,128)}), f32[32,288,128]{2,1,0:T(8,128)}, u32[]{:S(2)}, u32[]{:S(2)}) %all-to-all-start) | async-done | bytes 4718624 | tf_op jit(solution)/shard_map/all_to_all | solution.py:377
  88.3 13.3 %window_scores.1 = (bf16[32,128,256]{2,1,0:T(8,128)(2,1)}, bf16[32,128,256]{2,1,0:T(8,128)(2,1)}, bf16[32,128,128]{2,1,0:T(8,128)(2,1)}, f32[32,16,128]{2,1,0:T(8,128)}) custom-call(f32[32,288,128]{2,1,0:T(8,128)} %all-to-all-done.buf_ref, f32[32,40,128]{2,1,0:T(8,128)} %copy-done.1, bf16[1024,896]{1,0:T(8,128)(2,1)} %copy-done.5, bf16[48,384]{1,0:T(8,128)(2,1)} %copy-done.6), custom_call_target="tpu_custom_call" | custom-call | flops 6000000000 | bytes 14000000 | tf_op jit(solution)/shard_map/window_scores/pallas_call | solution.py:199
  101.6 10.7 %all-to-all-start.2 = ((f32[32,16,128]{2,1,0:T(8,128)}), f32[32,16,128]{2,1,0:T(8,128)S(1)}, u32[]{:S(2)}, u32[]{:S(2)}) async-start(f32[32,16,128]{2,1,0:T(8,128)} %get-tuple-element.14), calls=%async_computation.2 | async-start | bytes 524288 | tf_op jit(solution)/shard_map/all_to_all | solution.py:377
  112.4 9.4 %all-to-all-done.2.scores_ref = f32[32,16,128]{2,1,0:T(8,128)S(1)} async-done(((f32[32,16,128]{2,1,0:T(8,128)}), f32[32,16,128]{2,1,0:T(8,128)S(1)}, u32[]{:S(2)}, u32[]{:S(2)}) %all-to-all-start.2) | async-done | bytes 262176 | tf_op jit(solution)/shard_map/all_to_all | solution.py:377
  121.7 1.1 home.1
  122.9 13.1 %all_to_all.25.refs_0_ = f32[32,16,128]{2,1,0:T(8,128)} all-to-all(f32[32,16,128]{2,1,0:T(8,128)S(1)} %get-tuple-element.17), channel_id=1, replica_groups=mesh['dir'=16,'z'=8,'xlo'=2] {'dir','xlo'}, dimensions={0} | all-to-all | bytes 524288 | tf_op jit(solution)/shard_map/all_to_all | solution.py:377
  136.0 8.3 %sums_halo.1 = f32[512,384]{1,0:T(8,128)} custom-call(f32[32,16,128]{2,1,0:T(8,128)} %all_to_all.25.refs_0_, f32[32,40,128]{2,1,0:T(8,128)} %copy-done.1, bf16[32,128,256]{2,1,0:T(8,128)(2,1)} %get-tuple-element.18.refs_2_, bf16[32,128,256]{2,1,0:T(8,128)(2,1)} %get-tuple-element.19.refs_3_, bf16[32,128,128]{2,1,0:T(8,128)(2,1)} %get-tuple-element.20.refs_4_), custom_call_target="tpu_custom_call" | custom-call | flops 4000000000 | bytes 6000000 | tf_op jit(solution)/shard_map/sums_halo/pallas_call | solution.py:307
  144.2 1.2 fusion.2
  145.4 3.2 %collective-permute-start.2 = (f32[256,384]{1,0:T(8,128)S(1)}, f32[256,384]{1,0:T(8,128)S(1)}, u32[]{:S(2)}, u32[]{:S(2)}) collective-permute-start(f32[256,384]{1,0:T(8,128)S(1)} %get-tuple-element.22), channel_id=1, source_target_pairs={{0,2},{2,4},{4,6},{6,8},{8,10},{10,12},{12,14},{14,0},{1,3},{3,5},... | collective-permute-start | bytes 1179656 | tf_op jit(solution)/shard_map/ppermute | solution.py:382
  148.6 10.0 %sums_own.1.own_ref = f32[512,384]{1,0:T(8,128)} custom-call(f32[32,16,128]{2,1,0:T(8,128)} %all_to_all.25.refs_0_, f32[32,40,128]{2,1,0:T(8,128)} %copy-done.1, bf16[32,128,256]{2,1,0:T(8,128)(2,1)} %get-tuple-element.18.refs_2_, bf16[32,128,256]{2,1,0:T(8,128)(2,1)} %get-tuple-element.19.refs_3_, bf16[32,128,128]{2,1,0:T(8,128)(2,1)} %get-tuple-element.20.refs_4_), custom_call_target="tpu_custom_call" | custom-call | flops 4000000000 | bytes 6000000 | tf_op jit(solution)/shard_map/sums_own/pallas_call | solution.py:307
  158.6 1.4 collective-permute-done.3.above_ref
  160.0 1.1 copy-done.2
  161.2 1.1 averages.1
  162.3 16.9 %all_to_all.26.got_ref = f32[32,40,128]{2,1,0:T(8,128)S(1)} all-to-all(f32[32,40,128]{2,1,0:T(8,128)S(1)} %averages.1), channel_id=1, replica_groups=mesh['dir'=16,'z'=8,'xlo'=2] {'dir','xlo'}, dimensions={0} | all-to-all | bytes 1310720 | tf_op jit(solution)/shard_map/all_to_all | solution.py:377
  (28 shorter events, 4.0 us)
Async XLA Ops:
  0.6 28.5 %copy-start = (f32[16,9216]{1,0:T(8,128)S(1)}, f32[16,9216]{1,0:T(8,128)}, u32[]{:S(2)}) copy-start(f32[16,9216]{1,0:T(8,128)} %param.11) | copy-start | bytes 1769476
  1.4 1.1 copy-start.3
  3.5 20.7 %all-to-all-start.1 = ((f32[32,40,128]{2,1,0:T(8,128)}), f32[32,40,128]{2,1,0:T(8,128)S(1)}, u32[]{:S(2)}, u32[]{:S(2)}) async-start(f32[32,40,128]{2,1,0:T(8,128)} %pack_templates.1), calls=%async_computation.1 | async-start | bytes 1310720 | tf_op jit(solution)/shard_map/all_to_all | solution.py:377
  24.3 18.8 %copy-start.1 = (f32[32,40,128]{2,1,0:T(8,128)}, f32[32,40,128]{2,1,0:T(8,128)S(1)}, u32[]{:S(2)}) copy-start(f32[32,40,128]{2,1,0:T(8,128)S(1)} %all-to-all-done.1.tpl_ref.refs_1_) | copy-start | bytes 1966084
  24.3 64.0 %all-to-all-start = ((f32[32,288,128]{2,1,0:T(8,128)}), f32[32,288,128]{2,1,0:T(8,128)}, u32[]{:S(2)}, u32[]{:S(2)}) async-start(f32[32,288,128]{2,1,0:T(8,128)} %pack_images.1), calls=%async_computation | async-start | bytes 9437184 | tf_op jit(solution)/shard_map/all_to_all | solution.py:377
  29.2 10.4 %collective-permute-start = (f32[16,40,128]{2,1,0:T(8,128)S(1)}, f32[16,40,128]{2,1,0:T(8,128)S(1)}, u32[]{:S(2)}, u32[]{:S(2)}) collective-permute-start(f32[16,40,128]{2,1,0:T(8,128)S(1)} %get-tuple-element.24), channel_id=1, source_target_pairs={{0,2},{2,4},{4,6},{6,8},{8,10},{10,12},{12,14},{14,0},{1,3},{3,5},... | collective-permute-start | bytes 983048 | tf_op jit(solution)/shard_map/ppermute | solution.py:382
  32.4 10.6 %collective-permute-start.1 = (f32[16,40,128]{2,1,0:T(8,128)S(1)}, f32[16,40,128]{2,1,0:T(8,128)S(1)}, u32[]{:S(2)}, u32[]{:S(2)}) collective-permute-start(f32[16,40,128]{2,1,0:T(8,128)S(1)} %get-tuple-element.23), channel_id=1, source_target_pairs={{0,14},{2,0},{4,2},{6,4},{8,6},{10,8},{12,10},{14,12},{1,15},{3,1}... | collective-permute-start | bytes 983048 | tf_op jit(solution)/shard_map/ppermute | solution.py:382
  45.4 1.2 copy-start.5
  46.6 0.6 copy-start.6
  88.3 33.5 %copy-start.4 = (s32[128]{0:T(128)S(1)}, s32[128]{0:T(128)}, u32[]{:S(2)}) copy-start(s32[128]{0:T(128)} %param.8) | copy-start | bytes 1540
  101.6 20.2 %all-to-all-start.2 = ((f32[32,16,128]{2,1,0:T(8,128)}), f32[32,16,128]{2,1,0:T(8,128)S(1)}, u32[]{:S(2)}, u32[]{:S(2)}) async-start(f32[32,16,128]{2,1,0:T(8,128)} %get-tuple-element.14), calls=%async_computation.2 | async-start | bytes 524288 | tf_op jit(solution)/shard_map/all_to_all | solution.py:377
  145.4 13.2 %collective-permute-start.2 = (f32[256,384]{1,0:T(8,128)S(1)}, f32[256,384]{1,0:T(8,128)S(1)}, u32[]{:S(2)}, u32[]{:S(2)}) collective-permute-start(f32[256,384]{1,0:T(8,128)S(1)} %get-tuple-element.22), channel_id=1, source_target_pairs={{0,2},{2,4},{4,6},{6,8},{8,10},{10,12},{12,14},{14,0},{1,3},{3,5},... | collective-permute-start | bytes 1179656 | tf_op jit(solution)/shard_map/ppermute | solution.py:382
  148.6 11.4 %collective-permute-start.3 = (f32[256,384]{1,0:T(8,128)S(1)}, f32[256,384]{1,0:T(8,128)S(1)}, u32[]{:S(2)}, u32[]{:S(2)}) collective-permute-start(f32[256,384]{1,0:T(8,128)S(1)} %get-tuple-element.21), channel_id=1, source_target_pairs={{0,14},{2,0},{4,2},{6,4},{8,6},{10,8},{12,10},{14,12},{1,15},{3,1}... | collective-permute-start | bytes 1179656 | tf_op jit(solution)/shard_map/ppermute | solution.py:382
  160.0 1.1 copy-start.2

commit v3 on v2

--- a/solution.py
+++ b/solution.py
@@ -72,30 +72,37 @@
     )(images, images)
 
 
-def pack_templates_kernel(tpl_ref, meta_ref, out_ref):
-    meta = meta_ref[...]
-    for t in range(8):
-        rem = [tpl_ref[b, :, pl.ds((64 + t) * LANES, LANES)] for b in range(4)]
-        for q in range(4):
-            dest = 4 * t + q
-            for j in range(2):
-                for b in range(4):
-                    out_ref[dest, pl.ds(16 * j + 4 * b, 4), :] = tpl_ref[b, :, pl.ds((2 * dest + j) * LANES, LANES)]
-            out_ref[dest, pl.ds(32, 4), :] = pick_groups([turned(rem[b], b - q) for b in range(4)])
-            out_ref[dest, pl.ds(META, 4), :] = meta
-
-
-def pack_templates(templates, meta):
-    vmem = pl.BlockSpec(memory_space=pltpu.VMEM)
+def pack_templates_kernel(tpl_ref, rem_ref, bin_ref, class_ref, out_ref):
+    bins = bin_ref[...].astype(F32)
+    classes = class_ref[...].astype(F32)
+    rem = [rem_ref[b] for b in range(4)]
+    for q in range(4):
+        for j in range(2):
+            for b in range(4):
+                out_ref[q, pl.ds(16 * j + 4 * b, 4), :] = tpl_ref[b, :, pl.ds((2 * q + j) * LANES, LANES)]
+        out_ref[q, pl.ds(32, 4), :] = pick_groups([turned(rem[b], b - q) for b in range(4)])
+        out_ref[q, pl.ds(META, 2), :] = jnp.broadcast_to(bins, (2, LANES))
+        out_ref[q, pl.ds(META + 2, 2), :] = jnp.broadcast_to(classes, (2, LANES))
+
+
+def pack_templates(templates, bins, classes):
+    steps = 8
+    one = pl.BlockSpec((1, LANES), lambda t: (0, 0))
     return pl.pallas_call(
         pack_templates_kernel,
-        in_specs=[vmem, vmem],
-        out_specs=vmem,
-        out_shape=jax.ShapeDtypeStruct((32, TPL, LANES), F32),
-        compiler_params=params(8),
+        grid=(steps,),
+        in_specs=[
+            pl.BlockSpec((4, 4, 1024), lambda t: (0, 0, t)),
+            pl.BlockSpec((4, 4, LANES), lambda t: (0, 0, 64 + t)),
+            one,
+            one,
+        ],
+        out_specs=pl.BlockSpec((4, TPL, LANES), lambda t: (t, 0, 0)),
+        out_shape=jax.ShapeDtypeStruct((4 * steps, TPL, LANES), F32),
+        compiler_params=params(60),
         cost_estimate=cost(0, 1_300_000),
         name="pack_templates",
-    )(templates, meta)
+    )(templates, templates, bins, classes)
 
 
 def operands_kernel(tpl_ref, below_ref, above_ref, ctf_ref, sq_ref, y_ref, ce_ref, tf_ref):
@@ -121,8 +128,7 @@
             tail = jnp.where(lane < 64, hi[:, 256:].astype(F32), lo[:, 256:].astype(F32))
             y_ref[out, pl.ds(0, 256)] = hi[:, :256]
             y_ref[out, pl.ds(256, 256)] = lo[:, :256]
-            y_ref[out, pl.ds(512, 256)] = hi[:, :256]
-            y_ref[out, pl.ds(768, 128)] = jnp.where(lane < 96, tail, last).astype(BF)
+            y_ref[out, pl.ds(512, 128)] = jnp.where(lane < 96, tail, last).astype(BF)
     ctf = ctf_ref[...]
     hi, mid = split(ctf)
     ce_ref[pl.ds(0, 16), :] = hi
@@ -136,7 +142,7 @@
         operands_kernel,
         in_specs=[vmem] * 5,
         out_specs=[vmem, vmem],
-        out_shape=[jax.ShapeDtypeStruct((1024, 896), BF), jax.ShapeDtypeStruct((48, 384), BF)],
+        out_shape=[jax.ShapeDtypeStruct((1024, 640), BF), jax.ShapeDtypeStruct((48, 384), BF)],
         scratch_shapes=[pltpu.VMEM((256, 384), F32)],
         compiler_params=params(12),
         cost_estimate=cost(600_000_000, 4_000_000),
@@ -176,9 +182,9 @@
             [jnp.concatenate([xh_ref[s], xh_ref[s], xl_ref[s], xr_ref[s]], axis=1) for s in pair], axis=0
         )
         mine = row_bin == bins_of(tpl_ref, [4 * step + s for s in pair])
-        all_rows = lax.dot_general(
-            y_ref[pl.ds(256 * side, 768), :], x, (((1,), (1,)), ((), ())), preferred_element_type=F32
-        )
+        y = y_ref[pl.ds(256 * side, 768), :]
+        y = jnp.concatenate([y[:, :512], y[:, :256], y[:, 512:]], axis=1)
+        all_rows = lax.dot_general(y, x, (((1,), (1,)), ((), ())), preferred_element_type=F32)
         blocks = []
         for k in range(3):
             kept = jnp.where(mine, all_rows[256 * k : 256 * k + 256], 0.0)
@@ -199,7 +205,7 @@
     return pl.pallas_call(
         scores_kernel,
         grid=(n // 4,),
-        in_specs=[block(4, IMG, LANES), whole((n, TPL, LANES)), whole((1024, 896)), whole((48, 384))],
+        in_specs=[block(4, IMG, LANES), whole((n, TPL, LANES)), whole((1024, 640)), whole((48, 384))],
         out_specs=[block(4, 128, 256), block(4, 128, 256), block(4, 128, 128), block(4, 16, 128)],
         out_shape=[
             jax.ShapeDtypeStruct((n, 128, 256), BF),
@@ -207,15 +213,15 @@
             jax.ShapeDtypeStruct((n, 128, 128), BF),
             jax.ShapeDtypeStruct((n, 16, 128), F32),
         ],
-        compiler_params=params(60),
+        compiler_params=params(24),
         cost_estimate=cost(6_000_000_000, 14_000_000),
         name="window_scores",
     )(buf, tpl, y, ctf)
 
 
-def home_kernel(place_ref, scores_ref, centre_ref, total_ref, shift_ref, p_ref):
-    xlo = place_ref[0]
-    first = place_ref[1]
+def home_kernel(scores_ref, centre_ref, total_ref, shift_ref, p_ref):
+    xlo = lax.axis_index("xlo")
+    first = lax.axis_index("z") * 8
     n = scores_ref.shape[0]
     scores = scores_ref[0]
     for s in range(1, n):
@@ -234,12 +240,12 @@
         p_ref[s] = p
 
 
-def home(place, scores, centre):
+def home(scores, centre):
     n = scores.shape[0]
     vmem = pl.BlockSpec(memory_space=pltpu.VMEM)
     return pl.pallas_call(
         home_kernel,
-        in_specs=[pl.BlockSpec(memory_space=pltpu.SMEM), vmem, vmem],
+        in_specs=[vmem, vmem],
         out_specs=[vmem, vmem, vmem],
         out_shape=[
             jax.ShapeDtypeStruct((1, 128), F32),
@@ -249,7 +255,7 @@
         compiler_params=params(4),
         cost_estimate=cost(200_000, 600_000),
         name="home",
-    )(place, scores, centre)
+    )(scores, centre)
 
 
 def spread(p8, bins, first_bin, rows):
@@ -310,7 +316,7 @@
         in_specs=[block(4, 16, 128), whole((n, TPL, LANES)), block(4, 128, 256), block(4, 128, 256), block(4, 128, 128)],
         out_specs=whole((512, 384)),
         out_shape=jax.ShapeDtypeStruct((512, 384), F32),
-        compiler_params=params(60),
+        compiler_params=params(24),
         cost_estimate=cost(4_000_000_000, 6_000_000),
         name="sums_" + which,
     )(p, tpl, xh, xl, xr)
@@ -386,8 +392,6 @@
     pixels = images.shape[1]
     xlo = lax.axis_index("xlo")
     chunk = lax.axis_index("dir") * 2 + xlo
-    first = lax.axis_index("z") * 8
-    meta = jnp.stack([prior_bin, prior_center, defocus_class, defocus_class]).astype(F32)
     ctf_main = lax.dynamic_slice(ctf_table, (0, 256 * chunk), (CLASSES, 256))
     ctf_rem = lax.dynamic_slice(ctf_table, (0, 8192 + 32 * chunk), (CLASSES, 32))
     eye = jnp.eye(CLASSES, dtype=F32)
@@ -397,7 +401,7 @@
     to_class = jnp.pad(jnp.concatenate([square.T, square.T], axis=1), ((0, 96), (96, 0)))
     to_pixel = jnp.pad(square, ((96, 16), (0, 96)))
 
-    tpl = exchange(pack_templates(templates, meta))
+    tpl = exchange(pack_templates(templates, prior_bin[None], defocus_class[None]))
     n = tpl.shape[0]
     buf = exchange(pack_images(images))
     sides = tpl.reshape(n // 2, 2, TPL, LANES)
@@ -405,8 +409,7 @@
     above = along_z(sides[:, 0], -1)
     y, ctf = operands(tpl, below, above, ctf_ext, to_class)
     xh, xl, xr, partial = window_scores(buf, tpl, y, ctf)
-    place = jnp.stack([xlo, first]).astype(jnp.int32)
-    log_total, mean_shift, p = home(place, exchange(partial), prior_center[None])
+    log_total, mean_shift, p = home(exchange(partial), prior_center[None])
     p = exchange(p)
     edge = sums("halo", p, tpl, xh, xl, xr)
     from_above = along_z(edge[:256], -1)

time: 182 us -> 174 us (0.956)
  blocking collectives: 30 us -> 49.2 us
  starting transfers between devices: 29.3 us -> 18.6 us
  Pallas kernels: 45.1 us -> 39.9 us
  local copies, waits for them, and re-layouts: 5.66 us -> 0.48 us
  waiting for transfers between devices: 68.5 us -> 64.1 us
    all_to_all x2 -> x3, blocking collectives: 30 us -> 49.2 us  [exchange(): return lax.all_to_all(value, PLANE, split_axis=0, concat_axis=0, tiled=True)]
    all_to_all x3 -> x2, starting transfers between devices: 22.9 us -> 12.2 us  [exchange(): return lax.all_to_all(value, PLANE, split_axis=0, concat_axis=0, tiled=True)]
    all_to_all x3 -> x2, waiting for transfers between devices: 56.8 us -> 49.3 us  [exchange(): return lax.all_to_all(value, PLANE, split_axis=0, concat_axis=0, tiled=True)]
    pallas_call x2, Pallas kernels: 18.2 us -> 10.9 us  [sums(): pl.pallas_call(body, grid=(n // 4,), in_specs=[block(4, 16, 128), whole((...]
    unnamed x15 -> x5, local copies, waits for them, and re-layouts: 4.16 us -> 0.11 us
    pallas_call x2, Pallas kernels: 2.19 us -> 5.75 us  [the longest x1 5.16 us: pack_templates(): pl.pallas_call(pack_templates_kernel, grid=(steps,), in_specs=[pl.BlockSp...]
    ppermute x4, waiting for transfers between devices: 11.7 us -> 14.9 us  [along_z(): return lax.ppermute(value, 'z', [(i, (i + by) % size) for i in range(size)])]
  transfers between devices with their start and end apart: 7 -> 6, of which waited for: 6 -> 6; matrix products, arithmetic and copies ran while one was open for 0% -> 0% of each run, Pallas kernels for 11% -> 9%
where the time goes in v3:
time: 174 us; the launch traced here: 173 us
  waiting for transfers between devices  64.1 us (37%)
  blocking collectives  49.2 us (28%)
  Pallas kernels  39.9 us (23%)
  starting transfers between devices  18.6 us (11%)
    all_to_all x2, waiting for transfers between devices, exchange(): return lax.all_to_all(value, PLANE, split_axis=0, concat_axis=0, tiled=True)  49.3 us
    all_to_all x3, blocking collectives, exchange(): return lax.all_to_all(value, PLANE, split_axis=0, concat_axis=0, tiled=True)  49.2 us
    ppermute x4, waiting for transfers between devices, along_z(): return lax.ppermute(value, 'z', [(i, (i + by) % size) for i in range(size)])  14.9 us
    all_to_all x2, starting transfers between devices, exchange(): return lax.all_to_all(value, PLANE, split_axis=0, concat_axis=0, tiled=True)  12.2 us
    pallas_call x1, Pallas kernels, window_scores(): pl.pallas_call(scores_kernel, grid=(n // 4,), in_specs=[block(4, IMG, LAN...  11.8 us
    pallas_call x2, Pallas kernels, sums(): pl.pallas_call(body, grid=(n // 4,), in_specs=[block(4, 16, 128), whole((...  10.9 us
    pallas_call x1, Pallas kernels, pack_images(): pl.pallas_call(pack_images_kernel, grid=(steps,), in_specs=[pl.BlockSpec(...  7.02 us
    ppermute x4, starting transfers between devices, along_z(): return lax.ppermute(value, 'z', [(i, (i + by) % size) for i in range(size)])  6.42 us
  transfers between devices with their start and end apart: 6, of which 6 were waited for; matrix products, arithmetic and copies ran while one was open for 0% of the time, Pallas kernels for 9%

profile of v3, /device:TPU:96, one launch (start us, length us, event | category | flops | bytes accessed | tf_op | source)
XLA Modules:
  0.0 173.1 jit_solution(15421586671396068493)
XLA Ops:
  0.6 5.2 %pack_templates.1 = f32[32,40,128]{2,1,0:T(8,128)} custom-call(f32[4,4,9216]{2,1,0:T(4,128)} %rem_ref.3, f32[4,4,9216]{2,1,0:T(4,128)} %rem_ref.3, s32[1,128]{1,0:T(1,128)} %bitcast.18, s32[1,128]{1,0:T(1,128)} %bitcast.19), custom_call_target="tpu_custom_call" | custom-call | bytes 1300000 | tf_op jit(solution)/shard_map/pack_templates/pallas_call | solution.py:91
  5.8 7.3 %all-to-all-start.1 = ((f32[32,40,128]{2,1,0:T(8,128)}), f32[32,40,128]{2,1,0:T(8,128)S(1)}, u32[]{:S(2)}, u32[]{:S(2)}) async-start(f32[32,40,128]{2,1,0:T(8,128)} %pack_templates.1), calls=%async_computation.1 | async-start | bytes 1310720 | tf_op jit(solution)/shard_map/all_to_all | solution.py:383
  13.1 7.0 %pack_images.1 = f32[32,288,128]{2,1,0:T(8,128)} custom-call(f32[128,9216]{1,0:T(8,128)} %rem_ref.2, f32[128,9216]{1,0:T(8,128)} %rem_ref.2), custom_call_target="tpu_custom_call" | custom-call | bytes 9500000 | tf_op jit(solution)/shard_map/pack_images/pallas_call | solution.py:60
  20.2 6.4 %all-to-all-done.1.tpl_ref.refs_1_ = f32[32,40,128]{2,1,0:T(8,128)S(1)} async-done(((f32[32,40,128]{2,1,0:T(8,128)}), f32[32,40,128]{2,1,0:T(8,128)S(1)}, u32[]{:S(2)}, u32[]{:S(2)}) %all-to-all-start.1) | async-done | bytes 655392 | tf_op jit(solution)/shard_map/all_to_all | solution.py:383
  26.5 4.9 %all-to-all-start = ((f32[32,288,128]{2,1,0:T(8,128)}), f32[32,288,128]{2,1,0:T(8,128)}, u32[]{:S(2)}, u32[]{:S(2)}) async-start(f32[32,288,128]{2,1,0:T(8,128)} %pack_images.1), calls=%async_computation | async-start | bytes 9437184 | tf_op jit(solution)/shard_map/all_to_all | solution.py:383
  31.5 3.2 %collective-permute-start = (f32[16,40,128]{2,1,0:T(8,128)S(1)}, f32[16,40,128]{2,1,0:T(8,128)S(1)}, u32[]{:S(2)}, u32[]{:S(2)}) collective-permute-start(f32[16,40,128]{2,1,0:T(8,128)S(1)} %get-tuple-element.24), channel_id=1, source_target_pairs={{0,2},{2,4},{4,6},{6,8},{8,10},{10,12},{12,14},{14,0},{1,3},{3,5},... | collective-permute-start | bytes 983048 | tf_op jit(solution)/shard_map/ppermute | solution.py:388
  34.8 0.1 copy.14
  35.0 0.1 pad.8.clone.sq_ref
  35.1 6.9 %collective-permute-done.below_ref = f32[16,40,128]{2,1,0:T(8,128)S(1)} collective-permute-done((f32[16,40,128]{2,1,0:T(8,128)S(1)}, f32[16,40,128]{2,1,0:T(8,128)S(1)}, u32[]{:S(2)}, u32[]{:S(2)}) %collective-permute-start) | collective-permute-done | bytes 327712 | tf_op jit(solution)/shard_map/ppermute | solution.py:388
  42.0 3.4 %collective-permute-done.1.above_ref = f32[16,40,128]{2,1,0:T(8,128)S(1)} collective-permute-done((f32[16,40,128]{2,1,0:T(8,128)S(1)}, f32[16,40,128]{2,1,0:T(8,128)S(1)}, u32[]{:S(2)}, u32[]{:S(2)}) %collective-permute-start.1) | collective-permute-done | bytes 327712 | tf_op jit(solution)/shard_map/ppermute | solution.py:388
  45.4 2.2 %operands.1 = (bf16[1024,640]{1,0:T(8,128)(2,1)S(1)}, bf16[48,384]{1,0:T(8,128)(2,1)S(1)}) custom-call(f32[32,40,128]{2,1,0:T(8,128)S(1)} %all-to-all-done.1.tpl_ref.refs_1_, f32[16,40,128]{2,1,0:T(8,128)S(1)} %collective-permute-done.below_ref, f32[16,40,128]{2,1,0:T(8,128)S(1)} %collective-permute-done.1.above_ref, f32[16,384]{1,0:T(8,128)S(1)} %concatenate.9.ctf_ref, ...), custom_call_target="tpu_custom_call" | custom-call | flops 600000000 | bytes 4000000 | tf_op jit(solution)/shard_map/operands/pallas_call | solution.py:141
  47.7 42.9 %all-to-all-done.buf_ref = f32[32,288,128]{2,1,0:T(8,128)} async-done(((f32[32,288,128]{2,1,0:T(8,128)}), f32[32,288,128]{2,1,0:T(8,128)}, u32[]{:S(2)}, u32[]{:S(2)}) %all-to-all-start) | async-done | bytes 4718624 | tf_op jit(solution)/shard_map/all_to_all | solution.py:383
  90.5 11.8 %window_scores.1 = (bf16[32,128,256]{2,1,0:T(8,128)(2,1)S(1)}, bf16[32,128,256]{2,1,0:T(8,128)(2,1)S(1)}, bf16[32,128,128]{2,1,0:T(8,128)(2,1)S(1)}, f32[32,16,128]{2,1,0:T(8,128)S(1)}) custom-call(f32[32,288,128]{2,1,0:T(8,128)} %all-to-all-done.buf_ref, f32[32,40,128]{2,1,0:T(8,128)S(1)} %all-to-all-done.1.tpl_ref.refs_1_, ...), custom_call_target="tpu_custom_call" | custom-call | flops 6000000000 | bytes 14000000 | tf_op jit(solution)/shard_map/window_scores/pallas_call | solution.py:205
  102.4 20.0 %all_to_all.25.scores_ref = f32[32,16,128]{2,1,0:T(8,128)S(1)} all-to-all(f32[32,16,128]{2,1,0:T(8,128)S(1)} %get-tuple-element.14), channel_id=1, replica_groups=mesh['dir'=16,'z'=8,'xlo'=2] {'dir','xlo'}, dimensions={0} | all-to-all | bytes 524288 | tf_op jit(solution)/shard_map/all_to_all | solution.py:383
  122.4 0.6 home.1
  123.0 12.4 %all_to_all.26.refs_0_ = f32[32,16,128]{2,1,0:T(8,128)S(1)} all-to-all(f32[32,16,128]{2,1,0:T(8,128)S(1)} %get-tuple-element.17), channel_id=1, replica_groups=mesh['dir'=16,'z'=8,'xlo'=2] {'dir','xlo'}, dimensions={0} | all-to-all | bytes 524288 | tf_op jit(solution)/shard_map/all_to_all | solution.py:383
  135.4 4.1 %sums_halo.1 = f32[512,384]{1,0:T(8,128)S(1)} custom-call(f32[32,16,128]{2,1,0:T(8,128)S(1)} %all_to_all.26.refs_0_, f32[32,40,128]{2,1,0:T(8,128)S(1)} %all-to-all-done.1.tpl_ref.refs_1_, bf16[32,128,256]{2,1,0:T(8,128)(2,1)S(1)} %get-tuple-element.18.refs_2_, bf16[32,128,256]{2,1,0:T(8,128)(2,1)S(1)} %get-tuple-element.19.refs_3_, ...), custom_call_target="tpu_custom_call" | custom-call | flops 4000000000 | bytes 6000000 | tf_op jit(solution)/shard_map/sums_halo/pallas_call | solution.py:313
  139.5 3.2 %collective-permute-start.2 = (f32[256,384]{1,0:T(8,128)S(1)}, f32[256,384]{1,0:T(8,128)S(1)}, u32[]{:S(2)}, u32[]{:S(2)}) collective-permute-start(f32[256,384]{1,0:T(8,128)S(1)} %get-tuple-element.22), channel_id=1, source_target_pairs={{0,2},{2,4},{4,6},{6,8},{8,10},{10,12},{12,14},{14,0},{1,3},{3,5},... | collective-permute-start | bytes 1179656 | tf_op jit(solution)/shard_map/ppermute | solution.py:388
  142.8 6.8 %sums_own.1.own_ref = f32[512,384]{1,0:T(8,128)S(1)} custom-call(f32[32,16,128]{2,1,0:T(8,128)S(1)} %all_to_all.26.refs_0_, f32[32,40,128]{2,1,0:T(8,128)S(1)} %all-to-all-done.1.tpl_ref.refs_1_, bf16[32,128,256]{2,1,0:T(8,128)(2,1)S(1)} %get-tuple-element.18.refs_2_, bf16[32,128,256]{2,1,0:T(8,128)(2,1)S(1)} %get-tuple-element.19.refs_3_, ...), custom_call_target="tpu_custom_call" | custom-call | flops 4000000000 | bytes 6000000 | tf_op jit(solution)/shard_map/sums_own/pallas_call | solution.py:313
  149.6 1.1 collective-permute-done.2.below_ref
  150.8 3.4 %collective-permute-done.3.above_ref = f32[256,384]{1,0:T(8,128)S(1)} collective-permute-done((f32[256,384]{1,0:T(8,128)S(1)}, f32[256,384]{1,0:T(8,128)S(1)}, u32[]{:S(2)}, u32[]{:S(2)}) %collective-permute-start.3) | collective-permute-done | bytes 393248 | tf_op jit(solution)/shard_map/ppermute | solution.py:388
  154.2 1.1 averages.1
  155.3 16.8 %all_to_all.27.got_ref = f32[32,40,128]{2,1,0:T(8,128)S(1)} all-to-all(f32[32,40,128]{2,1,0:T(8,128)S(1)} %averages.1), channel_id=1, replica_groups=mesh['dir'=16,'z'=8,'xlo'=2] {'dir','xlo'}, dimensions={0} | all-to-all | bytes 1310720 | tf_op jit(solution)/shard_map/all_to_all | solution.py:383
  172.1 1.0 unpack.1
  (15 shorter events, 0.3 us)
Async XLA Ops:
  0.6 30.8 %copy-start = (f32[16,9216]{1,0:T(8,128)S(1)}, f32[16,9216]{1,0:T(8,128)}, u32[]{:S(2)}) copy-start(f32[16,9216]{1,0:T(8,128)} %param.11) | copy-start | bytes 1769476
  5.8 20.7 %all-to-all-start.1 = ((f32[32,40,128]{2,1,0:T(8,128)}), f32[32,40,128]{2,1,0:T(8,128)S(1)}, u32[]{:S(2)}, u32[]{:S(2)}) async-start(f32[32,40,128]{2,1,0:T(8,128)} %pack_templates.1), calls=%async_computation.1 | async-start | bytes 1310720 | tf_op jit(solution)/shard_map/all_to_all | solution.py:383
  26.5 64.0 %all-to-all-start = ((f32[32,288,128]{2,1,0:T(8,128)}), f32[32,288,128]{2,1,0:T(8,128)}, u32[]{:S(2)}, u32[]{:S(2)}) async-start(f32[32,288,128]{2,1,0:T(8,128)} %pack_images.1), calls=%async_computation | async-start | bytes 9437184 | tf_op jit(solution)/shard_map/all_to_all | solution.py:383
  31.5 10.4 %collective-permute-start = (f32[16,40,128]{2,1,0:T(8,128)S(1)}, f32[16,40,128]{2,1,0:T(8,128)S(1)}, u32[]{:S(2)}, u32[]{:S(2)}) collective-permute-start(f32[16,40,128]{2,1,0:T(8,128)S(1)} %get-tuple-element.24), channel_id=1, source_target_pairs={{0,2},{2,4},{4,6},{6,8},{8,10},{10,12},{12,14},{14,0},{1,3},{3,5},... | collective-permute-start | bytes 983048 | tf_op jit(solution)/shard_map/ppermute | solution.py:388
  34.8 10.6 %collective-permute-start.1 = (f32[16,40,128]{2,1,0:T(8,128)S(1)}, f32[16,40,128]{2,1,0:T(8,128)S(1)}, u32[]{:S(2)}, u32[]{:S(2)}) collective-permute-start(f32[16,40,128]{2,1,0:T(8,128)S(1)} %get-tuple-element.23), channel_id=1, source_target_pairs={{0,14},{2,0},{4,2},{6,4},{8,6},{10,8},{12,10},{14,12},{1,15},{3,1}... | collective-permute-start | bytes 983048 | tf_op jit(solution)/shard_map/ppermute | solution.py:388
  90.5 31.8 %copy-start.1 = (s32[128]{0:T(128)S(1)}, s32[128]{0:T(128)}, u32[]{:S(2)}) copy-start(s32[128]{0:T(128)} %param.8) | copy-start | bytes 1540
  139.5 11.2 %collective-permute-start.2 = (f32[256,384]{1,0:T(8,128)S(1)}, f32[256,384]{1,0:T(8,128)S(1)}, u32[]{:S(2)}, u32[]{:S(2)}) collective-permute-start(f32[256,384]{1,0:T(8,128)S(1)} %get-tuple-element.22), channel_id=1, source_target_pairs={{0,2},{2,4},{4,6},{6,8},{8,10},{10,12},{12,14},{14,0},{1,3},{3,5},... | collective-permute-start | bytes 1179656 | tf_op jit(solution)/shard_map/ppermute | solution.py:388
  142.7 11.4 %collective-permute-start.3 = (f32[256,384]{1,0:T(8,128)S(1)}, f32[256,384]{1,0:T(8,128)S(1)}, u32[]{:S(2)}, u32[]{:S(2)}) collective-permute-start(f32[256,384]{1,0:T(8,128)S(1)} %get-tuple-element.21), channel_id=1, source_target_pairs={{0,14},{2,0},{4,2},{6,4},{8,6},{10,8},{12,10},{14,12},{1,15},{3,1}... | collective-permute-start | bytes 1179656 | tf_op jit(solution)/shard_map/ppermute | solution.py:388

commit v4 on v3

--- a/solution.py
+++ b/solution.py
@@ -72,37 +72,33 @@
     )(images, images)
 
 
-def pack_templates_kernel(tpl_ref, rem_ref, bin_ref, class_ref, out_ref):
-    bins = bin_ref[...].astype(F32)
-    classes = class_ref[...].astype(F32)
-    rem = [rem_ref[b] for b in range(4)]
-    for q in range(4):
-        for j in range(2):
-            for b in range(4):
-                out_ref[q, pl.ds(16 * j + 4 * b, 4), :] = tpl_ref[b, :, pl.ds((2 * q + j) * LANES, LANES)]
-        out_ref[q, pl.ds(32, 4), :] = pick_groups([turned(rem[b], b - q) for b in range(4)])
-        out_ref[q, pl.ds(META, 2), :] = jnp.broadcast_to(bins, (2, LANES))
-        out_ref[q, pl.ds(META + 2, 2), :] = jnp.broadcast_to(classes, (2, LANES))
+def pack_templates_kernel(tpl_ref, bin_ref, class_ref, out_ref):
+    bins = jnp.broadcast_to(bin_ref[...].astype(F32), (2, LANES))
+    classes = jnp.broadcast_to(class_ref[...].astype(F32), (2, LANES))
+    for t in range(8):
+        rem = [tpl_ref[b, :, pl.ds((64 + t) * LANES, LANES)] for b in range(4)]
+        for q in range(4):
+            dest = 4 * t + q
+            for j in range(2):
+                for b in range(4):
+                    out_ref[dest, pl.ds(16 * j + 4 * b, 4), :] = tpl_ref[b, :, pl.ds((2 * dest + j) * LANES, LANES)]
+            out_ref[dest, pl.ds(32, 4), :] = pick_groups([turned(rem[b], b - q) for b in range(4)])
+            out_ref[dest, pl.ds(META, 2), :] = bins
+            out_ref[dest, pl.ds(META + 2, 2), :] = classes
 
 
 def pack_templates(templates, bins, classes):
-    steps = 8
-    one = pl.BlockSpec((1, LANES), lambda t: (0, 0))
+    whole = lambda shape: pl.BlockSpec(shape, lambda i: (0,) * len(shape))
     return pl.pallas_call(
         pack_templates_kernel,
-        grid=(steps,),
-        in_specs=[
-            pl.BlockSpec((4, 4, 1024), lambda t: (0, 0, t)),
-            pl.BlockSpec((4, 4, LANES), lambda t: (0, 0, 64 + t)),
-            one,
-            one,
-        ],
-        out_specs=pl.BlockSpec((4, TPL, LANES), lambda t: (t, 0, 0)),
-        out_shape=jax.ShapeDtypeStruct((4 * steps, TPL, LANES), F32),
+        grid=(1,),
+        in_specs=[whole(templates.shape), whole((1, LANES)), whole((1, LANES))],
+        out_specs=whole((32, TPL, LANES)),
+        out_shape=jax.ShapeDtypeStruct((32, TPL, LANES), F32),
         compiler_params=params(60),
         cost_estimate=cost(0, 1_300_000),
         name="pack_templates",
-    )(templates, templates, bins, classes)
+    )(templates, bins, classes)
 
 
 def operands_kernel(tpl_ref, below_ref, above_ref, ctf_ref, sq_ref, y_ref, ce_ref, tf_ref):
@@ -155,27 +151,26 @@
     return jnp.concatenate(rows, axis=1).astype(jnp.int32)
 
 
-def scores_kernel(buf_ref, tpl_ref, y_ref, ce_ref, xh_ref, xl_ref, xr_ref, out_ref):
+def scores_kernel(buf0, buf1, buf2, buf3, tpl_ref, y_ref, ce_ref, xh_ref, xl_ref, xr_ref, out_ref):
     step = pl.program_id(0)
     group = lane_group((128, LANES))
-    for s in range(4):
+    for s, buf_ref in enumerate((buf0, buf1, buf2, buf3)):
         source = 4 * step + s
         classes = tpl_ref[source, pl.ds(META + 2, 1), :].astype(jnp.int32)
         row_class = lax.broadcasted_iota(jnp.int32, (48, 128), 0) % CLASSES
         onehot = jnp.where(row_class == classes, 1.0, 0.0).astype(BF)
         ctf = lax.dot_general(onehot, ce_ref[...], (((0,), (0,)), ((), ())), preferred_element_type=F32)
         for j in range(2):
-            hi, lo = split(ctf[:, 128 * j : 128 * j + 128] * buf_ref[s, pl.ds(128 * j, 128), :])
+            hi, lo = split(ctf[:, 128 * j : 128 * j + 128] * buf_ref[0, pl.ds(128 * j, 128), :])
             xh_ref[s, :, pl.ds(128 * j, 128)] = hi
             xl_ref[s, :, pl.ds(128 * j, 128)] = lo
-        packed = buf_ref[s, pl.ds(256, 32), :]
+        packed = buf_ref[0, pl.ds(256, 32), :]
         v = [turned(packed, j) for j in range(4)]
         one = jnp.ones_like(packed)
         rem = jnp.concatenate([pick_groups([v[(q - g) % 4] for q in (0, 1, 2)] + [one]) for g in range(4)], axis=0)
         hi, lo = split(ctf[:, 256:] * rem)
         xr_ref[s, :, :] = jnp.where(group == 1, lo.astype(F32), hi.astype(F32)).astype(BF)
     row_bin = lax.broadcasted_iota(jnp.int32, (256, 256), 0) // 4
-    half = lax.broadcasted_iota(jnp.int32, (8, 256), 0) < 4
     for side in range(2):
         pair = (side, 2 + side)
         x = jnp.concatenate(
@@ -185,63 +180,61 @@
         y = y_ref[pl.ds(256 * side, 768), :]
         y = jnp.concatenate([y[:, :512], y[:, :256], y[:, 512:]], axis=1)
         all_rows = lax.dot_general(y, x, (((1,), (1,)), ((), ())), preferred_element_type=F32)
-        blocks = []
         for k in range(3):
             kept = jnp.where(mine, all_rows[256 * k : 256 * k + 256], 0.0)
             total = jnp.sum(kept.reshape(32, 8, 256), axis=0)
-            blocks.append(total + pltpu.roll(total, 4, 0))
-        edge, low, high = blocks if side == 0 else (blocks[2], blocks[0], blocks[1])
-        own = jnp.where(half, low, high)
-        for k, s in enumerate(pair):
-            cols = slice(128 * k, 128 * k + 128)
-            out_ref[s, pl.ds(0, 8), :] = own[:, cols]
-            out_ref[s, pl.ds(8, 8), :] = edge[:, cols]
+            total = total + pltpu.roll(total, 4, 0)
+            for half, s in enumerate(pair):
+                out_ref[3 * s + k] = total[:4, 128 * half : 128 * half + 128]
 
 
 def window_scores(buf, tpl, y, ctf):
     n = buf.shape[0]
     whole = lambda shape: pl.BlockSpec(shape, lambda p: (0,) * len(shape))
     block = lambda *shape: pl.BlockSpec(shape, lambda p: (p,) + (0,) * (len(shape) - 1))
+    image = lambda k: pl.BlockSpec((1, IMG, LANES), lambda p: (4 * p + k, 0, 0))
     return pl.pallas_call(
         scores_kernel,
         grid=(n // 4,),
-        in_specs=[block(4, IMG, LANES), whole((n, TPL, LANES)), whole((1024, 640)), whole((48, 384))],
-        out_specs=[block(4, 128, 256), block(4, 128, 256), block(4, 128, 128), block(4, 16, 128)],
+        in_specs=[image(k) for k in range(4)] + [whole((n, TPL, LANES)), whole((1024, 640)), whole((48, 384))],
+        out_specs=[block(4, 128, 256), block(4, 128, 256), block(4, 128, 128), block(12, 4, 128)],
         out_shape=[
             jax.ShapeDtypeStruct((n, 128, 256), BF),
             jax.ShapeDtypeStruct((n, 128, 256), BF),
             jax.ShapeDtypeStruct((n, 128, 128), BF),
-            jax.ShapeDtypeStruct((n, 16, 128), F32),
+            jax.ShapeDtypeStruct((3 * n, 4, 128), F32),
         ],
         compiler_params=params(24),
         cost_estimate=cost(6_000_000_000, 14_000_000),
         name="window_scores",
-    )(buf, tpl, y, ctf)
+    )(buf, buf, buf, buf, tpl, y, ctf)
 
 
 def home_kernel(scores_ref, centre_ref, total_ref, shift_ref, p_ref):
-    xlo = lax.axis_index("xlo")
-    first = lax.axis_index("z") * 8
-    n = scores_ref.shape[0]
-    scores = scores_ref[0]
-    for s in range(1, n):
-        scores = scores + scores_ref[s]
-    row = lax.broadcasted_iota(jnp.int32, scores.shape, 0)
-    angle = jnp.where(row < 8, row + 4, row - 8 + 12 * xlo)
-    offset = angle - (centre_ref[...] - first + 4)
-    inside = jnp.logical_and(jnp.abs(offset) <= HALF, row < 12)
-    safe = jnp.where(inside, scores, 0.0)
-    total = jnp.log(jnp.sum(jnp.where(inside, jnp.exp(safe), 0.0), axis=0, keepdims=True))
-    p = jnp.where(inside, jnp.exp(safe - total), 0.0)
+    n = scores_ref.shape[0] // 3
+    start = 4 * lax.axis_index("xlo") + 8 * lax.axis_index("z") - 4 - centre_ref[...]
+    row = lax.broadcasted_iota(jnp.int32, (4, 128), 0)
+    offsets, inside, safe = [], [], []
+    for k in range(3):
+        scores = scores_ref[k]
+        for s in range(1, n):
+            scores = scores + scores_ref[3 * s + k]
+        offset = row + 4 * k + start
+        keep = jnp.abs(offset) <= HALF
+        offsets.append(offset.astype(F32))
+        inside.append(keep)
+        safe.append(jnp.where(keep, scores, 0.0))
+    mass = sum(jnp.where(keep, jnp.exp(v), 0.0) for keep, v in zip(inside, safe))
+    total = jnp.log(jnp.sum(mass, axis=0, keepdims=True))
+    p = [jnp.where(keep, jnp.exp(v - total), 0.0) for keep, v in zip(inside, safe)]
     total_ref[...] = total
-    shift_ref[...] = jnp.sum(p * offset.astype(F32), axis=0, keepdims=True)
-    p = jnp.where(row < 12, p, pltpu.roll(p, 4, 0))
-    for s in range(n):
-        p_ref[s] = p
+    shift_ref[...] = jnp.sum(sum(a * b for a, b in zip(p, offsets)), axis=0, keepdims=True)
+    for k in range(3):
+        for s in range(n):
+            p_ref[3 * s + k] = p[k]
 
 
 def home(scores, centre):
-    n = scores.shape[0]
     vmem = pl.BlockSpec(memory_space=pltpu.VMEM)
     return pl.pallas_call(
         home_kernel,
@@ -250,7 +243,7 @@
         out_shape=[
             jax.ShapeDtypeStruct((1, 128), F32),
             jax.ShapeDtypeStruct((1, 128), F32),
-            jax.ShapeDtypeStruct((n, 16, 128), F32),
+            jax.ShapeDtypeStruct(scores.shape, F32),
         ],
         compiler_params=params(4),
         cost_estimate=cost(200_000, 600_000),
@@ -275,9 +268,11 @@
     def _():
         out_ref[...] = jnp.zeros_like(out_ref)
 
-    def add(rows, high, low, sources):
+    def add(rows, parts, sources):
         stack = lambda ref: jnp.concatenate([ref[s] for s in sources], axis=0)
         xh, xl, xr = stack(xh_ref), stack(xl_ref), stack(xr_ref)
+        high = jnp.concatenate([part[0] for part in parts], axis=0)
+        low = jnp.concatenate([part[1] for part in parts], axis=0)
         left = jnp.concatenate([high, low, high], axis=1)
         main = jnp.dot(left, jnp.concatenate([xh, xh, xl], axis=0), preferred_element_type=F32)
         wide = left.shape[1] // 3 * 2
@@ -285,21 +280,21 @@
         out_ref[rows, pl.ds(0, 256)] += main
         out_ref[rows, pl.ds(256, 128)] += tail
 
+    def twice(sources, blocks):
+        p4 = jnp.concatenate([p_ref[3 * s + k] for s, k in zip(sources, blocks)], axis=1)
+        return jnp.concatenate([p4, p4], axis=0)
+
     if which == "halo":
         for side in range(2):
             pair = (side, 2 + side)
-            p8 = jnp.concatenate([p_ref[s, pl.ds(8, 8), :] for s in pair], axis=1)
-            high, low = spread(p8, bins_of(tpl_ref, [4 * step + s for s in pair]), 0, 256)
-            add(pl.ds(256 * side, 256), high, low, pair)
+            bins = bins_of(tpl_ref, [4 * step + s for s in pair])
+            p8 = twice(pair, (2 * side, 2 * side))
+            add(pl.ds(256 * side, 256), [spread(p8, bins, 0, 256)], pair)
     else:
         four = range(4)
-        half = lax.broadcasted_iota(jnp.int32, (8, 512), 0) < 4
         bins = bins_of(tpl_ref, [4 * step + s for s in four])
-        own = jnp.concatenate([p_ref[s, pl.ds(0, 8), :] for s in four], axis=1)
-        other = pltpu.roll(own, 4, 0)
-        for k, p8 in enumerate((jnp.where(half, own, other), jnp.where(half, other, own))):
-            high, low = spread(p8, bins, 0, 256)
-            add(pl.ds(256 * k, 256), high, low, four)
+        parts = [spread(twice(four, [k + 1 - s % 2 for s in four]), bins, 0, 256) for k in range(2)]
+        add(pl.ds(0, 512), parts, four)
 
 
 def sums(which, p, tpl, xh, xl, xr):
@@ -313,7 +308,7 @@
     return pl.pallas_call(
         body,
         grid=(n // 4,),
-        in_specs=[block(4, 16, 128), whole((n, TPL, LANES)), block(4, 128, 256), block(4, 128, 256), block(4, 128, 128)],
+        in_specs=[block(12, 4, 128), whole((n, TPL, LANES)), block(4, 128, 256), block(4, 128, 256), block(4, 128, 128)],
         out_specs=whole((512, 384)),
         out_shape=jax.ShapeDtypeStruct((512, 384), F32),
         compiler_params=params(24),
@@ -333,12 +328,13 @@
             mean = jnp.concatenate([total[:, :256], tail], axis=1) / (weight + 1.0)
             for d in range(4):
                 dest = 2 * (4 * c + d) + side
-                piece = mean[16 * d : 16 * d + 16]
-                out_ref[dest, pl.ds(0, 16), :] = piece[:, :128]
-                out_ref[dest, pl.ds(16, 16), :] = piece[:, 128:256]
-                rem = [piece[4 * b : 4 * b + 4, 256:] for b in range(4)]
-                out_ref[dest, pl.ds(32, 4), :] = pick_groups([turned(rem[b], b) for b in range(4)])
-                out_ref[dest, pl.ds(36, 4), :] = jnp.zeros((4, LANES), F32)
+                rem = []
+                for b in range(4):
+                    piece = mean[16 * d + 4 * b : 16 * d + 4 * b + 4]
+                    out_ref[9 * dest + b] = piece[:, :128]
+                    out_ref[9 * dest + 4 + b] = piece[:, 128:256]
+                    rem.append(turned(piece[:, 256:], b))
+                out_ref[9 * dest + 8] = pick_groups(rem)
 
 
 def averages(own, below, above, squares, n):
@@ -347,7 +343,7 @@
         average_kernel,
         in_specs=[vmem] * 4,
         out_specs=vmem,
-        out_shape=jax.ShapeDtypeStruct((n, 40, LANES), F32),
+        out_shape=jax.ShapeDtypeStruct((9 * n, 4, LANES), F32),
         compiler_params=params(8),
         cost_estimate=cost(200_000_000, 3_000_000),
         name="averages",
@@ -355,13 +351,13 @@
 
 
 def unpack_kernel(got_ref, out_ref):
-    n = got_ref.shape[0]
+    n = got_ref.shape[0] // 9
     for i in range(n):
         for j in range(2):
             for b in range(4):
-                out_ref[b, :, pl.ds(256 * i + 128 * j, 128)] = got_ref[i, pl.ds(16 * j + 4 * b, 4), :]
+                out_ref[b, :, pl.ds(256 * i + 128 * j, 128)] = got_ref[9 * i + 4 * j + b]
     for t in range(n // 4):
-        rem = [got_ref[4 * t + q, pl.ds(32, 4), :] for q in range(4)]
+        rem = [got_ref[9 * (4 * t + q) + 8] for q in range(4)]
         for b in range(4):
             out_ref[b, :, pl.ds(256 * n + 128 * t, 128)] = pick_groups([turned(rem[q], q - b) for q in range(4)])
 

time: 174 us -> 169 us (0.971)
  Pallas kernels: 39.9 us -> 37.4 us
  blocking collectives: 49.2 us -> 47.2 us
    pallas_call x4, Pallas kernels: 27.9 us -> 25.4 us  [the longest x1 12.1 us: window_scores(): pl.pallas_call(scores_kernel, grid=(n // 4,), in_specs=[image(k) for k in...]
    all_to_all x3, blocking collectives: 49.2 us -> 47.2 us  [exchange(): return lax.all_to_all(value, PLANE, split_axis=0, concat_axis=0, tiled=True)]
  transfers between devices with their start and end apart: 6 -> 6, of which waited for: 6 -> 6; matrix products, arithmetic and copies ran while one was open for 0% -> 0% of each run, Pallas kernels for 9% -> 10%
where the time goes in v4:
time: 169 us; the launch traced here: 168 us
  waiting for transfers between devices  64 us (38%)
  blocking collectives  47.2 us (28%)
  Pallas kernels  37.4 us (22%)
  starting transfers between devices  18.6 us (11%)
    all_to_all x2, waiting for transfers between devices, exchange(): return lax.all_to_all(value, PLANE, split_axis=0, concat_axis=0, tiled=True)  49.3 us
    all_to_all x3, blocking collectives, exchange(): return lax.all_to_all(value, PLANE, split_axis=0, concat_axis=0, tiled=True)  47.2 us
    ppermute x4, waiting for transfers between devices, along_z(): return lax.ppermute(value, 'z', [(i, (i + by) % size) for i in range(size)])  14.8 us
    all_to_all x2, starting transfers between devices, exchange(): return lax.all_to_all(value, PLANE, split_axis=0, concat_axis=0, tiled=True)  12.2 us
    pallas_call x1, Pallas kernels, window_scores(): pl.pallas_call(scores_kernel, grid=(n // 4,), in_specs=[image(k) for k in...  12.1 us
    pallas_call x2, Pallas kernels, sums(): pl.pallas_call(body, grid=(n // 4,), in_specs=[block(12, 4, 128), whole((...  11.1 us
    pallas_call x1, Pallas kernels, pack_images(): pl.pallas_call(pack_images_kernel, grid=(steps,), in_specs=[pl.BlockSpec(...  7.02 us
    ppermute x4, starting transfers between devices, along_z(): return lax.ppermute(value, 'z', [(i, (i + by) % size) for i in range(size)])  6.42 us
  transfers between devices with their start and end apart: 6, of which 6 were waited for; matrix products, arithmetic and copies ran while one was open for 0% of the time, Pallas kernels for 10%

profile of v4, /device:TPU:96, one launch (start us, length us, event | category | flops | bytes accessed | tf_op | source)
XLA Modules:
  0.0 168.5 jit_solution(7165395565940098603)
XLA Ops:
  0.6 2.2 %pack_templates.1 = f32[32,40,128]{2,1,0:T(8,128)} custom-call(f32[4,4,9216]{2,1,0:T(4,128)} %tpl_ref.1, s32[1,128]{1,0:T(1,128)} %bitcast.18, s32[1,128]{1,0:T(1,128)} %bitcast.19), custom_call_target="tpu_custom_call" | custom-call | bytes 1300000 | tf_op jit(solution)/shard_map/pack_templates/pallas_call | solution.py:92
  2.8 7.3 %all-to-all-start.1 = ((f32[32,40,128]{2,1,0:T(8,128)}), f32[32,40,128]{2,1,0:T(8,128)S(1)}, u32[]{:S(2)}, u32[]{:S(2)}) async-start(f32[32,40,128]{2,1,0:T(8,128)} %pack_templates.1), calls=%async_computation.1 | async-start | bytes 1310720 | tf_op jit(solution)/shard_map/all_to_all | solution.py:379
  10.2 7.0 %pack_images.1 = f32[32,288,128]{2,1,0:T(8,128)} custom-call(f32[128,9216]{1,0:T(8,128)} %rem_ref.1, f32[128,9216]{1,0:T(8,128)} %rem_ref.1), custom_call_target="tpu_custom_call" | custom-call | bytes 9500000 | tf_op jit(solution)/shard_map/pack_images/pallas_call | solution.py:60
  17.2 6.4 %all-to-all-done.1.tpl_ref.refs_1_ = f32[32,40,128]{2,1,0:T(8,128)S(1)} async-done(((f32[32,40,128]{2,1,0:T(8,128)}), f32[32,40,128]{2,1,0:T(8,128)S(1)}, u32[]{:S(2)}, u32[]{:S(2)}) %all-to-all-start.1) | async-done | bytes 655392 | tf_op jit(solution)/shard_map/all_to_all | solution.py:379
  23.6 4.9 %all-to-all-start = ((f32[32,288,128]{2,1,0:T(8,128)}), f32[32,288,128]{2,1,0:T(8,128)}, u32[]{:S(2)}, u32[]{:S(2)}) async-start(f32[32,288,128]{2,1,0:T(8,128)} %pack_images.1), calls=%async_computation | async-start | bytes 9437184 | tf_op jit(solution)/shard_map/all_to_all | solution.py:379
  28.6 3.2 %collective-permute-start = (f32[16,40,128]{2,1,0:T(8,128)S(1)}, f32[16,40,128]{2,1,0:T(8,128)S(1)}, u32[]{:S(2)}, u32[]{:S(2)}) collective-permute-start(f32[16,40,128]{2,1,0:T(8,128)S(1)} %get-tuple-element.24), channel_id=1, source_target_pairs={{0,2},{2,4},{4,6},{6,8},{8,10},{10,12},{12,14},{14,0},{1,3},{3,5},... | collective-permute-start | bytes 983048 | tf_op jit(solution)/shard_map/ppermute | solution.py:384
  31.8 0.1 copy.14
  32.0 0.1 pad.8.clone.sq_ref
  32.1 6.9 %collective-permute-done.below_ref = f32[16,40,128]{2,1,0:T(8,128)S(1)} collective-permute-done((f32[16,40,128]{2,1,0:T(8,128)S(1)}, f32[16,40,128]{2,1,0:T(8,128)S(1)}, u32[]{:S(2)}, u32[]{:S(2)}) %collective-permute-start) | collective-permute-done | bytes 327712 | tf_op jit(solution)/shard_map/ppermute | solution.py:384
  39.0 3.4 %collective-permute-done.1.above_ref = f32[16,40,128]{2,1,0:T(8,128)S(1)} collective-permute-done((f32[16,40,128]{2,1,0:T(8,128)S(1)}, f32[16,40,128]{2,1,0:T(8,128)S(1)}, u32[]{:S(2)}, u32[]{:S(2)}) %collective-permute-start.1) | collective-permute-done | bytes 327712 | tf_op jit(solution)/shard_map/ppermute | solution.py:384
  42.4 2.2 %operands.1 = (bf16[1024,640]{1,0:T(8,128)(2,1)S(1)}, bf16[48,384]{1,0:T(8,128)(2,1)S(1)}) custom-call(f32[32,40,128]{2,1,0:T(8,128)S(1)} %all-to-all-done.1.tpl_ref.refs_1_, f32[16,40,128]{2,1,0:T(8,128)S(1)} %collective-permute-done.below_ref, f32[16,40,128]{2,1,0:T(8,128)S(1)} %collective-permute-done.1.above_ref, f32[16,384]{1,0:T(8,128)S(1)} %concatenate.9.ctf_ref, ...), custom_call_target="tpu_custom_call" | custom-call | flops 600000000 | bytes 4000000 | tf_op jit(solution)/shard_map/operands/pallas_call | solution.py:137
  44.7 42.9 %all-to-all-done.buf0.buf1.buf2.buf3 = f32[32,288,128]{2,1,0:T(8,128)} async-done(((f32[32,288,128]{2,1,0:T(8,128)}), f32[32,288,128]{2,1,0:T(8,128)}, u32[]{:S(2)}, u32[]{:S(2)}) %all-to-all-start) | async-done | bytes 4718624 | tf_op jit(solution)/shard_map/all_to_all | solution.py:379
  87.6 12.1 %window_scores.1 = (bf16[32,128,256]{2,1,0:T(8,128)(2,1)S(1)}, bf16[32,128,256]{2,1,0:T(8,128)(2,1)S(1)}, bf16[32,128,128]{2,1,0:T(8,128)(2,1)S(1)}, f32[96,4,128]{2,1,0:T(4,128)S(1)}) custom-call(f32[32,288,128]{2,1,0:T(8,128)} %all-to-all-done.buf0.buf1.buf2.buf3, f32[32,288,128]{2,1,0:T(8,128)} %all-to-all-done.buf0.buf1.buf2.buf3, ...), custom_call_target="tpu_custom_call" | custom-call | flops 6000000000 | bytes 14000000 | tf_op jit(solution)/shard_map/window_scores/pallas_call | solution.py:196
  99.7 19.3 %all_to_all.25.scores_ref = f32[96,4,128]{2,1,0:T(4,128)S(1)} all-to-all(f32[96,4,128]{2,1,0:T(4,128)S(1)} %get-tuple-element.14), channel_id=1, replica_groups=mesh['dir'=16,'z'=8,'xlo'=2] {'dir','xlo'}, dimensions={0} | all-to-all | bytes 393216 | tf_op jit(solution)/shard_map/all_to_all | solution.py:379
  119.0 0.6 home.1
  119.6 11.8 %all_to_all.26.refs_0_ = f32[96,4,128]{2,1,0:T(4,128)S(1)} all-to-all(f32[96,4,128]{2,1,0:T(4,128)S(1)} %get-tuple-element.17), channel_id=1, replica_groups=mesh['dir'=16,'z'=8,'xlo'=2] {'dir','xlo'}, dimensions={0} | all-to-all | bytes 393216 | tf_op jit(solution)/shard_map/all_to_all | solution.py:379
  131.4 4.1 %sums_halo.1 = f32[512,384]{1,0:T(8,128)S(1)} custom-call(f32[96,4,128]{2,1,0:T(4,128)S(1)} %all_to_all.26.refs_0_, f32[32,40,128]{2,1,0:T(8,128)S(1)} %all-to-all-done.1.tpl_ref.refs_1_, bf16[32,128,256]{2,1,0:T(8,128)(2,1)S(1)} %get-tuple-element.18.refs_2_, bf16[32,128,256]{2,1,0:T(8,128)(2,1)S(1)} %get-tuple-element.19.refs_3_, ...), custom_call_target="tpu_custom_call" | custom-call | flops 4000000000 | bytes 6000000 | tf_op jit(solution)/shard_map/sums_halo/pallas_call | solution.py:308
  135.5 3.2 %collective-permute-start.2 = (f32[256,384]{1,0:T(8,128)S(1)}, f32[256,384]{1,0:T(8,128)S(1)}, u32[]{:S(2)}, u32[]{:S(2)}) collective-permute-start(f32[256,384]{1,0:T(8,128)S(1)} %get-tuple-element.22), channel_id=1, source_target_pairs={{0,2},{2,4},{4,6},{6,8},{8,10},{10,12},{12,14},{14,0},{1,3},{3,5},... | collective-permute-start | bytes 1179656 | tf_op jit(solution)/shard_map/ppermute | solution.py:384
  138.8 7.0 %sums_own.1.own_ref = f32[512,384]{1,0:T(8,128)S(1)} custom-call(f32[96,4,128]{2,1,0:T(4,128)S(1)} %all_to_all.26.refs_0_, f32[32,40,128]{2,1,0:T(8,128)S(1)} %all-to-all-done.1.tpl_ref.refs_1_, bf16[32,128,256]{2,1,0:T(8,128)(2,1)S(1)} %get-tuple-element.18.refs_2_, bf16[32,128,256]{2,1,0:T(8,128)(2,1)S(1)} %get-tuple-element.19.refs_3_, ...), custom_call_target="tpu_custom_call" | custom-call | flops 4000000000 | bytes 6000000 | tf_op jit(solution)/shard_map/sums_own/pallas_call | solution.py:308
  145.8 1.1 collective-permute-done.2.below_ref
  146.8 3.4 %collective-permute-done.3.above_ref = f32[256,384]{1,0:T(8,128)S(1)} collective-permute-done((f32[256,384]{1,0:T(8,128)S(1)}, f32[256,384]{1,0:T(8,128)S(1)}, u32[]{:S(2)}, u32[]{:S(2)}) %collective-permute-start.3) | collective-permute-done | bytes 393248 | tf_op jit(solution)/shard_map/ppermute | solution.py:384
  150.2 1.1 averages.1
  151.4 16.1 %all_to_all.27.got_ref = f32[288,4,128]{2,1,0:T(4,128)S(1)} all-to-all(f32[288,4,128]{2,1,0:T(4,128)S(1)} %averages.1), channel_id=1, replica_groups=mesh['dir'=16,'z'=8,'xlo'=2] {'dir','xlo'}, dimensions={0} | all-to-all | bytes 1179648 | tf_op jit(solution)/shard_map/all_to_all | solution.py:379
  167.5 1.0 unpack.1
  (15 shorter events, 0.3 us)
Async XLA Ops:
  0.6 27.8 %copy-start = (f32[16,9216]{1,0:T(8,128)S(1)}, f32[16,9216]{1,0:T(8,128)}, u32[]{:S(2)}) copy-start(f32[16,9216]{1,0:T(8,128)} %param.11) | copy-start | bytes 1769476
  2.8 20.7 %all-to-all-start.1 = ((f32[32,40,128]{2,1,0:T(8,128)}), f32[32,40,128]{2,1,0:T(8,128)S(1)}, u32[]{:S(2)}, u32[]{:S(2)}) async-start(f32[32,40,128]{2,1,0:T(8,128)} %pack_templates.1), calls=%async_computation.1 | async-start | bytes 1310720 | tf_op jit(solution)/shard_map/all_to_all | solution.py:379
  23.6 64.0 %all-to-all-start = ((f32[32,288,128]{2,1,0:T(8,128)}), f32[32,288,128]{2,1,0:T(8,128)}, u32[]{:S(2)}, u32[]{:S(2)}) async-start(f32[32,288,128]{2,1,0:T(8,128)} %pack_images.1), calls=%async_computation | async-start | bytes 9437184 | tf_op jit(solution)/shard_map/all_to_all | solution.py:379
  28.6 10.4 %collective-permute-start = (f32[16,40,128]{2,1,0:T(8,128)S(1)}, f32[16,40,128]{2,1,0:T(8,128)S(1)}, u32[]{:S(2)}, u32[]{:S(2)}) collective-permute-start(f32[16,40,128]{2,1,0:T(8,128)S(1)} %get-tuple-element.24), channel_id=1, source_target_pairs={{0,2},{2,4},{4,6},{6,8},{8,10},{10,12},{12,14},{14,0},{1,3},{3,5},... | collective-permute-start | bytes 983048 | tf_op jit(solution)/shard_map/ppermute | solution.py:384
  31.8 10.6 %collective-permute-start.1 = (f32[16,40,128]{2,1,0:T(8,128)S(1)}, f32[16,40,128]{2,1,0:T(8,128)S(1)}, u32[]{:S(2)}, u32[]{:S(2)}) collective-permute-start(f32[16,40,128]{2,1,0:T(8,128)S(1)} %get-tuple-element.23), channel_id=1, source_target_pairs={{0,14},{2,0},{4,2},{6,4},{8,6},{10,8},{12,10},{14,12},{1,15},{3,1}... | collective-permute-start | bytes 983048 | tf_op jit(solution)/shard_map/ppermute | solution.py:384
  87.6 31.4 %copy-start.1 = (s32[128]{0:T(128)S(1)}, s32[128]{0:T(128)}, u32[]{:S(2)}) copy-start(s32[128]{0:T(128)} %param.8) | copy-start | bytes 1540
  135.5 11.3 %collective-permute-start.2 = (f32[256,384]{1,0:T(8,128)S(1)}, f32[256,384]{1,0:T(8,128)S(1)}, u32[]{:S(2)}, u32[]{:S(2)}) collective-permute-start(f32[256,384]{1,0:T(8,128)S(1)} %get-tuple-element.22), channel_id=1, source_target_pairs={{0,2},{2,4},{4,6},{6,8},{8,10},{10,12},{12,14},{14,0},{1,3},{3,5},... | collective-permute-start | bytes 1179656 | tf_op jit(solution)/shard_map/ppermute | solution.py:384
  138.7 11.5 %collective-permute-start.3 = (f32[256,384]{1,0:T(8,128)S(1)}, f32[256,384]{1,0:T(8,128)S(1)}, u32[]{:S(2)}, u32[]{:S(2)}) collective-permute-start(f32[256,384]{1,0:T(8,128)S(1)} %get-tuple-element.21), channel_id=1, source_target_pairs={{0,14},{2,0},{4,2},{6,4},{8,6},{10,8},{12,10},{14,12},{1,15},{3,1}... | collective-permute-start | bytes 1179656 | tf_op jit(solution)/shard_map/ppermute | solution.py:384

commit v5 on v4

--- a/solution.py
+++ b/solution.py
@@ -162,21 +162,21 @@
         ctf = lax.dot_general(onehot, ce_ref[...], (((0,), (0,)), ((), ())), preferred_element_type=F32)
         for j in range(2):
             hi, lo = split(ctf[:, 128 * j : 128 * j + 128] * buf_ref[0, pl.ds(128 * j, 128), :])
-            xh_ref[s, :, pl.ds(128 * j, 128)] = hi
-            xl_ref[s, :, pl.ds(128 * j, 128)] = lo
+            xh_ref[source, :, pl.ds(128 * j, 128)] = hi
+            xl_ref[source, :, pl.ds(128 * j, 128)] = lo
         packed = buf_ref[0, pl.ds(256, 32), :]
         v = [turned(packed, j) for j in range(4)]
         one = jnp.ones_like(packed)
         rem = jnp.concatenate([pick_groups([v[(q - g) % 4] for q in (0, 1, 2)] + [one]) for g in range(4)], axis=0)
         hi, lo = split(ctf[:, 256:] * rem)
-        xr_ref[s, :, :] = jnp.where(group == 1, lo.astype(F32), hi.astype(F32)).astype(BF)
+        xr_ref[source] = jnp.where(group == 1, lo.astype(F32), hi.astype(F32)).astype(BF)
     row_bin = lax.broadcasted_iota(jnp.int32, (256, 256), 0) // 4
     for side in range(2):
-        pair = (side, 2 + side)
+        pair = (4 * step + side, 4 * step + 2 + side)
         x = jnp.concatenate(
             [jnp.concatenate([xh_ref[s], xh_ref[s], xl_ref[s], xr_ref[s]], axis=1) for s in pair], axis=0
         )
-        mine = row_bin == bins_of(tpl_ref, [4 * step + s for s in pair])
+        mine = row_bin == bins_of(tpl_ref, pair)
         y = y_ref[pl.ds(256 * side, 768), :]
         y = jnp.concatenate([y[:, :512], y[:, :256], y[:, 512:]], axis=1)
         all_rows = lax.dot_general(y, x, (((1,), (1,)), ((), ())), preferred_element_type=F32)
@@ -190,14 +190,13 @@
 
 def window_scores(buf, tpl, y, ctf):
     n = buf.shape[0]
-    whole = lambda shape: pl.BlockSpec(shape, lambda p: (0,) * len(shape))
-    block = lambda *shape: pl.BlockSpec(shape, lambda p: (p,) + (0,) * (len(shape) - 1))
+    vmem = pl.BlockSpec(memory_space=pltpu.VMEM)
     image = lambda k: pl.BlockSpec((1, IMG, LANES), lambda p: (4 * p + k, 0, 0))
     return pl.pallas_call(
         scores_kernel,
         grid=(n // 4,),
-        in_specs=[image(k) for k in range(4)] + [whole((n, TPL, LANES)), whole((1024, 640)), whole((48, 384))],
-        out_specs=[block(4, 128, 256), block(4, 128, 256), block(4, 128, 128), block(12, 4, 128)],
+        in_specs=[image(k) for k in range(4)] + [vmem] * 3,
+        out_specs=[vmem] * 4,
         out_shape=[
             jax.ShapeDtypeStruct((n, 128, 256), BF),
             jax.ShapeDtypeStruct((n, 128, 256), BF),
@@ -286,21 +285,20 @@
 
     if which == "halo":
         for side in range(2):
-            pair = (side, 2 + side)
-            bins = bins_of(tpl_ref, [4 * step + s for s in pair])
+            pair = (4 * step + side, 4 * step + 2 + side)
+            bins = bins_of(tpl_ref, pair)
             p8 = twice(pair, (2 * side, 2 * side))
             add(pl.ds(256 * side, 256), [spread(p8, bins, 0, 256)], pair)
     else:
-        four = range(4)
-        bins = bins_of(tpl_ref, [4 * step + s for s in four])
-        parts = [spread(twice(four, [k + 1 - s % 2 for s in four]), bins, 0, 256) for k in range(2)]
+        four = [4 * step + s for s in range(4)]
+        bins = bins_of(tpl_ref, four)
+        parts = [spread(twice(four, [k + 1, k, k + 1, k]), bins, 0, 256) for k in range(2)]
         add(pl.ds(0, 512), parts, four)
 
 
 def sums(which, p, tpl, xh, xl, xr):
     n = xh.shape[0]
-    whole = lambda shape: pl.BlockSpec(shape, lambda i: (0,) * len(shape))
-    block = lambda *shape: pl.BlockSpec(shape, lambda i: (i,) + (0,) * (len(shape) - 1))
+    vmem = pl.BlockSpec(memory_space=pltpu.VMEM)
 
     def body(*refs):
         sums_kernel(which, *refs)
@@ -308,8 +306,8 @@
     return pl.pallas_call(
         body,
         grid=(n // 4,),
-        in_specs=[block(12, 4, 128), whole((n, TPL, LANES)), block(4, 128, 256), block(4, 128, 256), block(4, 128, 128)],
-        out_specs=whole((512, 384)),
+        in_specs=[vmem] * 5,
+        out_specs=vmem,
         out_shape=jax.ShapeDtypeStruct((512, 384), F32),
         compiler_params=params(24),
         cost_estimate=cost(4_000_000_000, 6_000_000),

time: 169 us -> 169 us (level)
  no operation moved by 1% of the time
where the time goes in v5:
time: 169 us; the launch traced here: 168 us
  waiting for transfers between devices  64 us (38%)
  blocking collectives  47.2 us (28%)
  Pallas kernels  37.4 us (22%)
  starting transfers between devices  18.6 us (11%)
    all_to_all x2, waiting for transfers between devices, exchange(): return lax.all_to_all(value, PLANE, split_axis=0, concat_axis=0, tiled=True)  49.3 us
    all_to_all x3, blocking collectives, exchange(): return lax.all_to_all(value, PLANE, split_axis=0, concat_axis=0, tiled=True)  47.2 us
    ppermute x4, waiting for transfers between devices, along_z(): return lax.ppermute(value, 'z', [(i, (i + by) % size) for i in range(size)])  14.8 us
    all_to_all x2, starting transfers between devices, exchange(): return lax.all_to_all(value, PLANE, split_axis=0, concat_axis=0, tiled=True)  12.2 us
    pallas_call x1, Pallas kernels, window_scores(): pl.pallas_call(scores_kernel, grid=(n // 4,), in_specs=[image(k) for k in...  12.1 us
    pallas_call x2, Pallas kernels, sums(): pl.pallas_call(body, grid=(n // 4,), in_specs=[vmem] * 5, out_specs=vmem,...  11.1 us
    pallas_call x1, Pallas kernels, pack_images(): pl.pallas_call(pack_images_kernel, grid=(steps,), in_specs=[pl.BlockSpec(...  7.02 us
    ppermute x4, starting transfers between devices, along_z(): return lax.ppermute(value, 'z', [(i, (i + by) % size) for i in range(size)])  6.41 us
  transfers between devices with their start and end apart: 6, of which 6 were waited for; matrix products, arithmetic and copies ran while one was open for 0% of the time, Pallas kernels for 10%

profile of v5, /device:TPU:96, one launch (start us, length us, event | category | flops | bytes accessed | tf_op | source)
XLA Modules:
  0.0 168.5 jit_solution(9380337790655231259)
XLA Ops:
  0.6 2.2 %pack_templates.1 = f32[32,40,128]{2,1,0:T(8,128)} custom-call(f32[4,4,9216]{2,1,0:T(4,128)} %tpl_ref.1, s32[1,128]{1,0:T(1,128)} %bitcast.18, s32[1,128]{1,0:T(1,128)} %bitcast.19), custom_call_target="tpu_custom_call" | custom-call | bytes 1300000 | tf_op jit(solution)/shard_map/pack_templates/pallas_call | solution.py:92
  2.8 7.3 %all-to-all-start.1 = ((f32[32,40,128]{2,1,0:T(8,128)}), f32[32,40,128]{2,1,0:T(8,128)S(1)}, u32[]{:S(2)}, u32[]{:S(2)}) async-start(f32[32,40,128]{2,1,0:T(8,128)} %pack_templates.1), calls=%async_computation.1 | async-start | bytes 1310720 | tf_op jit(solution)/shard_map/all_to_all | solution.py:377
  10.2 7.0 %pack_images.1 = f32[32,288,128]{2,1,0:T(8,128)} custom-call(f32[128,9216]{1,0:T(8,128)} %rem_ref.1, f32[128,9216]{1,0:T(8,128)} %rem_ref.1), custom_call_target="tpu_custom_call" | custom-call | bytes 9500000 | tf_op jit(solution)/shard_map/pack_images/pallas_call | solution.py:60
  17.2 6.4 %all-to-all-done.1.tpl_ref.refs_1_ = f32[32,40,128]{2,1,0:T(8,128)S(1)} async-done(((f32[32,40,128]{2,1,0:T(8,128)}), f32[32,40,128]{2,1,0:T(8,128)S(1)}, u32[]{:S(2)}, u32[]{:S(2)}) %all-to-all-start.1) | async-done | bytes 655392 | tf_op jit(solution)/shard_map/all_to_all | solution.py:377
  23.6 4.9 %all-to-all-start = ((f32[32,288,128]{2,1,0:T(8,128)}), f32[32,288,128]{2,1,0:T(8,128)}, u32[]{:S(2)}, u32[]{:S(2)}) async-start(f32[32,288,128]{2,1,0:T(8,128)} %pack_images.1), calls=%async_computation | async-start | bytes 9437184 | tf_op jit(solution)/shard_map/all_to_all | solution.py:377
  28.6 3.2 %collective-permute-start = (f32[16,40,128]{2,1,0:T(8,128)S(1)}, f32[16,40,128]{2,1,0:T(8,128)S(1)}, u32[]{:S(2)}, u32[]{:S(2)}) collective-permute-start(f32[16,40,128]{2,1,0:T(8,128)S(1)} %get-tuple-element.24), channel_id=1, source_target_pairs={{0,2},{2,4},{4,6},{6,8},{8,10},{10,12},{12,14},{14,0},{1,3},{3,5},... | collective-permute-start | bytes 983048 | tf_op jit(solution)/shard_map/ppermute | solution.py:382
  31.8 0.1 copy.14
  32.0 0.1 pad.8.clone.sq_ref
  32.1 6.9 %collective-permute-done.below_ref = f32[16,40,128]{2,1,0:T(8,128)S(1)} collective-permute-done((f32[16,40,128]{2,1,0:T(8,128)S(1)}, f32[16,40,128]{2,1,0:T(8,128)S(1)}, u32[]{:S(2)}, u32[]{:S(2)}) %collective-permute-start) | collective-permute-done | bytes 327712 | tf_op jit(solution)/shard_map/ppermute | solution.py:382
  39.0 3.4 %collective-permute-done.1.above_ref = f32[16,40,128]{2,1,0:T(8,128)S(1)} collective-permute-done((f32[16,40,128]{2,1,0:T(8,128)S(1)}, f32[16,40,128]{2,1,0:T(8,128)S(1)}, u32[]{:S(2)}, u32[]{:S(2)}) %collective-permute-start.1) | collective-permute-done | bytes 327712 | tf_op jit(solution)/shard_map/ppermute | solution.py:382
  42.4 2.2 %operands.1 = (bf16[1024,640]{1,0:T(8,128)(2,1)S(1)}, bf16[48,384]{1,0:T(8,128)(2,1)S(1)}) custom-call(f32[32,40,128]{2,1,0:T(8,128)S(1)} %all-to-all-done.1.tpl_ref.refs_1_, f32[16,40,128]{2,1,0:T(8,128)S(1)} %collective-permute-done.below_ref, f32[16,40,128]{2,1,0:T(8,128)S(1)} %collective-permute-done.1.above_ref, f32[16,384]{1,0:T(8,128)S(1)} %concatenate.9.ctf_ref, ...), custom_call_target="tpu_custom_call" | custom-call | flops 600000000 | bytes 4000000 | tf_op jit(solution)/shard_map/operands/pallas_call | solution.py:137
  44.7 42.9 %all-to-all-done.buf0.buf1.buf2.buf3 = f32[32,288,128]{2,1,0:T(8,128)} async-done(((f32[32,288,128]{2,1,0:T(8,128)}), f32[32,288,128]{2,1,0:T(8,128)}, u32[]{:S(2)}, u32[]{:S(2)}) %all-to-all-start) | async-done | bytes 4718624 | tf_op jit(solution)/shard_map/all_to_all | solution.py:377
  87.6 12.1 %window_scores.1 = (bf16[32,128,256]{2,1,0:T(8,128)(2,1)S(1)}, bf16[32,128,256]{2,1,0:T(8,128)(2,1)S(1)}, bf16[32,128,128]{2,1,0:T(8,128)(2,1)S(1)}, f32[96,4,128]{2,1,0:T(4,128)S(1)}) custom-call(f32[32,288,128]{2,1,0:T(8,128)} %all-to-all-done.buf0.buf1.buf2.buf3, f32[32,288,128]{2,1,0:T(8,128)} %all-to-all-done.buf0.buf1.buf2.buf3, ...), custom_call_target="tpu_custom_call" | custom-call | flops 6000000000 | bytes 14000000 | tf_op jit(solution)/shard_map/window_scores/pallas_call | solution.py:195
  99.7 19.3 %all_to_all.25.scores_ref = f32[96,4,128]{2,1,0:T(4,128)S(1)} all-to-all(f32[96,4,128]{2,1,0:T(4,128)S(1)} %get-tuple-element.14), channel_id=1, replica_groups=mesh['dir'=16,'z'=8,'xlo'=2] {'dir','xlo'}, dimensions={0} | all-to-all | bytes 393216 | tf_op jit(solution)/shard_map/all_to_all | solution.py:377
  119.0 0.6 home.1
  119.6 11.8 %all_to_all.26.refs_0_ = f32[96,4,128]{2,1,0:T(4,128)S(1)} all-to-all(f32[96,4,128]{2,1,0:T(4,128)S(1)} %get-tuple-element.17), channel_id=1, replica_groups=mesh['dir'=16,'z'=8,'xlo'=2] {'dir','xlo'}, dimensions={0} | all-to-all | bytes 393216 | tf_op jit(solution)/shard_map/all_to_all | solution.py:377
  131.4 4.1 %sums_halo.1 = f32[512,384]{1,0:T(8,128)S(1)} custom-call(f32[96,4,128]{2,1,0:T(4,128)S(1)} %all_to_all.26.refs_0_, f32[32,40,128]{2,1,0:T(8,128)S(1)} %all-to-all-done.1.tpl_ref.refs_1_, bf16[32,128,256]{2,1,0:T(8,128)(2,1)S(1)} %get-tuple-element.18.refs_2_, bf16[32,128,256]{2,1,0:T(8,128)(2,1)S(1)} %get-tuple-element.19.refs_3_, ...), custom_call_target="tpu_custom_call" | custom-call | flops 4000000000 | bytes 6000000 | tf_op jit(solution)/shard_map/sums_halo/pallas_call | solution.py:306
  135.5 3.2 %collective-permute-start.2 = (f32[256,384]{1,0:T(8,128)S(1)}, f32[256,384]{1,0:T(8,128)S(1)}, u32[]{:S(2)}, u32[]{:S(2)}) collective-permute-start(f32[256,384]{1,0:T(8,128)S(1)} %get-tuple-element.22), channel_id=1, source_target_pairs={{0,2},{2,4},{4,6},{6,8},{8,10},{10,12},{12,14},{14,0},{1,3},{3,5},... | collective-permute-start | bytes 1179656 | tf_op jit(solution)/shard_map/ppermute | solution.py:382
  138.8 7.0 %sums_own.1.own_ref = f32[512,384]{1,0:T(8,128)S(1)} custom-call(f32[96,4,128]{2,1,0:T(4,128)S(1)} %all_to_all.26.refs_0_, f32[32,40,128]{2,1,0:T(8,128)S(1)} %all-to-all-done.1.tpl_ref.refs_1_, bf16[32,128,256]{2,1,0:T(8,128)(2,1)S(1)} %get-tuple-element.18.refs_2_, bf16[32,128,256]{2,1,0:T(8,128)(2,1)S(1)} %get-tuple-element.19.refs_3_, ...), custom_call_target="tpu_custom_call" | custom-call | flops 4000000000 | bytes 6000000 | tf_op jit(solution)/shard_map/sums_own/pallas_call | solution.py:306
  145.8 1.1 collective-permute-done.2.below_ref
  146.8 3.4 %collective-permute-done.3.above_ref = f32[256,384]{1,0:T(8,128)S(1)} collective-permute-done((f32[256,384]{1,0:T(8,128)S(1)}, f32[256,384]{1,0:T(8,128)S(1)}, u32[]{:S(2)}, u32[]{:S(2)}) %collective-permute-start.3) | collective-permute-done | bytes 393248 | tf_op jit(solution)/shard_map/ppermute | solution.py:382
  150.2 1.1 averages.1
  151.4 16.1 %all_to_all.27.got_ref = f32[288,4,128]{2,1,0:T(4,128)S(1)} all-to-all(f32[288,4,128]{2,1,0:T(4,128)S(1)} %averages.1), channel_id=1, replica_groups=mesh['dir'=16,'z'=8,'xlo'=2] {'dir','xlo'}, dimensions={0} | all-to-all | bytes 1179648 | tf_op jit(solution)/shard_map/all_to_all | solution.py:377
  167.5 1.0 unpack.1
  (15 shorter events, 0.3 us)
Async XLA Ops:
  0.6 27.8 %copy-start = (f32[16,9216]{1,0:T(8,128)S(1)}, f32[16,9216]{1,0:T(8,128)}, u32[]{:S(2)}) copy-start(f32[16,9216]{1,0:T(8,128)} %param.11) | copy-start | bytes 1769476
  2.8 20.7 %all-to-all-start.1 = ((f32[32,40,128]{2,1,0:T(8,128)}), f32[32,40,128]{2,1,0:T(8,128)S(1)}, u32[]{:S(2)}, u32[]{:S(2)}) async-start(f32[32,40,128]{2,1,0:T(8,128)} %pack_templates.1), calls=%async_computation.1 | async-start | bytes 1310720 | tf_op jit(solution)/shard_map/all_to_all | solution.py:377
  23.6 64.0 %all-to-all-start = ((f32[32,288,128]{2,1,0:T(8,128)}), f32[32,288,128]{2,1,0:T(8,128)}, u32[]{:S(2)}, u32[]{:S(2)}) async-start(f32[32,288,128]{2,1,0:T(8,128)} %pack_images.1), calls=%async_computation | async-start | bytes 9437184 | tf_op jit(solution)/shard_map/all_to_all | solution.py:377
  28.6 10.4 %collective-permute-start = (f32[16,40,128]{2,1,0:T(8,128)S(1)}, f32[16,40,128]{2,1,0:T(8,128)S(1)}, u32[]{:S(2)}, u32[]{:S(2)}) collective-permute-start(f32[16,40,128]{2,1,0:T(8,128)S(1)} %get-tuple-element.24), channel_id=1, source_target_pairs={{0,2},{2,4},{4,6},{6,8},{8,10},{10,12},{12,14},{14,0},{1,3},{3,5},... | collective-permute-start | bytes 983048 | tf_op jit(solution)/shard_map/ppermute | solution.py:382
  31.8 10.6 %collective-permute-start.1 = (f32[16,40,128]{2,1,0:T(8,128)S(1)}, f32[16,40,128]{2,1,0:T(8,128)S(1)}, u32[]{:S(2)}, u32[]{:S(2)}) collective-permute-start(f32[16,40,128]{2,1,0:T(8,128)S(1)} %get-tuple-element.23), channel_id=1, source_target_pairs={{0,14},{2,0},{4,2},{6,4},{8,6},{10,8},{12,10},{14,12},{1,15},{3,1}... | collective-permute-start | bytes 983048 | tf_op jit(solution)/shard_map/ppermute | solution.py:382
  87.6 31.4 %copy-start.1 = (s32[128]{0:T(128)S(1)}, s32[128]{0:T(128)}, u32[]{:S(2)}) copy-start(s32[128]{0:T(128)} %param.8) | copy-start | bytes 1540
  135.5 11.3 %collective-permute-start.2 = (f32[256,384]{1,0:T(8,128)S(1)}, f32[256,384]{1,0:T(8,128)S(1)}, u32[]{:S(2)}, u32[]{:S(2)}) collective-permute-start(f32[256,384]{1,0:T(8,128)S(1)} %get-tuple-element.22), channel_id=1, source_target_pairs={{0,2},{2,4},{4,6},{6,8},{8,10},{10,12},{12,14},{14,0},{1,3},{3,5},... | collective-permute-start | bytes 1179656 | tf_op jit(solution)/shard_map/ppermute | solution.py:382
  138.7 11.5 %collective-permute-start.3 = (f32[256,384]{1,0:T(8,128)S(1)}, f32[256,384]{1,0:T(8,128)S(1)}, u32[]{:S(2)}, u32[]{:S(2)}) collective-permute-start(f32[256,384]{1,0:T(8,128)S(1)} %get-tuple-element.21), channel_id=1, source_target_pairs={{0,14},{2,0},{4,2},{6,4},{8,6},{10,8},{12,10},{14,12},{1,15},{3,1}... | collective-permute-start | bytes 1179656 | tf_op jit(solution)/shard_map/ppermute | solution.py:382

commit v6 on v5

--- a/solution.py
+++ b/solution.py
@@ -151,31 +151,37 @@
     return jnp.concatenate(rows, axis=1).astype(jnp.int32)
 
 
-def scores_kernel(buf0, buf1, buf2, buf3, tpl_ref, y_ref, ce_ref, xh_ref, xl_ref, xr_ref, out_ref):
-    step = pl.program_id(0)
+def weigh(buf_ref, step, tpl_ref, ce_ref, x_ref, xh_ref, xl_ref, xr_ref):
     group = lane_group((128, LANES))
-    for s, buf_ref in enumerate((buf0, buf1, buf2, buf3)):
+    for s in range(4):
         source = 4 * step + s
         classes = tpl_ref[source, pl.ds(META + 2, 1), :].astype(jnp.int32)
         row_class = lax.broadcasted_iota(jnp.int32, (48, 128), 0) % CLASSES
         onehot = jnp.where(row_class == classes, 1.0, 0.0).astype(BF)
         ctf = lax.dot_general(onehot, ce_ref[...], (((0,), (0,)), ((), ())), preferred_element_type=F32)
+        rows = pl.ds(256 * (s % 2) + 128 * (s // 2), 128)
         for j in range(2):
-            hi, lo = split(ctf[:, 128 * j : 128 * j + 128] * buf_ref[0, pl.ds(128 * j, 128), :])
+            hi, lo = split(ctf[:, 128 * j : 128 * j + 128] * buf_ref[s, pl.ds(128 * j, 128), :])
             xh_ref[source, :, pl.ds(128 * j, 128)] = hi
             xl_ref[source, :, pl.ds(128 * j, 128)] = lo
-        packed = buf_ref[0, pl.ds(256, 32), :]
+            x_ref[rows, pl.ds(128 * j, 128)] = hi
+            x_ref[rows, pl.ds(256 + 128 * j, 128)] = lo
+        packed = buf_ref[s, pl.ds(256, 32), :]
         v = [turned(packed, j) for j in range(4)]
         one = jnp.ones_like(packed)
         rem = jnp.concatenate([pick_groups([v[(q - g) % 4] for q in (0, 1, 2)] + [one]) for g in range(4)], axis=0)
         hi, lo = split(ctf[:, 256:] * rem)
-        xr_ref[source] = jnp.where(group == 1, lo.astype(F32), hi.astype(F32)).astype(BF)
+        tail = jnp.where(group == 1, lo.astype(F32), hi.astype(F32)).astype(BF)
+        xr_ref[source] = tail
+        x_ref[rows, pl.ds(512, 128)] = tail
+
+
+def score(step, x_ref, tpl_ref, y_ref, out_ref):
     row_bin = lax.broadcasted_iota(jnp.int32, (256, 256), 0) // 4
     for side in range(2):
         pair = (4 * step + side, 4 * step + 2 + side)
-        x = jnp.concatenate(
-            [jnp.concatenate([xh_ref[s], xh_ref[s], xl_ref[s], xr_ref[s]], axis=1) for s in pair], axis=0
-        )
+        x = x_ref[pl.ds(256 * side, 256), :]
+        x = jnp.concatenate([x[:, :256], x], axis=1)
         mine = row_bin == bins_of(tpl_ref, pair)
         y = y_ref[pl.ds(256 * side, 768), :]
         y = jnp.concatenate([y[:, :512], y[:, :256], y[:, 512:]], axis=1)
@@ -188,14 +194,30 @@
                 out_ref[3 * s + k] = total[:4, 128 * half : 128 * half + 128]
 
 
+def scores_kernel(first_ref, odd_ref, even_ref, tpl_ref, y_ref, ce_ref, xh_ref, xl_ref, xr_ref, out_ref, xa_ref, xb_ref):
+    i = pl.program_id(0)
+    last = 2 * pl.num_programs(0) - 1
+    kept = (xh_ref, xl_ref, xr_ref)
+
+    @pl.when(i == 0)
+    def _():
+        weigh(first_ref, 0, tpl_ref, ce_ref, xa_ref, *kept)
+
+    weigh(odd_ref, 2 * i + 1, tpl_ref, ce_ref, xb_ref, *kept)
+    score(2 * i, xa_ref, tpl_ref, y_ref, out_ref)
+    weigh(even_ref, jnp.minimum(2 * i + 2, last), tpl_ref, ce_ref, xa_ref, *kept)
+    score(2 * i + 1, xb_ref, tpl_ref, y_ref, out_ref)
+
+
 def window_scores(buf, tpl, y, ctf):
     n = buf.shape[0]
-    vmem = pl.BlockSpec(memory_space=pltpu.VMEM)
-    image = lambda k: pl.BlockSpec((1, IMG, LANES), lambda p: (4 * p + k, 0, 0))
+    blocks = n // 4
+    vmem = pl.BlockSpec(memory_space=pltpu.VMEM)
+    image = lambda at: pl.BlockSpec((4, IMG, LANES), lambda p: (at(p), 0, 0))
     return pl.pallas_call(
         scores_kernel,
-        grid=(n // 4,),
-        in_specs=[image(k) for k in range(4)] + [vmem] * 3,
+        grid=(blocks // 2,),
+        in_specs=[image(lambda p: 0), image(lambda p: 2 * p + 1), image(lambda p: jnp.minimum(2 * p + 2, blocks - 1))] + [vmem] * 3,
         out_specs=[vmem] * 4,
         out_shape=[
             jax.ShapeDtypeStruct((n, 128, 256), BF),
@@ -203,10 +225,11 @@
             jax.ShapeDtypeStruct((n, 128, 128), BF),
             jax.ShapeDtypeStruct((3 * n, 4, 128), F32),
         ],
+        scratch_shapes=[pltpu.VMEM((512, 640), BF), pltpu.VMEM((512, 640), BF)],
         compiler_params=params(24),
         cost_estimate=cost(6_000_000_000, 14_000_000),
         name="window_scores",
-    )(buf, buf, buf, buf, tpl, y, ctf)
+    )(buf, buf, buf, tpl, y, ctf)
 
 
 def home_kernel(scores_ref, centre_ref, total_ref, shift_ref, p_ref):

time: 169 us -> 168 us (level)
  no operation moved by 1% of the time
where the time goes in v6:
time: 168 us; the launch traced here: 167 us
  waiting for transfers between devices  64.1 us (38%)
  blocking collectives  47.2 us (28%)
  Pallas kernels  36.2 us (22%)
  starting transfers between devices  18.6 us (11%)
    all_to_all x2, waiting for transfers between devices, exchange(): return lax.all_to_all(value, PLANE, split_axis=0, concat_axis=0, tiled=True)  49.3 us
    all_to_all x3, blocking collectives, exchange(): return lax.all_to_all(value, PLANE, split_axis=0, concat_axis=0, tiled=True)  47.2 us
    ppermute x4, waiting for transfers between devices, along_z(): return lax.ppermute(value, 'z', [(i, (i + by) % size) for i in range(size)])  14.8 us
    all_to_all x2, starting transfers between devices, exchange(): return lax.all_to_all(value, PLANE, split_axis=0, concat_axis=0, tiled=True)  12.2 us
    pallas_call x2, Pallas kernels, sums(): pl.pallas_call(body, grid=(n // 4,), in_specs=[vmem] * 5, out_specs=vmem,...  11.1 us
    pallas_call x1, Pallas kernels, window_scores(): pl.pallas_call(scores_kernel, grid=(blocks // 2,), in_specs=[image(lambda...  10.9 us
    pallas_call x1, Pallas kernels, pack_images(): pl.pallas_call(pack_images_kernel, grid=(steps,), in_specs=[pl.BlockSpec(...  7.02 us
    ppermute x4, starting transfers between devices, along_z(): return lax.ppermute(value, 'z', [(i, (i + by) % size) for i in range(size)])  6.41 us
  transfers between devices with their start and end apart: 6, of which 6 were waited for; matrix products, arithmetic and copies ran while one was open for 0% of the time, Pallas kernels for 10%

profile of v6, /device:TPU:96, one launch (start us, length us, event | category | flops | bytes accessed | tf_op | source)
XLA Modules:
  0.0 167.3 jit_solution(9809734989997910788)
XLA Ops:
  0.6 2.2 %pack_templates.1 = f32[32,40,128]{2,1,0:T(8,128)} custom-call(f32[4,4,9216]{2,1,0:T(4,128)} %tpl_ref.1, s32[1,128]{1,0:T(1,128)} %bitcast.18, s32[1,128]{1,0:T(1,128)} %bitcast.19), custom_call_target="tpu_custom_call" | custom-call | bytes 1300000 | tf_op jit(solution)/shard_map/pack_templates/pallas_call | solution.py:92
  2.8 7.3 %all-to-all-start.1 = ((f32[32,40,128]{2,1,0:T(8,128)}), f32[32,40,128]{2,1,0:T(8,128)S(1)}, u32[]{:S(2)}, u32[]{:S(2)}) async-start(f32[32,40,128]{2,1,0:T(8,128)} %pack_templates.1), calls=%async_computation.1 | async-start | bytes 1310720 | tf_op jit(solution)/shard_map/all_to_all | solution.py:400
  10.2 7.0 %pack_images.1 = f32[32,288,128]{2,1,0:T(8,128)} custom-call(f32[128,9216]{1,0:T(8,128)} %rem_ref.1, f32[128,9216]{1,0:T(8,128)} %rem_ref.1), custom_call_target="tpu_custom_call" | custom-call | bytes 9500000 | tf_op jit(solution)/shard_map/pack_images/pallas_call | solution.py:60
  17.2 6.4 %all-to-all-done.1.tpl_ref.refs_1_ = f32[32,40,128]{2,1,0:T(8,128)S(1)} async-done(((f32[32,40,128]{2,1,0:T(8,128)}), f32[32,40,128]{2,1,0:T(8,128)S(1)}, u32[]{:S(2)}, u32[]{:S(2)}) %all-to-all-start.1) | async-done | bytes 655392 | tf_op jit(solution)/shard_map/all_to_all | solution.py:400
  23.6 4.9 %all-to-all-start = ((f32[32,288,128]{2,1,0:T(8,128)}), f32[32,288,128]{2,1,0:T(8,128)}, u32[]{:S(2)}, u32[]{:S(2)}) async-start(f32[32,288,128]{2,1,0:T(8,128)} %pack_images.1), calls=%async_computation | async-start | bytes 9437184 | tf_op jit(solution)/shard_map/all_to_all | solution.py:400
  28.6 3.2 %collective-permute-start = (f32[16,40,128]{2,1,0:T(8,128)S(1)}, f32[16,40,128]{2,1,0:T(8,128)S(1)}, u32[]{:S(2)}, u32[]{:S(2)}) collective-permute-start(f32[16,40,128]{2,1,0:T(8,128)S(1)} %get-tuple-element.24), channel_id=1, source_target_pairs={{0,2},{2,4},{4,6},{6,8},{8,10},{10,12},{12,14},{14,0},{1,3},{3,5},... | collective-permute-start | bytes 983048 | tf_op jit(solution)/shard_map/ppermute | solution.py:405
  31.8 0.1 copy.14
  32.0 0.1 pad.8.clone.sq_ref
  32.1 6.9 %collective-permute-done.below_ref = f32[16,40,128]{2,1,0:T(8,128)S(1)} collective-permute-done((f32[16,40,128]{2,1,0:T(8,128)S(1)}, f32[16,40,128]{2,1,0:T(8,128)S(1)}, u32[]{:S(2)}, u32[]{:S(2)}) %collective-permute-start) | collective-permute-done | bytes 327712 | tf_op jit(solution)/shard_map/ppermute | solution.py:405
  39.0 3.4 %collective-permute-done.1.above_ref = f32[16,40,128]{2,1,0:T(8,128)S(1)} collective-permute-done((f32[16,40,128]{2,1,0:T(8,128)S(1)}, f32[16,40,128]{2,1,0:T(8,128)S(1)}, u32[]{:S(2)}, u32[]{:S(2)}) %collective-permute-start.1) | collective-permute-done | bytes 327712 | tf_op jit(solution)/shard_map/ppermute | solution.py:405
  42.4 2.2 %operands.1 = (bf16[1024,640]{1,0:T(8,128)(2,1)S(1)}, bf16[48,384]{1,0:T(8,128)(2,1)S(1)}) custom-call(f32[32,40,128]{2,1,0:T(8,128)S(1)} %all-to-all-done.1.tpl_ref.refs_1_, f32[16,40,128]{2,1,0:T(8,128)S(1)} %collective-permute-done.below_ref, f32[16,40,128]{2,1,0:T(8,128)S(1)} %collective-permute-done.1.above_ref, f32[16,384]{1,0:T(8,128)S(1)} %concatenate.9.ctf_ref, ...), custom_call_target="tpu_custom_call" | custom-call | flops 600000000 | bytes 4000000 | tf_op jit(solution)/shard_map/operands/pallas_call | solution.py:137
  44.7 42.9 %all-to-all-done.first_ref.odd_ref.even_ref = f32[32,288,128]{2,1,0:T(8,128)} async-done(((f32[32,288,128]{2,1,0:T(8,128)}), f32[32,288,128]{2,1,0:T(8,128)}, u32[]{:S(2)}, u32[]{:S(2)}) %all-to-all-start) | async-done | bytes 4718624 | tf_op jit(solution)/shard_map/all_to_all | solution.py:400
  87.6 10.9 %window_scores.1 = (bf16[32,128,256]{2,1,0:T(8,128)(2,1)S(1)}, bf16[32,128,256]{2,1,0:T(8,128)(2,1)S(1)}, bf16[32,128,128]{2,1,0:T(8,128)(2,1)S(1)}, f32[96,4,128]{2,1,0:T(4,128)S(1)}) custom-call(f32[32,288,128]{2,1,0:T(8,128)} %all-to-all-done.first_ref.odd_ref.even_ref, f32[32,288,128]{2,1,0:T(8,128)} %all-to-all-done.first_ref.odd_ref.even_ref, ...), custom_call_target="tpu_custom_call" | custom-call | flops 6000000000 | bytes 14000000 | tf_op jit(solution)/shard_map/window_scores/pallas_call | solution.py:217
  98.5 19.3 %all_to_all.25.scores_ref = f32[96,4,128]{2,1,0:T(4,128)S(1)} all-to-all(f32[96,4,128]{2,1,0:T(4,128)S(1)} %get-tuple-element.14), channel_id=1, replica_groups=mesh['dir'=16,'z'=8,'xlo'=2] {'dir','xlo'}, dimensions={0} | all-to-all | bytes 393216 | tf_op jit(solution)/shard_map/all_to_all | solution.py:400
  117.8 0.6 home.1
  118.5 11.8 %all_to_all.26.refs_0_ = f32[96,4,128]{2,1,0:T(4,128)S(1)} all-to-all(f32[96,4,128]{2,1,0:T(4,128)S(1)} %get-tuple-element.17), channel_id=1, replica_groups=mesh['dir'=16,'z'=8,'xlo'=2] {'dir','xlo'}, dimensions={0} | all-to-all | bytes 393216 | tf_op jit(solution)/shard_map/all_to_all | solution.py:400
  130.2 4.1 %sums_halo.1 = f32[512,384]{1,0:T(8,128)S(1)} custom-call(f32[96,4,128]{2,1,0:T(4,128)S(1)} %all_to_all.26.refs_0_, f32[32,40,128]{2,1,0:T(8,128)S(1)} %all-to-all-done.1.tpl_ref.refs_1_, bf16[32,128,256]{2,1,0:T(8,128)(2,1)S(1)} %get-tuple-element.18.refs_2_, bf16[32,128,256]{2,1,0:T(8,128)(2,1)S(1)} %get-tuple-element.19.refs_3_, ...), custom_call_target="tpu_custom_call" | custom-call | flops 4000000000 | bytes 6000000 | tf_op jit(solution)/shard_map/sums_halo/pallas_call | solution.py:329
  134.4 3.2 %collective-permute-start.2 = (f32[256,384]{1,0:T(8,128)S(1)}, f32[256,384]{1,0:T(8,128)S(1)}, u32[]{:S(2)}, u32[]{:S(2)}) collective-permute-start(f32[256,384]{1,0:T(8,128)S(1)} %get-tuple-element.22), channel_id=1, source_target_pairs={{0,2},{2,4},{4,6},{6,8},{8,10},{10,12},{12,14},{14,0},{1,3},{3,5},... | collective-permute-start | bytes 1179656 | tf_op jit(solution)/shard_map/ppermute | solution.py:405
  137.6 7.0 %sums_own.1.own_ref = f32[512,384]{1,0:T(8,128)S(1)} custom-call(f32[96,4,128]{2,1,0:T(4,128)S(1)} %all_to_all.26.refs_0_, f32[32,40,128]{2,1,0:T(8,128)S(1)} %all-to-all-done.1.tpl_ref.refs_1_, bf16[32,128,256]{2,1,0:T(8,128)(2,1)S(1)} %get-tuple-element.18.refs_2_, bf16[32,128,256]{2,1,0:T(8,128)(2,1)S(1)} %get-tuple-element.19.refs_3_, ...), custom_call_target="tpu_custom_call" | custom-call | flops 4000000000 | bytes 6000000 | tf_op jit(solution)/shard_map/sums_own/pallas_call | solution.py:329
  144.6 1.1 collective-permute-done.2.below_ref
  145.7 3.4 %collective-permute-done.3.above_ref = f32[256,384]{1,0:T(8,128)S(1)} collective-permute-done((f32[256,384]{1,0:T(8,128)S(1)}, f32[256,384]{1,0:T(8,128)S(1)}, u32[]{:S(2)}, u32[]{:S(2)}) %collective-permute-start.3) | collective-permute-done | bytes 393248 | tf_op jit(solution)/shard_map/ppermute | solution.py:405
  149.1 1.1 averages.1
  150.2 16.1 %all_to_all.27.got_ref = f32[288,4,128]{2,1,0:T(4,128)S(1)} all-to-all(f32[288,4,128]{2,1,0:T(4,128)S(1)} %averages.1), channel_id=1, replica_groups=mesh['dir'=16,'z'=8,'xlo'=2] {'dir','xlo'}, dimensions={0} | all-to-all | bytes 1179648 | tf_op jit(solution)/shard_map/all_to_all | solution.py:400
  166.3 1.0 unpack.1
  (15 shorter events, 0.3 us)
Async XLA Ops:
  0.6 27.8 %copy-start = (f32[16,9216]{1,0:T(8,128)S(1)}, f32[16,9216]{1,0:T(8,128)}, u32[]{:S(2)}) copy-start(f32[16,9216]{1,0:T(8,128)} %param.11) | copy-start | bytes 1769476
  2.8 20.7 %all-to-all-start.1 = ((f32[32,40,128]{2,1,0:T(8,128)}), f32[32,40,128]{2,1,0:T(8,128)S(1)}, u32[]{:S(2)}, u32[]{:S(2)}) async-start(f32[32,40,128]{2,1,0:T(8,128)} %pack_templates.1), calls=%async_computation.1 | async-start | bytes 1310720 | tf_op jit(solution)/shard_map/all_to_all | solution.py:400
  23.6 64.0 %all-to-all-start = ((f32[32,288,128]{2,1,0:T(8,128)}), f32[32,288,128]{2,1,0:T(8,128)}, u32[]{:S(2)}, u32[]{:S(2)}) async-start(f32[32,288,128]{2,1,0:T(8,128)} %pack_images.1), calls=%async_computation | async-start | bytes 9437184 | tf_op jit(solution)/shard_map/all_to_all | solution.py:400
  28.6 10.4 %collective-permute-start = (f32[16,40,128]{2,1,0:T(8,128)S(1)}, f32[16,40,128]{2,1,0:T(8,128)S(1)}, u32[]{:S(2)}, u32[]{:S(2)}) collective-permute-start(f32[16,40,128]{2,1,0:T(8,128)S(1)} %get-tuple-element.24), channel_id=1, source_target_pairs={{0,2},{2,4},{4,6},{6,8},{8,10},{10,12},{12,14},{14,0},{1,3},{3,5},... | collective-permute-start | bytes 983048 | tf_op jit(solution)/shard_map/ppermute | solution.py:405
  31.8 10.6 %collective-permute-start.1 = (f32[16,40,128]{2,1,0:T(8,128)S(1)}, f32[16,40,128]{2,1,0:T(8,128)S(1)}, u32[]{:S(2)}, u32[]{:S(2)}) collective-permute-start(f32[16,40,128]{2,1,0:T(8,128)S(1)} %get-tuple-element.23), channel_id=1, source_target_pairs={{0,14},{2,0},{4,2},{6,4},{8,6},{10,8},{12,10},{14,12},{1,15},{3,1}... | collective-permute-start | bytes 983048 | tf_op jit(solution)/shard_map/ppermute | solution.py:405
  87.6 30.3 %copy-start.1 = (s32[128]{0:T(128)S(1)}, s32[128]{0:T(128)}, u32[]{:S(2)}) copy-start(s32[128]{0:T(128)} %param.8) | copy-start | bytes 1540
  134.4 11.3 %collective-permute-start.2 = (f32[256,384]{1,0:T(8,128)S(1)}, f32[256,384]{1,0:T(8,128)S(1)}, u32[]{:S(2)}, u32[]{:S(2)}) collective-permute-start(f32[256,384]{1,0:T(8,128)S(1)} %get-tuple-element.22), channel_id=1, source_target_pairs={{0,2},{2,4},{4,6},{6,8},{8,10},{10,12},{12,14},{14,0},{1,3},{3,5},... | collective-permute-start | bytes 1179656 | tf_op jit(solution)/shard_map/ppermute | solution.py:405
  137.6 11.5 %collective-permute-start.3 = (f32[256,384]{1,0:T(8,128)S(1)}, f32[256,384]{1,0:T(8,128)S(1)}, u32[]{:S(2)}, u32[]{:S(2)}) collective-permute-start(f32[256,384]{1,0:T(8,128)S(1)} %get-tuple-element.21), channel_id=1, source_target_pairs={{0,14},{2,0},{4,2},{6,4},{8,6},{10,8},{12,10},{14,12},{1,15},{3,1}... | collective-permute-start | bytes 1179656 | tf_op jit(solution)/shard_map/ppermute | solution.py:405

commit v7 on v6

--- a/solution.py
+++ b/solution.py
@@ -283,7 +283,7 @@
     return [jnp.where(mine, wide(v), 0.0).astype(BF) for v in (hi, lo)]
 
 
-def sums_kernel(which, p_ref, tpl_ref, xh_ref, xl_ref, xr_ref, out_ref):
+def sums_kernel(which, group, p_ref, tpl_ref, xh_ref, xl_ref, xr_ref, out_ref):
     step = pl.program_id(0)
 
     @pl.when(step == 0)
@@ -308,27 +308,26 @@
 
     if which == "halo":
         for side in range(2):
-            pair = (4 * step + side, 4 * step + 2 + side)
-            bins = bins_of(tpl_ref, pair)
-            p8 = twice(pair, (2 * side, 2 * side))
-            add(pl.ds(256 * side, 256), [spread(p8, bins, 0, 256)], pair)
+            mine = [group * step + s for s in range(side, group, 2)]
+            p8 = twice(mine, [2 * side] * len(mine))
+            add(pl.ds(256 * side, 256), [spread(p8, bins_of(tpl_ref, mine), 0, 256)], mine)
     else:
-        four = [4 * step + s for s in range(4)]
-        bins = bins_of(tpl_ref, four)
-        parts = [spread(twice(four, [k + 1, k, k + 1, k]), bins, 0, 256) for k in range(2)]
-        add(pl.ds(0, 512), parts, four)
-
-
-def sums(which, p, tpl, xh, xl, xr):
+        mine = [group * step + s for s in range(group)]
+        bins = bins_of(tpl_ref, mine)
+        parts = [spread(twice(mine, [k + 1, k] * (group // 2)), bins, 0, 256) for k in range(2)]
+        add(pl.ds(0, 512), parts, mine)
+
+
+def sums(which, p, tpl, xh, xl, xr, group=32):
     n = xh.shape[0]
     vmem = pl.BlockSpec(memory_space=pltpu.VMEM)
 
     def body(*refs):
-        sums_kernel(which, *refs)
+        sums_kernel(which, group, *refs)
 
     return pl.pallas_call(
         body,
-        grid=(n // 4,),
+        grid=(n // group,),
         in_specs=[vmem] * 5,
         out_specs=vmem,
         out_shape=jax.ShapeDtypeStruct((512, 384), F32),

time: 168 us -> 167 us (level)
  Pallas kernels: 36.2 us -> 33.6 us
    pallas_call x2, Pallas kernels: 11.1 us -> 8.53 us  [sums(): pl.pallas_call(body, grid=(n // group,), in_specs=[vmem] * 5, out_specs=v...]
  transfers between devices with their start and end apart: 6 -> 6, of which waited for: 6 -> 6; matrix products, arithmetic and copies ran while one was open for 0% -> 0% of each run, Pallas kernels for 10% -> 9%
where the time goes in v7:
time: 167 us; the launch traced here: 166 us
  waiting for transfers between devices  65.4 us (39%)
  blocking collectives  47.2 us (28%)
  Pallas kernels  33.6 us (20%)
  starting transfers between devices  18.8 us (11%)
    all_to_all x2, waiting for transfers between devices, exchange(): return lax.all_to_all(value, PLANE, split_axis=0, concat_axis=0, tiled=True)  49.3 us
    all_to_all x3, blocking collectives, exchange(): return lax.all_to_all(value, PLANE, split_axis=0, concat_axis=0, tiled=True)  47.2 us
    ppermute x4, waiting for transfers between devices, along_z(): return lax.ppermute(value, 'z', [(i, (i + by) % size) for i in range(size)])  16.2 us
    all_to_all x2, starting transfers between devices, exchange(): return lax.all_to_all(value, PLANE, split_axis=0, concat_axis=0, tiled=True)  12.2 us
    pallas_call x1, Pallas kernels, window_scores(): pl.pallas_call(scores_kernel, grid=(blocks // 2,), in_specs=[image(lambda...  10.9 us
    pallas_call x2, Pallas kernels, sums(): pl.pallas_call(body, grid=(n // group,), in_specs=[vmem] * 5, out_specs=v...  8.53 us
    pallas_call x1, Pallas kernels, pack_images(): pl.pallas_call(pack_images_kernel, grid=(steps,), in_specs=[pl.BlockSpec(...  7.02 us
    ppermute x4, starting transfers between devices, along_z(): return lax.ppermute(value, 'z', [(i, (i + by) % size) for i in range(size)])  6.59 us
  transfers between devices with their start and end apart: 6, of which 6 were waited for; matrix products, arithmetic and copies ran while one was open for 0% of the time, Pallas kernels for 9%

profile of v7, /device:TPU:96, one launch (start us, length us, event | category | flops | bytes accessed | tf_op | source)
XLA Modules:
  0.0 166.3 jit_solution(5343476249449749688)
XLA Ops:
  0.6 2.2 %pack_templates.1 = f32[32,40,128]{2,1,0:T(8,128)} custom-call(f32[4,4,9216]{2,1,0:T(4,128)} %tpl_ref.1, s32[1,128]{1,0:T(1,128)} %bitcast.18, s32[1,128]{1,0:T(1,128)} %bitcast.19), custom_call_target="tpu_custom_call" | custom-call | bytes 1300000 | tf_op jit(solution)/shard_map/pack_templates/pallas_call | solution.py:92
  2.8 7.3 %all-to-all-start.1 = ((f32[32,40,128]{2,1,0:T(8,128)}), f32[32,40,128]{2,1,0:T(8,128)S(1)}, u32[]{:S(2)}, u32[]{:S(2)}) async-start(f32[32,40,128]{2,1,0:T(8,128)} %pack_templates.1), calls=%async_computation.1 | async-start | bytes 1310720 | tf_op jit(solution)/shard_map/all_to_all | solution.py:399
  10.2 7.0 %pack_images.1 = f32[32,288,128]{2,1,0:T(8,128)} custom-call(f32[128,9216]{1,0:T(8,128)} %rem_ref.1, f32[128,9216]{1,0:T(8,128)} %rem_ref.1), custom_call_target="tpu_custom_call" | custom-call | bytes 9500000 | tf_op jit(solution)/shard_map/pack_images/pallas_call | solution.py:60
  17.2 6.4 %all-to-all-done.1.tpl_ref.refs_1_ = f32[32,40,128]{2,1,0:T(8,128)S(1)} async-done(((f32[32,40,128]{2,1,0:T(8,128)}), f32[32,40,128]{2,1,0:T(8,128)S(1)}, u32[]{:S(2)}, u32[]{:S(2)}) %all-to-all-start.1) | async-done | bytes 655392 | tf_op jit(solution)/shard_map/all_to_all | solution.py:399
  23.6 4.9 %all-to-all-start = ((f32[32,288,128]{2,1,0:T(8,128)}), f32[32,288,128]{2,1,0:T(8,128)}, u32[]{:S(2)}, u32[]{:S(2)}) async-start(f32[32,288,128]{2,1,0:T(8,128)} %pack_images.1), calls=%async_computation | async-start | bytes 9437184 | tf_op jit(solution)/shard_map/all_to_all | solution.py:399
  28.6 3.2 %collective-permute-start = (f32[16,40,128]{2,1,0:T(8,128)S(1)}, f32[16,40,128]{2,1,0:T(8,128)S(1)}, u32[]{:S(2)}, u32[]{:S(2)}) collective-permute-start(f32[16,40,128]{2,1,0:T(8,128)S(1)} %get-tuple-element.24), channel_id=1, source_target_pairs={{0,2},{2,4},{4,6},{6,8},{8,10},{10,12},{12,14},{14,0},{1,3},{3,5},... | collective-permute-start | bytes 983048 | tf_op jit(solution)/shard_map/ppermute | solution.py:404
  31.8 0.1 copy.14
  32.0 0.1 pad.8.clone.sq_ref
  32.1 6.9 %collective-permute-done.below_ref = f32[16,40,128]{2,1,0:T(8,128)S(1)} collective-permute-done((f32[16,40,128]{2,1,0:T(8,128)S(1)}, f32[16,40,128]{2,1,0:T(8,128)S(1)}, u32[]{:S(2)}, u32[]{:S(2)}) %collective-permute-start) | collective-permute-done | bytes 327712 | tf_op jit(solution)/shard_map/ppermute | solution.py:404
  39.0 3.4 %collective-permute-done.1.above_ref = f32[16,40,128]{2,1,0:T(8,128)S(1)} collective-permute-done((f32[16,40,128]{2,1,0:T(8,128)S(1)}, f32[16,40,128]{2,1,0:T(8,128)S(1)}, u32[]{:S(2)}, u32[]{:S(2)}) %collective-permute-start.1) | collective-permute-done | bytes 327712 | tf_op jit(solution)/shard_map/ppermute | solution.py:404
  42.4 2.2 %operands.1 = (bf16[1024,640]{1,0:T(8,128)(2,1)S(1)}, bf16[48,384]{1,0:T(8,128)(2,1)S(1)}) custom-call(f32[32,40,128]{2,1,0:T(8,128)S(1)} %all-to-all-done.1.tpl_ref.refs_1_, f32[16,40,128]{2,1,0:T(8,128)S(1)} %collective-permute-done.below_ref, f32[16,40,128]{2,1,0:T(8,128)S(1)} %collective-permute-done.1.above_ref, f32[16,384]{1,0:T(8,128)S(1)} %concatenate.9.ctf_ref, ...), custom_call_target="tpu_custom_call" | custom-call | flops 600000000 | bytes 4000000 | tf_op jit(solution)/shard_map/operands/pallas_call | solution.py:137
  44.7 42.9 %all-to-all-done.first_ref.odd_ref.even_ref = f32[32,288,128]{2,1,0:T(8,128)} async-done(((f32[32,288,128]{2,1,0:T(8,128)}), f32[32,288,128]{2,1,0:T(8,128)}, u32[]{:S(2)}, u32[]{:S(2)}) %all-to-all-start) | async-done | bytes 4718624 | tf_op jit(solution)/shard_map/all_to_all | solution.py:399
  87.6 10.9 %window_scores.1 = (bf16[32,128,256]{2,1,0:T(8,128)(2,1)S(1)}, bf16[32,128,256]{2,1,0:T(8,128)(2,1)S(1)}, bf16[32,128,128]{2,1,0:T(8,128)(2,1)S(1)}, f32[96,4,128]{2,1,0:T(4,128)S(1)}) custom-call(f32[32,288,128]{2,1,0:T(8,128)} %all-to-all-done.first_ref.odd_ref.even_ref, f32[32,288,128]{2,1,0:T(8,128)} %all-to-all-done.first_ref.odd_ref.even_ref, ...), custom_call_target="tpu_custom_call" | custom-call | flops 6000000000 | bytes 14000000 | tf_op jit(solution)/shard_map/window_scores/pallas_call | solution.py:217
  98.5 19.3 %all_to_all.25.scores_ref = f32[96,4,128]{2,1,0:T(4,128)S(1)} all-to-all(f32[96,4,128]{2,1,0:T(4,128)S(1)} %get-tuple-element.14), channel_id=1, replica_groups=mesh['dir'=16,'z'=8,'xlo'=2] {'dir','xlo'}, dimensions={0} | all-to-all | bytes 393216 | tf_op jit(solution)/shard_map/all_to_all | solution.py:399
  117.8 0.6 home.1
  118.5 11.8 %all_to_all.26.refs_0_ = f32[96,4,128]{2,1,0:T(4,128)S(1)} all-to-all(f32[96,4,128]{2,1,0:T(4,128)S(1)} %get-tuple-element.17), channel_id=1, replica_groups=mesh['dir'=16,'z'=8,'xlo'=2] {'dir','xlo'}, dimensions={0} | all-to-all | bytes 393216 | tf_op jit(solution)/shard_map/all_to_all | solution.py:399
  130.2 2.9 %sums_halo.1 = f32[512,384]{1,0:T(8,128)S(1)} custom-call(f32[96,4,128]{2,1,0:T(4,128)S(1)} %all_to_all.26.refs_0_, f32[32,40,128]{2,1,0:T(8,128)S(1)} %all-to-all-done.1.tpl_ref.refs_1_, bf16[32,128,256]{2,1,0:T(8,128)(2,1)S(1)} %get-tuple-element.18.refs_2_, bf16[32,128,256]{2,1,0:T(8,128)(2,1)S(1)} %get-tuple-element.19.refs_3_, ...), custom_call_target="tpu_custom_call" | custom-call | flops 4000000000 | bytes 6000000 | tf_op jit(solution)/shard_map/sums_halo/pallas_call | solution.py:328
  133.2 3.4 %collective-permute-start.2 = (f32[256,384]{1,0:T(8,128)S(1)}, f32[256,384]{1,0:T(8,128)S(1)}, u32[]{:S(2)}, u32[]{:S(2)}) collective-permute-start(f32[256,384]{1,0:T(8,128)S(1)} %get-tuple-element.22), channel_id=1, source_target_pairs={{0,2},{2,4},{4,6},{6,8},{8,10},{10,12},{12,14},{14,0},{1,3},{3,5},... | collective-permute-start | bytes 1179656 | tf_op jit(solution)/shard_map/ppermute | solution.py:404
  136.6 5.6 %sums_own.1.own_ref = f32[512,384]{1,0:T(8,128)S(1)} custom-call(f32[96,4,128]{2,1,0:T(4,128)S(1)} %all_to_all.26.refs_0_, f32[32,40,128]{2,1,0:T(8,128)S(1)} %all-to-all-done.1.tpl_ref.refs_1_, bf16[32,128,256]{2,1,0:T(8,128)(2,1)S(1)} %get-tuple-element.18.refs_2_, bf16[32,128,256]{2,1,0:T(8,128)(2,1)S(1)} %get-tuple-element.19.refs_3_, ...), custom_call_target="tpu_custom_call" | custom-call | flops 4000000000 | bytes 6000000 | tf_op jit(solution)/shard_map/sums_own/pallas_call | solution.py:328
  142.2 2.4 %collective-permute-done.2.below_ref = f32[256,384]{1,0:T(8,128)S(1)} collective-permute-done((f32[256,384]{1,0:T(8,128)S(1)}, f32[256,384]{1,0:T(8,128)S(1)}, u32[]{:S(2)}, u32[]{:S(2)}) %collective-permute-start.2) | collective-permute-done | bytes 393248 | tf_op jit(solution)/shard_map/ppermute | solution.py:404
  144.6 3.4 %collective-permute-done.3.above_ref = f32[256,384]{1,0:T(8,128)S(1)} collective-permute-done((f32[256,384]{1,0:T(8,128)S(1)}, f32[256,384]{1,0:T(8,128)S(1)}, u32[]{:S(2)}, u32[]{:S(2)}) %collective-permute-start.3) | collective-permute-done | bytes 393248 | tf_op jit(solution)/shard_map/ppermute | solution.py:404
  148.0 1.1 averages.1
  149.2 16.1 %all_to_all.27.got_ref = f32[288,4,128]{2,1,0:T(4,128)S(1)} all-to-all(f32[288,4,128]{2,1,0:T(4,128)S(1)} %averages.1), channel_id=1, replica_groups=mesh['dir'=16,'z'=8,'xlo'=2] {'dir','xlo'}, dimensions={0} | all-to-all | bytes 1179648 | tf_op jit(solution)/shard_map/all_to_all | solution.py:399
  165.3 1.0 unpack.1
  (15 shorter events, 0.3 us)
Async XLA Ops:
  0.6 27.8 %copy-start = (f32[16,9216]{1,0:T(8,128)S(1)}, f32[16,9216]{1,0:T(8,128)}, u32[]{:S(2)}) copy-start(f32[16,9216]{1,0:T(8,128)} %param.11) | copy-start | bytes 1769476
  2.8 20.7 %all-to-all-start.1 = ((f32[32,40,128]{2,1,0:T(8,128)}), f32[32,40,128]{2,1,0:T(8,128)S(1)}, u32[]{:S(2)}, u32[]{:S(2)}) async-start(f32[32,40,128]{2,1,0:T(8,128)} %pack_templates.1), calls=%async_computation.1 | async-start | bytes 1310720 | tf_op jit(solution)/shard_map/all_to_all | solution.py:399
  23.6 64.0 %all-to-all-start = ((f32[32,288,128]{2,1,0:T(8,128)}), f32[32,288,128]{2,1,0:T(8,128)}, u32[]{:S(2)}, u32[]{:S(2)}) async-start(f32[32,288,128]{2,1,0:T(8,128)} %pack_images.1), calls=%async_computation | async-start | bytes 9437184 | tf_op jit(solution)/shard_map/all_to_all | solution.py:399
  28.6 10.4 %collective-permute-start = (f32[16,40,128]{2,1,0:T(8,128)S(1)}, f32[16,40,128]{2,1,0:T(8,128)S(1)}, u32[]{:S(2)}, u32[]{:S(2)}) collective-permute-start(f32[16,40,128]{2,1,0:T(8,128)S(1)} %get-tuple-element.24), channel_id=1, source_target_pairs={{0,2},{2,4},{4,6},{6,8},{8,10},{10,12},{12,14},{14,0},{1,3},{3,5},... | collective-permute-start | bytes 983048 | tf_op jit(solution)/shard_map/ppermute | solution.py:404
  31.8 10.6 %collective-permute-start.1 = (f32[16,40,128]{2,1,0:T(8,128)S(1)}, f32[16,40,128]{2,1,0:T(8,128)S(1)}, u32[]{:S(2)}, u32[]{:S(2)}) collective-permute-start(f32[16,40,128]{2,1,0:T(8,128)S(1)} %get-tuple-element.23), channel_id=1, source_target_pairs={{0,14},{2,0},{4,2},{6,4},{8,6},{10,8},{12,10},{14,12},{1,15},{3,1}... | collective-permute-start | bytes 983048 | tf_op jit(solution)/shard_map/ppermute | solution.py:404
  87.6 30.3 %copy-start.1 = (s32[128]{0:T(128)S(1)}, s32[128]{0:T(128)}, u32[]{:S(2)}) copy-start(s32[128]{0:T(128)} %param.8) | copy-start | bytes 1540
  133.2 11.5 %collective-permute-start.2 = (f32[256,384]{1,0:T(8,128)S(1)}, f32[256,384]{1,0:T(8,128)S(1)}, u32[]{:S(2)}, u32[]{:S(2)}) collective-permute-start(f32[256,384]{1,0:T(8,128)S(1)} %get-tuple-element.22), channel_id=1, source_target_pairs={{0,2},{2,4},{4,6},{6,8},{8,10},{10,12},{12,14},{14,0},{1,3},{3,5},... | collective-permute-start | bytes 1179656 | tf_op jit(solution)/shard_map/ppermute | solution.py:404
  136.5 11.5 %collective-permute-start.3 = (f32[256,384]{1,0:T(8,128)S(1)}, f32[256,384]{1,0:T(8,128)S(1)}, u32[]{:S(2)}, u32[]{:S(2)}) collective-permute-start(f32[256,384]{1,0:T(8,128)S(1)} %get-tuple-element.21), channel_id=1, source_target_pairs={{0,14},{2,0},{4,2},{6,4},{8,6},{10,8},{12,10},{14,12},{1,15},{3,1}... | collective-permute-start | bytes 1179656 | tf_op jit(solution)/shard_map/ppermute | solution.py:404

commit v8 on v7

--- a/solution.py
+++ b/solution.py
@@ -283,6 +283,50 @@
     return [jnp.where(mine, wide(v), 0.0).astype(BF) for v in (hi, lo)]
 
 
+def pack_tail(tail):
+    group = lane_group((256, LANES))
+    tail = jnp.where(group == 0, tail + pltpu.roll(tail, 96, 1), tail)
+    first, second = tail[:128], pltpu.roll(tail[128:], 64, 1)
+    both = pick_groups([first, second, second, first])
+    return jnp.concatenate([both[:64], both[64:]], axis=1)
+
+
+def unpack_tail(ref, rows):
+    half = pl.ds(128 * (rows % 2), 128)
+    both = ref[pl.ds(256, 64), half]
+    both = both if rows < 2 else pltpu.roll(both, 64, 1)
+    group = lane_group((64, LANES))
+    return jnp.where(jnp.logical_or(group == 0, group == 3), both, 0.0)
+
+
+def edge_kernel(p_ref, tpl_ref, xh_ref, xl_ref, xr_ref, below_ref, above_ref):
+    n = xh_ref.shape[0]
+    for side, out_ref in enumerate((below_ref, above_ref)):
+        mine = range(side, n, 2)
+        stack = lambda ref: jnp.concatenate([ref[s] for s in mine], axis=0)
+        xh, xl, xr = stack(xh_ref), stack(xl_ref), stack(xr_ref)
+        p4 = jnp.concatenate([p_ref[3 * s + 2 * side] for s in mine], axis=1)
+        high, low = spread(jnp.concatenate([p4, p4], axis=0), bins_of(tpl_ref, mine), 0, 256)
+        left = jnp.concatenate([high, low, high], axis=1)
+        out_ref[pl.ds(0, 256), :] = jnp.dot(left, jnp.concatenate([xh, xh, xl], axis=0), preferred_element_type=F32)
+        wide = left.shape[1] // 3 * 2
+        tail = jnp.dot(left[:, :wide], jnp.concatenate([xr, xr], axis=0), preferred_element_type=F32)
+        out_ref[pl.ds(256, 64), :] = pack_tail(tail)
+
+
+def edge_sums(p, tpl, xh, xl, xr):
+    vmem = pl.BlockSpec(memory_space=pltpu.VMEM)
+    return pl.pallas_call(
+        edge_kernel,
+        in_specs=[vmem] * 5,
+        out_specs=[vmem] * 2,
+        out_shape=[jax.ShapeDtypeStruct((320, 256), F32)] * 2,
+        compiler_params=params(24),
+        cost_estimate=cost(3_000_000_000, 6_000_000),
+        name="edge_sums",
+    )(p, tpl, xh, xl, xr)
+
+
 def sums_kernel(which, group, p_ref, tpl_ref, xh_ref, xl_ref, xr_ref, out_ref):
     step = pl.program_id(0)
 
@@ -337,11 +381,13 @@
     )(p, tpl, xh, xl, xr)
 
 
-def average_kernel(own_ref, below_ref, above_ref, sq_ref, out_ref):
+def average_kernel(own_ref, below_ref, above_ref, square_ref, out_ref, sq_ref):
+    sq_ref[...] = jnp.zeros_like(sq_ref)
+    sq_ref[pl.ds(96, CLASSES), pl.ds(0, 288)] = square_ref[...]
     for side, other_ref in ((0, below_ref), (1, above_ref)):
         for c in range(4):
-            rows = pl.ds(64 * c, 64)
-            total = own_ref[pl.ds(256 * side + 64 * c, 64), :] + other_ref[rows, :]
+            other = jnp.concatenate([other_ref[pl.ds(64 * c, 64), :], unpack_tail(other_ref, c)], axis=1)
+            total = own_ref[pl.ds(256 * side + 64 * c, 64), :] + other
             weight = jnp.dot(total[:, 256:], sq_ref[...], precision=HIGHEST, preferred_element_type=F32)
             tail = total[:, 256:]
             tail = tail + pltpu.roll(tail, 96, 1)
@@ -364,6 +410,7 @@
         in_specs=[vmem] * 4,
         out_specs=vmem,
         out_shape=jax.ShapeDtypeStruct((9 * n, 4, LANES), F32),
+        scratch_shapes=[pltpu.VMEM((128, 384), F32)],
         compiler_params=params(8),
         cost_estimate=cost(200_000_000, 3_000_000),
         name="averages",
@@ -415,7 +462,6 @@
     square = jnp.concatenate([ctf_main, ctf_rem], axis=1)
     square = square * square
     to_class = jnp.pad(jnp.concatenate([square.T, square.T], axis=1), ((0, 96), (96, 0)))
-    to_pixel = jnp.pad(square, ((96, 16), (0, 96)))
 
     tpl = exchange(pack_templates(templates, prior_bin[None], defocus_class[None]))
     n = tpl.shape[0]
@@ -427,11 +473,11 @@
     xh, xl, xr, partial = window_scores(buf, tpl, y, ctf)
     log_total, mean_shift, p = home(exchange(partial), prior_center[None])
     p = exchange(p)
-    edge = sums("halo", p, tpl, xh, xl, xr)
-    from_above = along_z(edge[:256], -1)
-    from_below = along_z(edge[256:], 1)
+    down, up = edge_sums(p, tpl, xh, xl, xr)
+    from_above = along_z(down, -1)
+    from_below = along_z(up, 1)
     mine = sums("own", p, tpl, xh, xl, xr)
-    out = averages(mine, from_below, from_above, to_pixel, n)
+    out = averages(mine, from_below, from_above, square, n)
     average = unpack(exchange(out), pixels)
     return log_total[0], mean_shift[0], average
 

time: 167 us -> 165 us (0.988)
    ppermute x4, waiting for transfers between devices: 16.2 us -> 11.9 us  [along_z(): return lax.ppermute(value, 'z', [(i, (i + by) % size) for i in range(size)])]
    pallas_call x0 -> x1, Pallas kernels: none -> 3.03 us  [edge_sums(): pl.pallas_call(edge_kernel, in_specs=[vmem] * 5, out_specs=[vmem] * 2, ou...]
    pallas_call x2 -> x1, Pallas kernels: 8.53 us -> 5.64 us  [sums(): pl.pallas_call(body, grid=(n // group,), in_specs=[vmem] * 5, out_specs=v...]
    all_to_all x2, waiting for transfers between devices: 49.3 us -> 51.9 us  [exchange(): return lax.all_to_all(value, PLANE, split_axis=0, concat_axis=0, tiled=True)]
  transfers between devices with their start and end apart: 6 -> 6, of which waited for: 6 -> 5; matrix products, arithmetic and copies ran while one was open for 0% -> 0% of each run, Pallas kernels for 9% -> 9%
where the time goes in v8:
time: 165 us
  waiting for transfers between devices  63.9 us (39%)
  blocking collectives  47.2 us (29%)
  Pallas kernels  33.7 us (20%)
  starting transfers between devices  18.9 us (11%)
    all_to_all x2, waiting for transfers between devices, exchange(): return lax.all_to_all(value, PLANE, split_axis=0, concat_axis=0, tiled=True)  51.9 us
    all_to_all x3, blocking collectives, exchange(): return lax.all_to_all(value, PLANE, split_axis=0, concat_axis=0, tiled=True)  47.2 us
    all_to_all x2, starting transfers between devices, exchange(): return lax.all_to_all(value, PLANE, split_axis=0, concat_axis=0, tiled=True)  12.2 us
    ppermute x4, waiting for transfers between devices, along_z(): return lax.ppermute(value, 'z', [(i, (i + by) % size) for i in range(size)])  11.9 us
    pallas_call x1, Pallas kernels, window_scores(): pl.pallas_call(scores_kernel, grid=(blocks // 2,), in_specs=[image(lambda...  10.9 us
    pallas_call x1, Pallas kernels, pack_images(): pl.pallas_call(pack_images_kernel, grid=(steps,), in_specs=[pl.BlockSpec(...  7.02 us
    ppermute x4, starting transfers between devices, along_z(): return lax.ppermute(value, 'z', [(i, (i + by) % size) for i in range(size)])  6.68 us
    pallas_call x1, Pallas kernels, sums(): pl.pallas_call(body, grid=(n // group,), in_specs=[vmem] * 5, out_specs=v...  5.64 us
  transfers between devices with their start and end apart: 6, of which 5 were waited for; matrix products, arithmetic and copies ran while one was open for 0% of the time, Pallas kernels for 9%

profile of v8, /device:TPU:96, one launch (start us, length us, event | category | flops | bytes accessed | tf_op | source)
XLA Modules:
  0.0 164.9 jit_solution(17972153975292119347)
XLA Ops:
  0.6 2.2 %pack_templates.1 = f32[32,40,128]{2,1,0:T(8,128)} custom-call(f32[4,4,9216]{2,1,0:T(4,128)} %tpl_ref.1, s32[1,128]{1,0:T(1,128)} %bitcast.18, s32[1,128]{1,0:T(1,128)} %bitcast.19), custom_call_target="tpu_custom_call" | custom-call | bytes 1300000 | tf_op jit(solution)/shard_map/pack_templates/pallas_call | solution.py:92
  2.8 7.3 %all-to-all-start.1 = ((f32[32,40,128]{2,1,0:T(8,128)}), f32[32,40,128]{2,1,0:T(8,128)S(1)}, u32[]{:S(2)}, u32[]{:S(2)}) async-start(f32[32,40,128]{2,1,0:T(8,128)} %pack_templates.1), calls=%async_computation.1 | async-start | bytes 1310720 | tf_op jit(solution)/shard_map/all_to_all | solution.py:446
  10.2 7.0 %pack_images.1 = f32[32,288,128]{2,1,0:T(8,128)} custom-call(f32[128,9216]{1,0:T(8,128)} %rem_ref.1, f32[128,9216]{1,0:T(8,128)} %rem_ref.1), custom_call_target="tpu_custom_call" | custom-call | bytes 9500000 | tf_op jit(solution)/shard_map/pack_images/pallas_call | solution.py:60
  17.2 6.4 %all-to-all-done.1.tpl_ref.refs_1_ = f32[32,40,128]{2,1,0:T(8,128)S(1)} async-done(((f32[32,40,128]{2,1,0:T(8,128)}), f32[32,40,128]{2,1,0:T(8,128)S(1)}, u32[]{:S(2)}, u32[]{:S(2)}) %all-to-all-start.1) | async-done | bytes 655392 | tf_op jit(solution)/shard_map/all_to_all | solution.py:446
  23.6 4.9 %all-to-all-start = ((f32[32,288,128]{2,1,0:T(8,128)}), f32[32,288,128]{2,1,0:T(8,128)}, u32[]{:S(2)}, u32[]{:S(2)}) async-start(f32[32,288,128]{2,1,0:T(8,128)} %pack_images.1), calls=%async_computation | async-start | bytes 9437184 | tf_op jit(solution)/shard_map/all_to_all | solution.py:446
  28.5 0.2 collective-permute-start.1
  28.7 3.1 %collective-permute-start = (f32[16,40,128]{2,1,0:T(8,128)S(1)}, f32[16,40,128]{2,1,0:T(8,128)S(1)}, u32[]{:S(2)}, u32[]{:S(2)}) collective-permute-start(f32[16,40,128]{2,1,0:T(8,128)S(1)} %get-tuple-element.26), channel_id=1, source_target_pairs={{0,2},{2,4},{4,6},{6,8},{8,10},{10,12},{12,14},{14,0},{1,3},{3,5},... | collective-permute-start | bytes 983048 | tf_op jit(solution)/shard_map/ppermute | solution.py:451
  32.0 0.1 copy.14
  32.1 0.1 pad.4.clone.sq_ref
  32.2 7.5 %collective-permute-done.1.above_ref = f32[16,40,128]{2,1,0:T(8,128)S(1)} collective-permute-done((f32[16,40,128]{2,1,0:T(8,128)S(1)}, f32[16,40,128]{2,1,0:T(8,128)S(1)}, u32[]{:S(2)}, u32[]{:S(2)}) %collective-permute-start.1) | collective-permute-done | bytes 327712 | tf_op jit(solution)/shard_map/ppermute | solution.py:451
  39.7 2.3 %operands.1 = (bf16[1024,640]{1,0:T(8,128)(2,1)S(1)}, bf16[48,384]{1,0:T(8,128)(2,1)S(1)}) custom-call(f32[32,40,128]{2,1,0:T(8,128)S(1)} %all-to-all-done.1.tpl_ref.refs_1_, f32[16,40,128]{2,1,0:T(8,128)S(1)} %collective-permute-done.below_ref, f32[16,40,128]{2,1,0:T(8,128)S(1)} %collective-permute-done.1.above_ref, f32[16,384]{1,0:T(8,128)S(1)} %concatenate.9.ctf_ref, ...), custom_call_target="tpu_custom_call" | custom-call | flops 600000000 | bytes 4000000 | tf_op jit(solution)/shard_map/operands/pallas_call | solution.py:137
  42.0 45.6 %all-to-all-done.first_ref.odd_ref.even_ref = f32[32,288,128]{2,1,0:T(8,128)} async-done(((f32[32,288,128]{2,1,0:T(8,128)}), f32[32,288,128]{2,1,0:T(8,128)}, u32[]{:S(2)}, u32[]{:S(2)}) %all-to-all-start) | async-done | bytes 4718624 | tf_op jit(solution)/shard_map/all_to_all | solution.py:446
  87.6 10.9 %window_scores.1 = (bf16[32,128,256]{2,1,0:T(8,128)(2,1)S(1)}, bf16[32,128,256]{2,1,0:T(8,128)(2,1)S(1)}, bf16[32,128,128]{2,1,0:T(8,128)(2,1)S(1)}, f32[96,4,128]{2,1,0:T(4,128)S(1)}) custom-call(f32[32,288,128]{2,1,0:T(8,128)} %all-to-all-done.first_ref.odd_ref.even_ref, f32[32,288,128]{2,1,0:T(8,128)} %all-to-all-done.first_ref.odd_ref.even_ref, ...), custom_call_target="tpu_custom_call" | custom-call | flops 6000000000 | bytes 14000000 | tf_op jit(solution)/shard_map/window_scores/pallas_call | solution.py:217
  98.5 19.3 %all_to_all.25.scores_ref = f32[96,4,128]{2,1,0:T(4,128)S(1)} all-to-all(f32[96,4,128]{2,1,0:T(4,128)S(1)} %get-tuple-element.16), channel_id=1, replica_groups=mesh['dir'=16,'z'=8,'xlo'=2] {'dir','xlo'}, dimensions={0} | all-to-all | bytes 393216 | tf_op jit(solution)/shard_map/all_to_all | solution.py:446
  117.8 0.6 home.1
  118.5 11.8 %all_to_all.26.refs_0_.p_ref = f32[96,4,128]{2,1,0:T(4,128)S(1)} all-to-all(f32[96,4,128]{2,1,0:T(4,128)S(1)} %get-tuple-element.19), channel_id=1, replica_groups=mesh['dir'=16,'z'=8,'xlo'=2] {'dir','xlo'}, dimensions={0} | all-to-all | bytes 393216 | tf_op jit(solution)/shard_map/all_to_all | solution.py:446
  130.2 3.0 %edge_sums.1 = (f32[320,256]{1,0:T(8,128)S(1)}, f32[320,256]{1,0:T(8,128)S(1)}) custom-call(f32[96,4,128]{2,1,0:T(4,128)S(1)} %all_to_all.26.refs_0_.p_ref, f32[32,40,128]{2,1,0:T(8,128)S(1)} %all-to-all-done.1.tpl_ref.refs_1_, bf16[32,128,256]{2,1,0:T(8,128)(2,1)S(1)} %get-tuple-element.20.refs_2_.xh_ref, ...), custom_call_target="tpu_custom_call" | custom-call | flops 3000000000 | bytes 6000000 | tf_op jit(solution)/shard_map/edge_sums/pallas_call | solution.py:319
  133.2 3.4 %collective-permute-start.2 = (f32[320,256]{1,0:T(8,128)S(1)}, f32[320,256]{1,0:T(8,128)S(1)}, u32[]{:S(2)}, u32[]{:S(2)}) collective-permute-start(f32[320,256]{1,0:T(8,128)S(1)} %get-tuple-element.23), channel_id=1, source_target_pairs={{0,2},{2,4},{4,6},{6,8},{8,10},{10,12},{12,14},{14,0},{1,3},{3,5},... | collective-permute-start | bytes 983048 | tf_op jit(solution)/shard_map/ppermute | solution.py:451
  136.6 5.6 %sums_own.1.own_ref = f32[512,384]{1,0:T(8,128)S(1)} custom-call(f32[96,4,128]{2,1,0:T(4,128)S(1)} %all_to_all.26.refs_0_.p_ref, f32[32,40,128]{2,1,0:T(8,128)S(1)} %all-to-all-done.1.tpl_ref.refs_1_, bf16[32,128,256]{2,1,0:T(8,128)(2,1)S(1)} %get-tuple-element.20.refs_2_.xh_ref, bf16[32,128,256]{2,1,0:T(8,128)(2,1)S(1)} %get-tuple-element.21.refs_3_.xl_ref, ...), custom_call_target="tpu_custom_call" | custom-call | flops 4000000000 | bytes 6000000 | tf_op jit(solution)/shard_map/sums_own/pallas_call | solution.py:372
  142.3 1.0 collective-permute-done.2.below_ref
  143.3 3.4 %collective-permute-done.3.above_ref = f32[320,256]{1,0:T(8,128)S(1)} collective-permute-done((f32[320,256]{1,0:T(8,128)S(1)}, f32[320,256]{1,0:T(8,128)S(1)}, u32[]{:S(2)}, u32[]{:S(2)}) %collective-permute-start.3) | collective-permute-done | bytes 327712 | tf_op jit(solution)/shard_map/ppermute | solution.py:451
  146.7 1.0 averages.1
  147.8 16.1 %all_to_all.27.got_ref = f32[288,4,128]{2,1,0:T(4,128)S(1)} all-to-all(f32[288,4,128]{2,1,0:T(4,128)S(1)} %averages.1), channel_id=1, replica_groups=mesh['dir'=16,'z'=8,'xlo'=2] {'dir','xlo'}, dimensions={0} | all-to-all | bytes 1179648 | tf_op jit(solution)/shard_map/all_to_all | solution.py:446
  163.9 1.0 unpack.1
  (13 shorter events, 0.2 us)
Async XLA Ops:
  0.6 27.8 %copy-start = (f32[16,9216]{1,0:T(8,128)S(1)}, f32[16,9216]{1,0:T(8,128)}, u32[]{:S(2)}) copy-start(f32[16,9216]{1,0:T(8,128)} %param.11) | copy-start | bytes 1769476
  2.8 20.7 %all-to-all-start.1 = ((f32[32,40,128]{2,1,0:T(8,128)}), f32[32,40,128]{2,1,0:T(8,128)S(1)}, u32[]{:S(2)}, u32[]{:S(2)}) async-start(f32[32,40,128]{2,1,0:T(8,128)} %pack_templates.1), calls=%async_computation.1 | async-start | bytes 1310720 | tf_op jit(solution)/shard_map/all_to_all | solution.py:446
  23.6 64.0 %all-to-all-start = ((f32[32,288,128]{2,1,0:T(8,128)}), f32[32,288,128]{2,1,0:T(8,128)}, u32[]{:S(2)}, u32[]{:S(2)}) async-start(f32[32,288,128]{2,1,0:T(8,128)} %pack_images.1), calls=%async_computation | async-start | bytes 9437184 | tf_op jit(solution)/shard_map/all_to_all | solution.py:446
  28.5 11.2 %collective-permute-start.1 = (f32[16,40,128]{2,1,0:T(8,128)S(1)}, f32[16,40,128]{2,1,0:T(8,128)S(1)}, u32[]{:S(2)}, u32[]{:S(2)}) collective-permute-start(f32[16,40,128]{2,1,0:T(8,128)S(1)} %get-tuple-element.25), channel_id=1, source_target_pairs={{0,14},{2,0},{4,2},{6,4},{8,6},{10,8},{12,10},{14,12},{1,15},{3,1}... | collective-permute-start | bytes 983048 | tf_op jit(solution)/shard_map/ppermute | solution.py:451
  28.7 11.0 %collective-permute-start = (f32[16,40,128]{2,1,0:T(8,128)S(1)}, f32[16,40,128]{2,1,0:T(8,128)S(1)}, u32[]{:S(2)}, u32[]{:S(2)}) collective-permute-start(f32[16,40,128]{2,1,0:T(8,128)S(1)} %get-tuple-element.26), channel_id=1, source_target_pairs={{0,2},{2,4},{4,6},{6,8},{8,10},{10,12},{12,14},{14,0},{1,3},{3,5},... | collective-permute-start | bytes 983048 | tf_op jit(solution)/shard_map/ppermute | solution.py:451
  87.6 30.3 %copy-start.1 = (s32[128]{0:T(128)S(1)}, s32[128]{0:T(128)}, u32[]{:S(2)}) copy-start(s32[128]{0:T(128)} %param.8) | copy-start | bytes 1540
  133.2 10.1 %collective-permute-start.2 = (f32[320,256]{1,0:T(8,128)S(1)}, f32[320,256]{1,0:T(8,128)S(1)}, u32[]{:S(2)}, u32[]{:S(2)}) collective-permute-start(f32[320,256]{1,0:T(8,128)S(1)} %get-tuple-element.23), channel_id=1, source_target_pairs={{0,2},{2,4},{4,6},{6,8},{8,10},{10,12},{12,14},{14,0},{1,3},{3,5},... | collective-permute-start | bytes 983048 | tf_op jit(solution)/shard_map/ppermute | solution.py:451
  136.6 10.1 %collective-permute-start.3 = (f32[320,256]{1,0:T(8,128)S(1)}, f32[320,256]{1,0:T(8,128)S(1)}, u32[]{:S(2)}, u32[]{:S(2)}) collective-permute-start(f32[320,256]{1,0:T(8,128)S(1)} %get-tuple-element.24), channel_id=1, source_target_pairs={{0,14},{2,0},{4,2},{6,4},{8,6},{10,8},{12,10},{14,12},{1,15},{3,1}... | collective-permute-start | bytes 983048 | tf_op jit(solution)/shard_map/ppermute | solution.py:451
